TPU v7x, 32 devices: a whole 2x2x4 slice. The times are simulated.
32 devices in a mesh: batch: 8 (over z, core), head: 4 (over y, x).
Axes of the slice: x: 2, y: 2, z: 4, core: 2. Of those that a mesh axis runs over, the one named last changes fastest.
Arguments:
- hidden_in: bfloat16 [2048, 2048], P(('batch', 'head')), may hold values from -6 to 6
- norm1_gain: float32 [2048], replicated, may hold values from 0.5 to 1.5
- qkv_weight: bfloat16 [3, 2048, 2048], P(None, None, 'head'), may hold values from -0.125 to 0.125
- beta_weight: bfloat16 [2048, 16], P(None, 'head'), may hold values from -0.125 to 0.125
- conv_weight: bfloat16 [3, 4, 2048], P(None, None, 'head'), may hold values from -3 to 3
- out_gain: float32 [128], replicated, may hold values from 0.5 to 1.5
- out_weight: bfloat16 [2048, 2048], P('head'), may hold values from -0.125 to 0.125
- norm2_gain: float32 [2048], replicated, may hold values from 0.5 to 1.5
- gate_up_weight: bfloat16 [2, 2048, 5632], P(None, None, 'head'), may hold values from -0.125 to 0.125
- down_weight: bfloat16 [5632, 2048], P('head'), may hold values from -0.078125 to 0.078125
- block_segments: int32 [8, 4], P('batch'), may hold values from 0 to 2, never falling along the last dimension, each value on 1 to 2 neighbouring positions
- cotangent: bfloat16 [2048, 2048], P(('batch', 'head')), may hold values from -6 to 6
Outputs:
- block_out: bfloat16 [2048, 2048], P(('batch', 'head'))
- input_grad: float32 [2048, 2048], P(('batch', 'head'))
- norm1_gain_grad: float32 [2048], replicated
- qkv_grad: float32 [3, 2048, 2048], P(None, None, 'head')
- beta_grad: float32 [2048, 16], P(None, 'head')
- conv_grad: float32 [3, 4, 2048], P(None, None, 'head')
- out_gain_grad: float32 [128], replicated
- out_grad: float32 [2048, 2048], P('head')
- norm2_gain_grad: float32 [2048], replicated
- gate_up_grad: float32 [2, 2048, 5632], P(None, None, 'head')
- down_grad: float32 [5632, 2048], P('head')
Inputs may be any that keep to these rules, and one draw needn't show every extreme that they name: `block_segments`: each row gives, for each block of 64 tokens of one group in order, the number of the sequence it belongs to: three sequences in every group, numbered from 0 and never falling; each covers 1 to 2 blocks and one covers exactly 2.
All inputs are finite; a program needn't handle non-finite values.
Results may differ from a plain program's by a relative error of at most 0.02.
Values may be sent and summed in bfloat16 or wider, within the bound.
No kernel may reach another device: no remote copies, remote signals or barrier semaphores. Data moves between devices by JAX's collectives and lax.ppermute only.
A program may use at most 256 MiB of HBM per device.

v0:
```python
import jax
import jax.numpy as jnp
from jax import lax
from jax.sharding import PartitionSpec as P

highest_precision = lax.Precision.HIGHEST


def rms_norm(values, gain, epsilon):
    return values * lax.rsqrt(jnp.mean(values * values, axis=-1, keepdims=True) + epsilon) * gain


def unit_rows(field):
    return field * lax.rsqrt(jnp.sum(field * field, axis=-1, keepdims=True) + 1e-06)


def conv_masks(token_segments, taps):
    masks = []
    for shift in range(1, taps):
        earlier = jnp.concatenate([jnp.full((shift,), -1, jnp.int32), token_segments[:-shift]])
        masks.append((earlier == token_segments).astype(jnp.float32)[:, None])
    return masks


def short_conv(values, taps, masks):
    result = values * taps[0]
    for shift in range(1, taps.shape[0]):
        moved = jnp.concatenate(
            [jnp.zeros((shift, values.shape[1]), jnp.float32), values[:-shift]], axis=0
        )
        result = result + moved * taps[shift] * masks[shift - 1]
    return result


def block_step(running_state, inputs):
    query_rows, key, value, beta, keep = inputs
    running_state = running_state * keep
    length = key.shape[1]
    strict = jnp.tril(jnp.ones((length, length), jnp.float32), -1)
    inclusive = jnp.tril(jnp.ones((length, length), jnp.float32))
    keyed = (
        jnp.einsum("hck,hdk->hcd", key * beta[:, :, None], key, precision=highest_precision)
        * strict
    )
    power = -keyed
    inverse = jnp.eye(length, dtype=jnp.float32) + power
    for level in range(length.bit_length() - 2):
        power = jnp.einsum("hcd,hde->hce", power, power, precision=highest_precision)
        inverse = inverse + jnp.einsum("hcd,hde->hce", inverse, power, precision=highest_precision)
    weights = inverse * beta[:, None, :]
    weighted_key = jnp.einsum("hcd,hdk->hck", weights, key, precision=highest_precision)
    weighted_value = jnp.einsum("kzw,kwp->kzp", weights, value, precision=highest_precision)
    fresh_values = weighted_value - jnp.einsum(
        "imd,ide->ime", weighted_key, running_state, precision=highest_precision
    )
    score_matrix = (
        jnp.einsum("hck,hdk->hcd", query_rows, key, precision=highest_precision) * inclusive
    )
    output_rows = jnp.einsum(
        "imd,ide->ime", query_rows, running_state, precision=highest_precision
    ) + jnp.einsum("kzw,kwp->kzp", score_matrix, fresh_values, precision=highest_precision)
    running_state = running_state + jnp.einsum(
        "sbi,sbw->siw", key, fresh_values, precision=highest_precision
    )
    return (running_state, output_rows)


def local_mixer(projected, beta_logit, conv_taps, gain, token_segments, keep):
    masks = conv_masks(token_segments, conv_taps.shape[1])
    heads = beta_logit.shape[1]
    length = projected.shape[1]
    width = projected.shape[2] // heads
    blocks = keep.shape[0]
    size = length // blocks
    parts = []
    for which in range(3):
        convolved = jax.nn.silu(short_conv(projected[which], conv_taps[which], masks))
        parts.append(convolved.reshape(length, heads, width))
    query_rows = unit_rows(parts[0]) * width ** (-0.5)
    key = unit_rows(parts[1])
    value = parts[2]
    beta = jax.nn.sigmoid(beta_logit)

    def arrange(field):
        return field.reshape(blocks, size, heads, width).transpose(0, 2, 1, 3)

    beta_blocks = beta.reshape(blocks, size, heads).transpose(0, 2, 1)
    initial = jnp.zeros((heads, width, width), jnp.float32)
    final, outputs = lax.scan(
        jax.checkpoint(block_step),
        initial,
        (arrange(query_rows), arrange(key), arrange(value), beta_blocks, keep),
    )
    outputs = outputs.transpose(0, 2, 1, 3).reshape(length, heads, width)
    return rms_norm(outputs, gain, 1e-05).reshape(length, heads * width)


def norm_rows(values, gain):
    return rms_norm(values, gain, 1e-06)


def per_device(
    hidden_in,
    norm1_gain,
    qkv_weight,
    beta_weight,
    conv_weight,
    out_gain,
    out_weight,
    norm2_gain,
    gate_up_weight,
    down_weight,
    block_segments,
    cotangent,
):
    segments = block_segments[0]
    blocks = segments.shape[0]
    rows_in = hidden_in.astype(jnp.float32)
    normed_one, first_pull = jax.vjp(norm_rows, rows_in, norm1_gain)
    normed_low = normed_one.astype(jnp.bfloat16)
    normed_all = lax.all_gather(normed_low, "head", axis=0, tiled=True)
    length = normed_all.shape[0]
    token_segments = jnp.repeat(segments, length // blocks)
    keep = jnp.concatenate(
        [jnp.zeros((1,), jnp.float32), (segments[1:] == segments[:-1]).astype(jnp.float32)]
    )
    projected = jnp.einsum(
        "td,sde->ste", normed_all, qkv_weight, preferred_element_type=jnp.float32
    )
    beta_logit = jnp.dot(normed_all, beta_weight, preferred_element_type=jnp.float32)

    def mixer(projected_in, beta_in, conv_in, gain_in):
        return local_mixer(projected_in, beta_in, conv_in, gain_in, token_segments, keep)

    mixer_out, mixer_pull = jax.vjp(
        mixer, projected, beta_logit, conv_weight.astype(jnp.float32), out_gain
    )
    mixer_low = mixer_out.astype(jnp.bfloat16)
    piece = mixer_low
    attn_rows = lax.psum_scatter(
        jnp.dot(piece, out_weight, preferred_element_type=jnp.float32).astype(jnp.bfloat16),
        "head",
        scatter_dimension=0,
        tiled=True,
    ).astype(jnp.float32)
    middle = rows_in + attn_rows
    normed_two, second_pull = jax.vjp(norm_rows, middle, norm2_gain)
    second_low = normed_two.astype(jnp.bfloat16)
    second_all = lax.all_gather(second_low, "head", axis=0, tiled=True)
    gate_up = jnp.einsum(
        "td,sdf->stf", second_all, gate_up_weight, preferred_element_type=jnp.float32
    )
    sigmoid_gate = jax.nn.sigmoid(gate_up[0])
    silu_gate = gate_up[0] * sigmoid_gate
    hidden_low = (silu_gate * gate_up[1]).astype(jnp.bfloat16)
    piece = hidden_low
    ffn_rows = lax.psum_scatter(
        jnp.dot(piece, down_weight, preferred_element_type=jnp.float32).astype(jnp.bfloat16),
        "head",
        scatter_dimension=0,
        tiled=True,
    ).astype(jnp.float32)
    block_out = (middle + ffn_rows).astype(jnp.bfloat16)
    cot_all = lax.all_gather(cotangent, "head", axis=0, tiled=True)
    down_grad = jnp.einsum("tf,td->fd", hidden_low, cot_all, preferred_element_type=jnp.float32)
    hidden_grad = jnp.einsum("td,fd->tf", cot_all, down_weight, preferred_element_type=jnp.float32)
    gate_grad = hidden_grad * gate_up[1] * sigmoid_gate * (1.0 + gate_up[0] * (1.0 - sigmoid_gate))
    up_grad = hidden_grad * silu_gate
    gate_up_low = jnp.stack([gate_grad, up_grad]).astype(jnp.bfloat16)
    gate_up_grad = jnp.einsum(
        "td,stf->sdf", second_all, gate_up_low, preferred_element_type=jnp.float32
    )
    piece = gate_up_low
    second_grad = lax.psum_scatter(
        jnp.einsum("stf,sdf->td", piece, gate_up_weight, preferred_element_type=jnp.float32).astype(
            jnp.bfloat16
        ),
        "head",
        scatter_dimension=0,
        tiled=True,
    ).astype(jnp.float32)
    middle_part, norm2_gain_grad = second_pull(second_grad)
    middle_grad = cotangent.astype(jnp.float32) + middle_part
    mixer_grad_all = lax.all_gather(middle_grad.astype(jnp.bfloat16), "head", axis=0, tiled=True)
    out_grad = jnp.einsum(
        "tc,td->cd", mixer_low, mixer_grad_all, preferred_element_type=jnp.float32
    )
    mixer_in_grad = jnp.einsum(
        "td,cd->tc", mixer_grad_all, out_weight, preferred_element_type=jnp.float32
    )
    projected_grad, beta_logit_grad, conv_grad, out_gain_grad = mixer_pull(mixer_in_grad)
    projected_low = projected_grad.astype(jnp.bfloat16)
    beta_low = beta_logit_grad.astype(jnp.bfloat16)
    qkv_grad = jnp.einsum(
        "td,ste->sde", normed_all, projected_low, preferred_element_type=jnp.float32
    )
    beta_grad = jnp.einsum("td,th->dh", normed_all, beta_low, preferred_element_type=jnp.float32)
    piece = projected_low
    first_grad = lax.psum_scatter(
        (
            jnp.einsum("ste,sde->td", piece, qkv_weight, preferred_element_type=jnp.float32)
            + jnp.einsum("th,dh->td", beta_low, beta_weight, preferred_element_type=jnp.float32)
        ).astype(jnp.bfloat16),
        "head",
        scatter_dimension=0,
        tiled=True,
    ).astype(jnp.float32)
    rows_part, norm1_gain_grad = first_pull(first_grad)
    input_grad = middle_grad + rows_part
    norm1_gain_grad, norm2_gain_grad, out_gain_grad = lax.psum(
        (norm1_gain_grad, norm2_gain_grad, out_gain_grad), ("batch", "head")
    )
    qkv_grad, beta_grad, conv_grad, out_grad, gate_up_grad, down_grad = (
        lax.psum(qkv_grad.astype(jnp.bfloat16), "batch").astype(jnp.float32),
        lax.psum(beta_grad.astype(jnp.bfloat16), "batch").astype(jnp.float32),
        lax.psum(conv_grad.astype(jnp.bfloat16), "batch").astype(jnp.float32),
        lax.psum(out_grad.astype(jnp.bfloat16), "batch").astype(jnp.float32),
        lax.psum(gate_up_grad.astype(jnp.bfloat16), "batch").astype(jnp.float32),
        lax.psum(down_grad.astype(jnp.bfloat16), "batch").astype(jnp.float32),
    )
    return (
        block_out,
        input_grad,
        norm1_gain_grad,
        qkv_grad,
        beta_grad,
        conv_grad,
        out_gain_grad,
        out_grad,
        norm2_gain_grad,
        gate_up_grad,
        down_grad,
    )


def solution(mesh):
    placed = (
        P(("batch", "head"), None),
        P(),
        P(None, None, "head"),
        P(None, "head"),
        P(None, None, "head"),
        P(),
        P("head", None),
        P(),
        P(None, None, "head"),
        P("head", None),
        P("batch", None),
        P(("batch", "head"), None),
    )
    return jax.shard_map(
        per_device,
        mesh=mesh,
        in_specs=placed,
        out_specs=(
            P(("batch", "head"), None),
            P(("batch", "head"), None),
            P(),
            P(None, None, "head"),
            P(None, "head"),
            P(None, None, "head"),
            P(),
            P("head", None),
            P(),
            P(None, None, "head"),
            P("head", None),
        ),
        check_vma=False,
    )
```

profile of v0, /device:TPU:0, one launch (start us, length us, event | category | flops | bytes accessed | tf_op | source)
XLA Modules:
  0.0 1058.1 jit_solution(14581154062135182777)
XLA Ops:
  16.7 24.1 %all-gather.5.cloned.1.call-done = bf16[256,2048]{1,0:T(8,128)(2,1)} async-done(((bf16[64,2048]{1,0:T(8,128)(2,1)}), bf16[256,2048]{1,0:T(8,128)(2,1)}) %all-gather.5.cloned.1.call-update) | async-done | bytes 1048592 | tf_op jit(solution)/shard_map/all_gather | solution.py:121
  40.8 4.9 convolution_bitcast_fusion.4
  73.9 54.5 %while.38 = (s32[]{:T(128)}, f32[4,128,128]{2,1,0:T(8,128)S(1)}, f32[4,4,64,128]{3,2,1,0:T(8,128)}, f32[4,4,128,128]{3,2,1,0:T(8,128)}, f32[4]{0:T(128)}, /*inde...) while((s32[]{:T(128)}, f32[4,128,128]{2,1,0:T(8,128)S(1)}, ...), condition=%wide.region_4.5_spmd.clone, body=%wide.region_3.4_spmd.clone.sunk | while | flops 403464192 | bytes 6104994 | solution.py:89
  135.0 28.0 %reduce-scatter.5.cloned.1.call-done = bf16[64,2048]{1,0:T(8,128)(2,1)} async-done(((bf16[256,2048]{1,0:T(8,128)(2,1)}), bf16[64,2048]{1,0:T(8,128)(2,1)}) %reduce-scatter.5.cloned.1.call-update) | async-done | bytes 262160 | tf_op jit(solution)/shard_map/reduce_scatter | solution.py:140
  167.1 25.6 %all-gather.7.cloned.1.call-done = bf16[256,2048]{1,0:T(8,128)(2,1)} async-done(((bf16[64,2048]{1,0:T(8,128)(2,1)}), bf16[256,2048]{1,0:T(8,128)(2,1)}) %all-gather.7.cloned.1.call-update) | async-done | bytes 1048592 | tf_op jit(solution)/shard_map/all_gather | solution.py:149
  192.7 9.3 convolution_bitcast_fusion.1
  202.0 18.9 %all-gather.9.cloned.1.call-done = bf16[256,2048]{1,0:T(8,128)(2,1)} async-done(((bf16[64,2048]{1,0:T(8,128)(2,1)}), bf16[256,2048]{1,0:T(8,128)(2,1)}) %all-gather.9.cloned.1.call-update) | async-done | bytes 1048592 | tf_op jit(solution)/shard_map/all_gather | solution.py:164
  220.9 6.9 fusion.107
  228.9 8.5 fusion.96
  237.5 28.0 %reduce-scatter.9.cloned.1.call-done = bf16[64,2048]{1,0:T(8,128)(2,1)} async-done(((bf16[256,2048]{1,0:T(8,128)(2,1)}), bf16[64,2048]{1,0:T(8,128)(2,1)}) %reduce-scatter.9.cloned.1.call-update) | async-done | bytes 262160 | tf_op jit(solution)/shard_map/reduce_scatter | solution.py:174
  269.5 26.4 %all-gather.11.cloned.1.call-done = bf16[256,2048]{1,0:T(8,128)(2,1)} async-done(((bf16[64,2048]{1,0:T(8,128)(2,1)}), bf16[256,2048]{1,0:T(8,128)(2,1)}) %all-gather.11.cloned.1.call-update) | async-done | bytes 1048592 | tf_op jit(solution)/shard_map/all_gather | solution.py:184
  295.9 3.1 multiply_reduce_fusion.2
  304.0 119.3 %while.39 = (s32[]{:T(128)}, f32[4,128,128]{2,1,0:T(8,128)}, f32[4,4,64,128]{3,2,1,0:T(8,128)S(1)}, f32[4,4,64,128]{3,2,1,0:T(8,128)}, f32[4,4,64,128]{3,2,1,0:T...) while((s32[]{:T(128)}, f32[4,128,128]{2,1,0:T(8,128)}, ...), condition=%wide.region_15.16_spmd.clone, body=%wide.region_12.15_spmd.clone.sunk | while | flops 1083678464 | bytes 18188008 | solution.py:89
  441.9 5.2 convolution_bitcast_fusion.2
  448.6 5.5 convolution_convert_fusion.3
  454.3 4.2 convolution_convert_fusion
  458.5 6.5 convert_bitcast_fusion.1
  467.1 4.6 convert_bitcast_fusion.2
  472.1 28.4 %all-reduce.39 = (bf16[2048,4]{0,1:T(4,128)(2,1)S(1)}, bf16[3,4,512]{2,1,0:T(4,128)(2,1)S(1)}) all-reduce(bf16[2048,4]{0,1:T(4,128)(2,1)S(1)} %convolution_convert_fusion.4, bf16[3,4,512]{2,1,0:T(4,128)(2,1)S(1)} %add_convert_fusion.2), channel_id=1, replica_groups=mesh['batch'=8,'head'=4] {'batch'}, use_global_device_ids=true, to_apply=%region_23.24 | all-reduce | flops 14336 | bytes 57344 | tf_op jit(solution)/shard_map/psum | solution.py:215
  503.0 38.7 %all-reduce.38 = (f32[2048]{0:T(1024)}, f32[128]{0:T(128)}, f32[2048]{0:T(1024)}) all-reduce(f32[2048]{0:T(1024)S(1)} %get-tuple-element.622, f32[128]{0:T(128)S(1)} %bitcast_reduce_fusion, f32[2048]{0:T(1024)S(1)} %copy-done.74), channel_id=1, replica_groups=mesh['batch'=8,'head'=4] {'batch','head'}, use_global_device_ids=true, to_apply=%region_21.22 | all-reduce | flops 4224 | bytes 33792 | tf_op jit(solution)/shard_map/psum | solution.py:210
  544.1 469.2 %all-reduce.43.cloned.1.call-done = (bf16[3,2048,512]{1,2,0:T(8,128)(2,1)}, bf16[2,2048,1408]{1,2,0:T(8,128)(2,1)}, bf16[512,2048]{1,0:T(8,128)(2,1)}, bf16[1408,2048]{1,0:T(8,128)(2,1)}) async-done(((bf16[3,2048,512]{1,2,0:T(8,128)(2,1)}, bf16[2,2048,1408]{1,2,0:T(8,128)(2,1)}, bf16[512,2048]{1,0:T(8,128)(2,1)}, bf16[1408,2048]{1,0:T(8,128)(2,1)}), (bf16[3,2048,512]{1,2,0:T(8,128)(2,1)}, ...) | async-done | bytes 25690128 | tf_op jit(solution)/shard_map/psum | solution.py:214
  1013.3 17.0 %copy.272 = f32[2,2048,1408]{2,1,0:T(8,128)} copy(bf16[2,2048,1408]{1,2,0:T(8,128)(2,1)} %get-tuple-element.676) | data formatting | bytes 34603008
  1030.3 9.4 copy.271
  1039.7 8.8 convert_element_type.177
  (707 shorter events, 258.7 us)
Async XLA Ops:
  7.2 126.1 %copy-start = (bf16[512,2048]{1,0:T(8,128)(2,1)S(1)}, bf16[512,2048]{1,0:T(8,128)(2,1)}, u32[]{:S(2)}) copy-start(bf16[512,2048]{1,0:T(8,128)(2,1)} %param.22) | copy-start | bytes 6291460
  7.2 33.6 %all-gather.5.cloned.1.call-start = ((), (), s32[]{:S(2)}) async-start(), calls=%async_computation.4 | async-start | bytes 1310720 | tf_op jit(solution)/shard_map/all_gather | solution.py:121
  11.5 151.6 %reduce-scatter.5.cloned.1.call-start = ((), (), s32[]{:S(2)}) async-start(), calls=%async_computation.5 | async-start | bytes 1310720 | tf_op jit(solution)/shard_map/reduce_scatter | solution.py:140
  15.7 39.5 %copy-start.100 = (f32[256]{0:T(256)}, f32[256]{0:T(256)S(1)}, u32[]{:S(2)}) copy-start(f32[256]{0:T(256)S(1)} %get-tuple-element.767) | copy-start | bytes 3076
  15.7 39.5 %copy-start.102 = (f32[256]{0:T(256)}, f32[256]{0:T(256)S(1)}, u32[]{:S(2)}) copy-start(f32[256]{0:T(256)S(1)} %get-tuple-element.769) | copy-start | bytes 3076
  15.7 39.5 %copy-start.104 = (f32[256]{0:T(256)}, f32[256]{0:T(256)S(1)}, u32[]{:S(2)}) copy-start(f32[256]{0:T(256)S(1)} %get-tuple-element.768) | copy-start | bytes 3076
  16.7 38.5 %copy-start.92 = (f32[1,1,512]{2,1,0:T(1,128)}, f32[1,1,512]{2,1,0:T(1,128)S(1)}, u32[]{:S(2)}) copy-start(f32[1,1,512]{2,1,0:T(1,128)S(1)} %get-tuple-element.747) | copy-start | bytes 6148
  16.7 38.5 %copy-start.94 = (f32[1,1,512]{2,1,0:T(1,128)}, f32[1,1,512]{2,1,0:T(1,128)S(1)}, u32[]{:S(2)}) copy-start(f32[1,1,512]{2,1,0:T(1,128)S(1)} %get-tuple-element.750) | copy-start | bytes 6148
  16.7 38.5 %copy-start.96 = (f32[1,1,512]{2,1,0:T(1,128)}, f32[1,1,512]{2,1,0:T(1,128)S(1)}, u32[]{:S(2)}) copy-start(f32[1,1,512]{2,1,0:T(1,128)S(1)} %get-tuple-element.748) | copy-start | bytes 6148
  16.7 38.5 %copy-start.98 = (f32[1,1,512]{2,1,0:T(1,128)}, f32[1,1,512]{2,1,0:T(1,128)S(1)}, u32[]{:S(2)}) copy-start(f32[1,1,512]{2,1,0:T(1,128)S(1)} %get-tuple-element.749) | copy-start | bytes 6148
  135.0 57.7 %all-gather.7.cloned.1.call-start = ((), (), s32[]{:S(2)}) async-start(), calls=%async_computation.6 | async-start | bytes 1310720 | tf_op jit(solution)/shard_map/all_gather | solution.py:149
  164.2 103.1 %copy-start.108 = (f32[64]{0:T(128)}, f32[64]{0:T(128)S(1)}, u32[]{:S(2)}) copy-start(f32[64]{0:T(128)S(1)} %fusion.139) | copy-start | bytes 772
  166.0 54.9 %all-gather.9.cloned.1.call-start = ((), (), s32[]{:S(2)}) async-start(), calls=%async_computation.8 | async-start | bytes 1310720 | tf_op jit(solution)/shard_map/all_gather | solution.py:164
  166.6 98.9 %reduce-scatter.9.cloned.1.call-start = ((), (), s32[]{:S(2)}) async-start(), calls=%async_computation.9 | async-start | bytes 1310720 | tf_op jit(solution)/shard_map/reduce_scatter | solution.py:174
  237.4 58.4 %all-gather.11.cloned.1.call-start = ((), (), s32[]{:S(2)}) async-start(), calls=%async_computation.10 | async-start | bytes 1310720 | tf_op jit(solution)/shard_map/all_gather | solution.py:184
  269.2 232.5 %reduce-scatter.11.cloned.1.call-start = ((), (), s32[]{:S(2)}) async-start(), calls=%async_computation.11 | async-start | bytes 1310720 | tf_op jit(solution)/shard_map/reduce_scatter | solution.py:199
  448.6 93.2 %reduce-scatter.7.cloned.1.call-start = ((), (), s32[]{:S(2)}) async-start(), calls=%async_computation.7 | async-start | bytes 1310720 | tf_op jit(solution)/shard_map/reduce_scatter | solution.py:157
  454.2 559.1 %all-reduce.43.cloned.1.call-start = ((), (), s32[]{:S(2)}) async-start(), calls=%async_computation.12 | async-start | bytes 51380224 | tf_op jit(solution)/shard_map/psum | solution.py:214
  471.7 70.0 %copy-start.116 = (f32[64]{0:T(128)S(1)}, f32[64]{0:T(128)}, u32[]{:S(2)}) copy-start(f32[64]{0:T(128)} %copy-done.115) | copy-start | bytes 772
  471.7 70.1 %copy-start.9 = (bf16[64,2048]{1,0:T(8,128)(2,1)S(1)}, bf16[64,2048]{1,0:T(8,128)(2,1)}, u32[]{:S(2)}) copy-start(bf16[64,2048]{1,0:T(8,128)(2,1)} %reduce-scatter.5.cloned.1.call-done) | copy-start | bytes 786436
  471.7 70.1 %copy-start.41 = (bf16[64,2048]{1,0:T(8,128)(2,1)S(1)}, bf16[64,2048]{1,0:T(8,128)(2,1)}, u32[]{:S(2)}) copy-start(bf16[64,2048]{1,0:T(8,128)(2,1)} %param.27) | copy-start | bytes 786436
  471.7 70.0 %copy-start.42 = (bf16[64,2048]{1,0:T(8,128)(2,1)S(1)}, bf16[64,2048]{1,0:T(8,128)(2,1)}, u32[]{:S(2)}) copy-start(bf16[64,2048]{1,0:T(8,128)(2,1)} %reduce-scatter.9.cloned.1.call-done) | copy-start | bytes 786436
  471.7 70.0 %copy-start.109 = (f32[64]{0:T(128)S(1)}, f32[64]{0:T(128)}, u32[]{:S(2)}) copy-start(f32[64]{0:T(128)} %copy-done.108) | copy-start | bytes 772
  471.7 70.0 %copy-start.114 = (f32[64]{0:T(128)S(1)}, f32[64]{0:T(128)}, u32[]{:S(2)}) copy-start(f32[64]{0:T(128)} %copy-done.113) | copy-start | bytes 772
  (102 other events, 807.9 us)
Sparse Core Ops, SparseCore 0:
  11.6 29.2 all-gather.4
  135.1 27.9 reduce-scatter.4
  166.1 26.4 all-gather.6
  194.4 26.4 all-gather.8
  237.5 27.9 reduce-scatter.8
  269.3 26.4 all-gather.10
  448.7 27.9 reduce-scatter.10
  479.5 27.9 reduce-scatter.6
  511.6 501.7 all-reduce.42
where the time goes:
time: 1070 us; the launch traced here: 1060 us
  waiting for transfers between devices  621 us (58%)
  matrix products  200 us (19%)
  local copies, waits for them, and re-layouts  85.4 us (8%)
  blocking collectives  67 us (6%)
  other arithmetic  65.9 us (6%)
  between operations  15.8 us (1%)
    psum x1, waiting for transfers between devices, per_device(): lax.psum(qkv_grad.astype(jnp.bfloat16), 'batch').astype(jnp.float32)  469 us
    psum x1, blocking collectives, per_device(): lax.psum((norm1_gain_grad, norm2_gain_grad, out_gain_grad), ('batch', 'he...  38.7 us
    unnamed x237, local copies, waits for them, and re-layouts  34.6 us
    psum x1, blocking collectives, per_device(): lax.psum(beta_grad.astype(jnp.bfloat16), 'batch').astype(jnp.float32)  28.4 us
    reduce_scatter x1, waiting for transfers between devices, per_device(): lax.psum_scatter(jnp.einsum('stf,sdf->td', piece, gate_up_weight, preferr...  28 us
    reduce_scatter x1, waiting for transfers between devices, per_device(): lax.psum_scatter(jnp.dot(piece, out_weight, preferred_element_type=jnp.fl...  28 us
    all_gather x1, waiting for transfers between devices, per_device(): lax.all_gather(middle_grad.astype(jnp.bfloat16), 'head', axis=0, tiled=True)  26.4 us
    all_gather x1, waiting for transfers between devices, per_device(): second_all = lax.all_gather(second_low, 'head', axis=0, tiled=True)  25.6 us
  transfers between devices with their start and end apart: 9, of which 7 were waited for; matrix products, arithmetic and copies ran while one was open for 4% of the time, Pallas kernels for 0%

commit v1 on v0

v1 whole, which is shorter than its diff:
```python
import jax
import jax.numpy as jnp
from jax import lax
from jax.sharding import Mesh, PartitionSpec as P

highest_precision = lax.Precision.HIGHEST
f32 = jnp.float32
bf16 = jnp.bfloat16


def rms_norm(values, gain, epsilon):
    return values * lax.rsqrt(jnp.mean(values * values, axis=-1, keepdims=True) + epsilon) * gain


def unit_rows(field):
    return field * lax.rsqrt(jnp.sum(field * field, axis=-1, keepdims=True) + 1e-06)


def conv_masks(token_segments, taps):
    masks = []
    for shift in range(1, taps):
        earlier = jnp.concatenate([jnp.full((shift,), -1, jnp.int32), token_segments[:-shift]])
        masks.append((earlier == token_segments).astype(f32)[:, None])
    return masks


def short_conv(values, taps, masks):
    result = values * taps[0]
    for shift in range(1, taps.shape[0]):
        moved = jnp.concatenate([jnp.zeros((shift, values.shape[1]), f32), values[:-shift]], axis=0)
        result = result + moved * taps[shift] * masks[shift - 1]
    return result


def block_step(running_state, inputs):
    query_rows, key, value, beta, keep = inputs
    running_state = running_state * keep
    length = key.shape[1]
    strict = jnp.tril(jnp.ones((length, length), f32), -1)
    inclusive = jnp.tril(jnp.ones((length, length), f32))
    keyed = (
        jnp.einsum("hck,hdk->hcd", key * beta[:, :, None], key, precision=highest_precision)
        * strict
    )
    power = -keyed
    inverse = jnp.eye(length, dtype=f32) + power
    for level in range(length.bit_length() - 2):
        power = jnp.einsum("hcd,hde->hce", power, power, precision=highest_precision)
        inverse = inverse + jnp.einsum("hcd,hde->hce", inverse, power, precision=highest_precision)
    weights = inverse * beta[:, None, :]
    weighted_key = jnp.einsum("hcd,hdk->hck", weights, key, precision=highest_precision)
    weighted_value = jnp.einsum("kzw,kwp->kzp", weights, value, precision=highest_precision)
    fresh_values = weighted_value - jnp.einsum(
        "imd,ide->ime", weighted_key, running_state, precision=highest_precision
    )
    score_matrix = (
        jnp.einsum("hck,hdk->hcd", query_rows, key, precision=highest_precision) * inclusive
    )
    output_rows = jnp.einsum(
        "imd,ide->ime", query_rows, running_state, precision=highest_precision
    ) + jnp.einsum("kzw,kwp->kzp", score_matrix, fresh_values, precision=highest_precision)
    running_state = running_state + jnp.einsum(
        "sbi,sbw->siw", key, fresh_values, precision=highest_precision
    )
    return (running_state, output_rows)


def local_mixer(projected, beta_logit, conv_taps, gain, token_segments, keep):
    masks = conv_masks(token_segments, conv_taps.shape[1])
    heads = beta_logit.shape[1]
    length = projected.shape[1]
    width = projected.shape[2] // heads
    blocks = keep.shape[0]
    size = length // blocks
    parts = []
    for which in range(3):
        convolved = jax.nn.silu(short_conv(projected[which], conv_taps[which], masks))
        parts.append(convolved.reshape(length, heads, width))
    query_rows = unit_rows(parts[0]) * width ** (-0.5)
    key = unit_rows(parts[1])
    value = parts[2]
    beta = jax.nn.sigmoid(beta_logit)

    def arrange(field):
        return field.reshape(blocks, size, heads, width).transpose(0, 2, 1, 3)

    beta_blocks = beta.reshape(blocks, size, heads).transpose(0, 2, 1)
    initial = jnp.zeros((heads, width, width), f32)
    final, outputs = lax.scan(
        jax.checkpoint(block_step),
        initial,
        (arrange(query_rows), arrange(key), arrange(value), beta_blocks, keep),
    )
    outputs = outputs.transpose(0, 2, 1, 3).reshape(length, heads, width)
    return rms_norm(outputs, gain, 1e-05).reshape(length, heads * width)


def norm_rows(values, gain):
    return rms_norm(values, gain, 1e-06)


def dot(equation, left, right):
    return jnp.einsum(equation, left, right, preferred_element_type=f32)


def per_device(heads_axis, hidden_in, norm1_gain, qkv_weight, beta_weight, conv_weight, out_gain,
               out_weight, norm2_gain, gate_up_weight, down_weight, block_segments, cotangent):
    segments = block_segments[0]
    blocks = segments.shape[0]
    rows, model = hidden_in.shape
    shards = heads_axis
    length = rows * shards
    me = lax.axis_index("head")
    mine_z = lax.axis_index("z")

    def exchange(parts):
        return [parts[0]] + [
            lax.ppermute(parts[k], "head", [(i, i ^ k) for i in range(shards)])
            for k in range(1, shards)
        ]

    def gather_rows(own):
        return exchange([own] * shards)

    def scatter_sum(product):
        pieces = exchange([product[k * rows:(k + 1) * rows] for k in range(shards)])
        total = pieces[0].astype(f32)
        for piece in pieces[1:]:
            total = total + piece.astype(f32)
        return total

    def reorder(field, axis):
        pieces = [
            lax.dynamic_slice_in_dim(field, (me ^ k) * rows, rows, axis) for k in range(shards)
        ]
        return jnp.concatenate(pieces, axis)

    token_segments = jnp.repeat(segments, length // blocks)
    keep = jnp.concatenate(
        [jnp.zeros((1,), f32), (segments[1:] == segments[:-1]).astype(f32)]
    )
    hidden_parts = gather_rows(hidden_in)
    normed_all = jnp.concatenate(
        [norm_rows(part.astype(f32), norm1_gain).astype(bf16) for part in hidden_parts]
    )
    rows_in = hidden_in.astype(f32)
    cot_line = lax.all_gather(cotangent, "z", axis=0, tiled=True)
    hidden_line = lax.all_gather(hidden_in, "z", axis=0, tiled=True)
    line = cot_line.shape[0] // rows
    cot_every = jnp.concatenate(gather_rows(cot_line))
    hidden_every = jnp.stack(gather_rows(hidden_line)).reshape(shards, line, rows, model)

    projected = dot("td,sde->ste", normed_all, qkv_weight)
    beta_logit = dot("td,dh->th", normed_all, beta_weight)

    def mixer(projected_in, beta_in, conv_in, gain_in):
        return local_mixer(projected_in, beta_in, conv_in, gain_in, token_segments, keep)

    mixer_out, mixer_pull = jax.vjp(
        mixer, reorder(projected, 1), reorder(beta_logit, 0), conv_weight.astype(f32), out_gain
    )
    mixer_low = reorder(mixer_out.astype(bf16), 0)
    attn_rows = scatter_sum(dot("tc,cd->td", mixer_low, out_weight).astype(bf16))
    middle = rows_in + attn_rows
    normed_two, second_pull = jax.vjp(norm_rows, middle, norm2_gain)
    second_low = normed_two.astype(bf16)
    second_all = jnp.concatenate(gather_rows(second_low))
    second_line = lax.all_gather(second_low, "z", axis=0, tiled=True)
    second_every = jnp.concatenate(gather_rows(second_line))
    cot_all = lax.dynamic_index_in_dim(
        cot_every.reshape(shards, line, rows, model), mine_z, 1, False
    ).reshape(length, model)

    def feed_forward(second, cot):
        gate_up = dot("td,sdf->stf", second, gate_up_weight)
        sigmoid_gate = jax.nn.sigmoid(gate_up[0])
        silu_gate = gate_up[0] * sigmoid_gate
        hidden_low = (silu_gate * gate_up[1]).astype(bf16)
        hidden_grad = dot("td,fd->tf", cot, down_weight)
        gate_grad = hidden_grad * gate_up[1] * sigmoid_gate * (1.0 + gate_up[0] * (1.0 - sigmoid_gate))
        up_grad = hidden_grad * silu_gate
        return hidden_low, jnp.stack([gate_grad, up_grad]).astype(bf16)

    hidden_low, gate_up_low = feed_forward(second_all, cot_all)
    second_grad = scatter_sum(dot("stf,sdf->td", gate_up_low, gate_up_weight).astype(bf16))
    ffn_rows = scatter_sum(dot("tf,fd->td", hidden_low, down_weight).astype(bf16))
    block_out = (middle + ffn_rows).astype(bf16)
    middle_part, norm2_gain_grad = second_pull(second_grad)
    middle_grad = cotangent.astype(f32) + middle_part
    attn_grad_all = jnp.concatenate(gather_rows(middle_grad.astype(bf16)))
    mixer_in_grad = dot("td,cd->tc", attn_grad_all, out_weight)
    out_grad = dot("tc,td->cd", mixer_low, attn_grad_all).astype(bf16)

    hidden_every_low, gate_up_every = feed_forward(second_every, cot_every)
    down_grad = dot("tf,td->fd", hidden_every_low, cot_every).astype(bf16)
    gate_up_grad = dot("td,stf->sdf", second_every, gate_up_every).astype(bf16)

    projected_grad, beta_logit_grad, conv_grad, out_gain_grad = mixer_pull(reorder(mixer_in_grad, 0))
    projected_low = reorder(projected_grad.astype(bf16), 1)
    beta_low = reorder(beta_logit_grad.astype(bf16), 0)
    first_grad = scatter_sum(
        (dot("ste,sde->td", projected_low, qkv_weight) + dot("th,dh->td", beta_low, beta_weight)).astype(bf16)
    )
    r1 = lax.rsqrt(jnp.mean(rows_in * rows_in, axis=-1, keepdims=True) + 1e-06)
    m1 = rows_in * r1
    e1 = first_grad * norm1_gain
    norm1_gain_grad = jnp.sum(first_grad * m1, axis=0)
    input_grad = middle_grad + r1 * (e1 - m1 * jnp.mean(e1 * m1, axis=-1, keepdims=True))

    projected_line = lax.all_gather(projected_low, "z", axis=0)
    normed_every = norm_rows(hidden_every.astype(f32), norm1_gain).astype(bf16)
    normed_every = normed_every.transpose(1, 0, 2, 3).reshape(line, length, model)
    qkv_grad = dot("ztd,zste->sde", normed_every, projected_line).astype(bf16)
    beta_grad = dot("td,th->dh", normed_all, beta_low)

    def pair_sum(partial):
        other = lax.ppermute(partial, "core", [(0, 1), (1, 0)])
        return partial.astype(f32) + other.astype(f32)

    down_grad, gate_up_grad, qkv_grad = pair_sum(down_grad), pair_sum(gate_up_grad), pair_sum(qkv_grad)
    out_grad = lax.psum(out_grad, ("z", "core")).astype(f32)
    gains = jnp.concatenate([norm1_gain_grad, norm2_gain_grad, out_gain_grad])[None]
    gains = jnp.sum(lax.all_gather(gains, ("z", "core", "head"), axis=0, tiled=True), axis=0)
    small = jnp.concatenate([beta_grad.T.reshape(-1), conv_grad.reshape(-1)])[None]
    small = jnp.sum(lax.all_gather(small, ("z", "core"), axis=0, tiled=True), axis=0)
    beta_size = beta_grad.size
    beta_grad = small[:beta_size].reshape(beta_grad.shape[::-1]).T
    conv_grad = small[beta_size:].reshape(conv_grad.shape)
    return (
        block_out,
        input_grad,
        gains[:model],
        qkv_grad,
        beta_grad,
        conv_grad,
        gains[2 * model:],
        out_grad,
        gains[model:2 * model],
        gate_up_grad,
        down_grad,
    )


def solution(mesh):
    groups, shards = mesh.devices.shape
    split = Mesh(mesh.devices.reshape(groups // 2, 2, shards), ("z", "core", "head"))
    tokens = P(("z", "core", "head"), None)
    placed = (
        tokens,
        P(),
        P(None, None, "head"),
        P(None, "head"),
        P(None, None, "head"),
        P(),
        P("head", None),
        P(),
        P(None, None, "head"),
        P("head", None),
        P(("z", "core"), None),
        tokens,
    )
    return jax.shard_map(
        lambda *args: per_device(shards, *args),
        mesh=split,
        in_specs=placed,
        out_specs=(
            tokens,
            tokens,
            P(),
            P(None, None, "head"),
            P(None, "head"),
            P(None, None, "head"),
            P(),
            P("head", None),
            P(),
            P(None, None, "head"),
            P("head", None),
        ),
        check_vma=False,
    )
```

time: 1070 us -> 751 us (0.70)
  waiting for transfers between devices: 621 us -> 146 us
  matrix products: 200 us -> 254 us
  starting transfers between devices: 0.83 us -> 37.7 us
  local copies, waits for them, and re-layouts: 85.4 us -> 109 us
  other arithmetic: 65.9 us -> 89.2 us
  blocking collectives: 67 us -> 88.5 us
    psum x1, waiting for transfers between devices: 469 us -> 0.01 us  [per_device(): out_grad = lax.psum(out_grad, ('z', 'core')).astype(f32)]
    ppermute x0 -> x33, waiting for transfers between devices: none -> 145 us  [the longest x30 145 us: exchange(): lax.ppermute(parts[k], 'head', [(i, i ^ k) for i in range(shards)])]
    all_gather x4, waiting for transfers between devices: 95 us -> 0.01 us  [the longest x1 0.01 us: per_device(): cot_line = lax.all_gather(cotangent, 'z', axis=0, tiled=True)]
    all_gather x0 -> x2, blocking collectives: none -> 88.5 us  [the longest x1 73.6 us: per_device(): lax.all_gather(gains, ('z', 'core', 'head'), axis=0, tiled=True)]
    psum x2 -> x0, blocking collectives: 67 us -> none  [the longest x1 38.7 us: per_device(): lax.psum((norm1_gain_grad, norm2_gain_grad, out_gain_grad), ('batch', 'he...]
    dot_general x15 -> x17, matrix products: 64.4 us -> 122 us  [dot(): return jnp.einsum(equation, left, right, preferred_element_type=f32)]
    reduce_scatter x4 -> x0, waiting for transfers between devices: 56.1 us -> none  [the longest x1 28 us: per_device(): lax.psum_scatter(jnp.einsum('stf,sdf->td', piece, gate_up_weight, preferr...]
    add x10 -> x13, other arithmetic: 2.87 us -> 42.4 us  [the longest x3 41.3 us: pair_sum(): return partial.astype(f32) + other.astype(f32)]
  transfers between devices with their start and end apart: 9 -> 38, of which waited for: 7 -> 19; matrix products, arithmetic and copies ran while one was open for 4% -> 55% of each run, Pallas kernels for 0% -> 0%
where the time goes in v1:
time: 751 us; the launch traced here: 743 us
  matrix products  254 us (34%)
  waiting for transfers between devices  146 us (19%)
  local copies, waits for them, and re-layouts  109 us (15%)
  other arithmetic  89.2 us (12%)
  blocking collectives  88.5 us (12%)
  starting transfers between devices  37.7 us (5%)
  between operations  15.7 us (2%)
    ppermute x30, waiting for transfers between devices, exchange(): lax.ppermute(parts[k], 'head', [(i, i ^ k) for i in range(shards)])  145 us
    dot_general x17, matrix products, dot(): return jnp.einsum(equation, left, right, preferred_element_type=f32)  122 us
    all_gather x1, blocking collectives, per_device(): lax.all_gather(gains, ('z', 'core', 'head'), axis=0, tiled=True)  73.6 us
    unnamed x243, local copies, waits for them, and re-layouts  50.2 us
    add x3, other arithmetic, pair_sum(): return partial.astype(f32) + other.astype(f32)  41.3 us
    ppermute x30, starting transfers between devices, exchange(): lax.ppermute(parts[k], 'head', [(i, i ^ k) for i in range(shards)])  36.8 us
    dot_general x80, matrix products, block_step(): jnp.einsum('hcd,hde->hce', inverse, power, precision=highest_precision)  25 us
    dot_general x80, matrix products, block_step(): jnp.einsum('hcd,hde->hce', power, power, precision=highest_precision)  24.9 us
  transfers between devices with their start and end apart: 38, of which 19 were waited for; matrix products, arithmetic and copies ran while one was open for 55% of the time, Pallas kernels for 0%

profile of v1, /device:TPU:0, one launch (start us, length us, event | category | flops | bytes accessed | tf_op | source)
XLA Modules:
  0.0 742.8 jit_solution(14792911789845498493)
XLA Ops:
  58.1 49.4 %while.38 = (s32[]{:T(128)}, f32[4,128,128]{2,1,0:T(8,128)S(1)}, f32[4,4,64,128]{3,2,1,0:T(8,128)S(1)}, f32[4,4,128,128]{3,2,1,0:T(8,128)}, f32[4]{0:T(128)}, /*...) while((s32[]{:T(128)}, f32[4,128,128]{2,1,0:T(8,128)S(1)}, ...), condition=%wide.region_7.8_spmd.clone, body=%wide.region_6.7_spmd.clone.sunk | while | flops 403464192 | bytes 6104497 | solution.py:89
  139.8 9.4 %convolution_bitcast_fusion.2 = f32[2,256,1408]{2,1,0:T(8,128)} fusion(bf16[2,2048,1408]{2,1,0:T(8,128)(2,1)} %param.24, bf16[64,2048]{1,0:T(8,128)(2,1)} %collective-permute-done.8, bf16[64,2048]{1,0:T(8,128)(2,1)} %collective-permute-done.7, bf16[64,2048]{1,0:T(8,128)(2,1)} %collective-permute-done.6, bf16[64,2048]{1,0:T(8,128)(2,1)} %multiply_convert_fusion.8), kind=kOutput, calls=%fused_computation.181 | convolution fusion | flops 2956984320 | bytes 15466496 | tf_op jit(solution)/shard_map/td,sdf->stf/dot_general | solution.py:103
  163.9 12.7 %collective-permute-done.12 = bf16[256,2048]{1,0:T(8,128)(2,1)} collective-permute-done((bf16[256,2048]{1,0:T(8,128)(2,1)}, bf16[256,2048]{1,0:T(8,128)(2,1)}, u32[]{:S(2)}, u32[]{:S(2)}) %collective-permute-start.12) | collective-permute-done | bytes 1048608 | tf_op jit(solution)/shard_map/ppermute | solution.py:118
  183.9 15.6 %collective-permute-done.14 = bf16[256,2048]{1,0:T(8,128)(2,1)} collective-permute-done((bf16[256,2048]{1,0:T(8,128)(2,1)}, bf16[256,2048]{1,0:T(8,128)(2,1)}, u32[]{:S(2)}, u32[]{:S(2)}) %collective-permute-start.14) | collective-permute-done | bytes 1048608 | tf_op jit(solution)/shard_map/ppermute | solution.py:118
  209.5 7.5 %fusion.107 = bf16[256,2048]{1,0:T(8,128)(2,1)S(1)} fusion(bf16[2,2048,1408]{2,1,0:T(8,128)(2,1)} %param.24, bf16[1,256,1408]{2,1,0:T(8,128)(2,1)S(1)} %get-tuple-element.714, bf16[1,256,1408]{2,1,0:T(8,128)(2,1)S(1)} %get-tuple-element.713), kind=kOutput, calls=%fused_computation.188 | convolution fusion | flops 2954035200 | bytes 14024704 | tf_op jit(solution)/shard_map/stf,sdf->td/dot_general | solution.py:103
  218.0 15.2 %collective-permute-done.26 = bf16[256,2048]{1,0:T(8,128)(2,1)S(1)} collective-permute-done((bf16[256,2048]{1,0:T(8,128)(2,1)}, bf16[256,2048]{1,0:T(8,128)(2,1)S(1)}, u32[]{:S(2)}, u32[]{:S(2)}) %collective-permute-start.26) | collective-permute-done | bytes 1048608 | tf_op jit(solution)/shard_map/ppermute | solution.py:118
  234.5 12.5 %collective-permute-done.25 = bf16[256,2048]{1,0:T(8,128)(2,1)S(1)} collective-permute-done((bf16[256,2048]{1,0:T(8,128)(2,1)}, bf16[256,2048]{1,0:T(8,128)(2,1)S(1)}, u32[]{:S(2)}, u32[]{:S(2)}) %collective-permute-start.25) | collective-permute-done | bytes 1048608 | tf_op jit(solution)/shard_map/ppermute | solution.py:118
  248.0 7.2 collective-permute-done.24
  265.4 25.5 %collective-permute-done.16 = bf16[64,2048]{1,0:T(8,128)(2,1)} collective-permute-done((bf16[64,2048]{1,0:T(8,128)(2,1)}, bf16[64,2048]{1,0:T(8,128)(2,1)}, u32[]{:S(2)}, u32[]{:S(2)}) %collective-permute-start.16) | collective-permute-done | bytes 262176 | tf_op jit(solution)/shard_map/ppermute | solution.py:118
  311.2 15.6 %collective-permute-done.19 = bf16[64,2048]{1,0:T(8,128)(2,1)S(1)} collective-permute-done((bf16[64,2048]{1,0:T(8,128)(2,1)S(1)}, bf16[64,2048]{1,0:T(8,128)(2,1)S(1)}, u32[]{:S(2)}, u32[]{:S(2)}) %collective-permute-start.19) | collective-permute-done | bytes 262176 | tf_op jit(solution)/shard_map/ppermute | solution.py:118
  333.9 111.5 %while.39 = (s32[]{:T(128)}, f32[4,128,128]{2,1,0:T(8,128)S(1)}, f32[4,4,64,128]{3,2,1,0:T(8,128)}, f32[4,4,64,128]{3,2,1,0:T(8,128)}, f32[4,4,64,128]{3,2,1,0:T...) while((s32[]{:T(128)}, f32[4,128,128]{2,1,0:T(8,128)S(1)}, ...), condition=%wide.region_15.16_spmd.clone, body=%wide.region_12.15_spmd.clone.sunk | while | flops 1083678464 | bytes 18190672 | solution.py:89
  463.5 21.5 %convolution_bitcast_fusion.1 = f32[2,1024,1408]{2,1,0:T(8,128)} fusion(bf16[2,2048,1408]{2,1,0:T(8,128)(2,1)} %param.24, bf16[256,2048]{1,0:T(8,128)(2,1)} %collective-permute-done.30, bf16[256,2048]{1,0:T(8,128)(2,1)} %collective-permute-done.29, bf16[256,2048]{1,0:T(8,128)(2,1)} %collective-permute-done.28, ...), kind=kOutput, calls=%fused_computation.166 | convolution fusion | flops 11827937280 | bytes 27262976 | tf_op jit(solution)/shard_map/td,sdf->stf/dot_general | solution.py:103
  485.0 13.8 %fusion.106 = (bf16[1,1024,1408]{2,1,0:T(8,128)(2,1)S(1)}, bf16[1,1024,1408]{2,1,0:T(8,128)(2,1)}) fusion(f32[2,1024,1408]{2,1,0:T(8,128)} %convolution_bitcast_fusion.1, bf16[1024,2048]{1,0:T(8,128)(2,1)S(1)} %copy-done.38, bf16[1408,2048]{1,0:T(8,128)(2,1)} %param.25), kind=kOutput, calls=%fused_computation.184 | convolution fusion | flops 5924323328 | bytes 27262976 | tf_op jit(solution)/shard_map/td,fd->tf/dot_general | solution.py:103
  498.8 17.8 %convert_bitcast_fusion.1 = bf16[2,2048,1408]{1,2,0:T(8,128)(2,1)} fusion(bf16[1,1024,1408]{2,1,0:T(8,128)(2,1)} %get-tuple-element.712, bf16[1,1024,1408]{2,1,0:T(8,128)(2,1)S(1)} %get-tuple-element.711, bf16[256,2048]{1,0:T(8,128)(2,1)} %collective-permute-done.30, bf16[256,2048]{1,0:T(8,128)(2,1)} %collective-permute-done.29, ...), kind=kOutput, calls=%fused_computation.159 | convolution fusion | flops 11836588032 | bytes 21495808 | tf_op jit(solution)/shard_map/td,stf->sdf/dot_general | solution.py:103
  516.7 12.8 %convolution_convert_fusion = bf16[1408,2048]{1,0:T(8,128)(2,1)} fusion(bf16[1024,2048]{1,0:T(8,128)(2,1)S(1)} %copy-done.38, f32[2,1024,1408]{2,1,0:T(8,128)} %convolution_bitcast_fusion.1), kind=kOutput, calls=%fused_computation.165 | convolution fusion | flops 5917114368 | bytes 21495808 | tf_op jit(solution)/shard_map/tf,td->fd/dot_general | solution.py:103
  530.0 11.7 %fusion.99 = bf16[3,2048,512]{1,2,0:T(8,128)(2,1)} fusion(bf16[4,3,256,512]{3,2,1,0:T(8,128)(2,1)} %bitcast.841, bf16[4,256,2048,1]{2,1,3,0:T(8,128)(2,1)} %bitcast.774), kind=kOutput, calls=%fused_computation.167 | convolution fusion | flops 6445596672 | bytes 13631488 | tf_op jit(solution)/shard_map/ztd,zste->sde/dot_general | solution.py:103
  551.1 6.2 collective-permute-done.21
  558.3 14.9 %all-gather.2 = f32[114688]{0:T(1024)S(1)} all-gather(f32[14336]{0:T(1024)S(1)} %pad_maximum_fusion.9), channel_id=4, replica_groups=mesh['z'=4,'core'=2,'head'=4] {'z','core'}, dimensions={0}, use_global_device_ids=true | all-gather | bytes 516096 | tf_op jit(solution)/shard_map/all_gather | solution.py:225
  578.5 73.6 %all-gather.3 = f32[32,1,4224]{2,1,0:T(1,128)S(1)} all-gather(f32[1,1,4224]{2,1,0:T(1,128)S(1)} %reshape.555), channel_id=2, replica_groups=mesh['z'=4,'core'=2,'head'=4] {'z','core','head'}, dimensions={0}, use_global_device_ids=true | all-gather | bytes 557568 | tf_op jit(solution)/shard_map/all_gather | solution.py:223
  658.7 11.5 %convert_add_fusion.2 = f32[1408,2048]{1,0:T(8,128)} fusion(bf16[1408,2048]{1,0:T(8,128)(2,1)} %collective-permute-done.32, bf16[1408,2048]{1,0:T(8,128)(2,1)} %convolution_convert_fusion), kind=kLoop, calls=%fused_computation.158 | loop fusion | flops 8650752 | bytes 23068672 | tf_op jit(solution)/shard_map/add | solution.py:218
  670.2 12.4 %convert_add_fusion.1 = f32[3,2048,512]{1,2,0:T(8,128)} fusion(bf16[3,2048,512]{1,2,0:T(8,128)(2,1)} %collective-permute-done.27, bf16[3,2048,512]{1,2,0:T(8,128)(2,1)} %fusion.99), kind=kLoop, calls=%fused_computation.157 | loop fusion | flops 9437184 | bytes 25165824 | tf_op jit(solution)/shard_map/add | solution.py:218
  682.7 12.6 %copy.282 = f32[3,2048,512]{2,1,0:T(8,128)} copy(f32[3,2048,512]{1,2,0:T(8,128)} %convert_add_fusion.1) | data formatting | bytes 25165824
  695.3 17.3 %convert_add_fusion = f32[2,2048,1408]{1,2,0:T(8,128)} fusion(bf16[2,2048,1408]{1,2,0:T(8,128)(2,1)} %collective-permute-done.31, bf16[2,2048,1408]{1,2,0:T(8,128)(2,1)} %convert_bitcast_fusion.1), kind=kLoop, calls=%fused_computation.155 | loop fusion | flops 17301504 | bytes 46137344 | tf_op jit(solution)/shard_map/add | solution.py:218
  712.6 23.5 %copy.283 = f32[2,2048,1408]{2,1,0:T(8,128)} copy(f32[2,2048,1408]{1,2,0:T(8,128)} %convert_add_fusion) | data formatting | bytes 46137344
  (814 shorter events, 352.9 us)
Async XLA Ops:
  7.2 142.0 %all-gather.9.cloned.1.call-start = ((), (), s32[]{:S(2)}) async-start(), calls=%async_computation | async-start | bytes 1310720 | tf_op jit(solution)/shard_map/all_gather | solution.py:147
  7.9 156.0 %all-gather.11.cloned.1.call-start = ((), (), s32[]{:S(2)}) async-start(), calls=%async_computation.1 | async-start | bytes 1310720 | tf_op jit(solution)/shard_map/all_gather | solution.py:148
  12.6 249.7 %all-gather.13.cloned.1.call-start = ((), (), s32[]{:S(2)}) async-start(), calls=%async_computation.3 | async-start | bytes 1310720 | tf_op jit(solution)/shard_map/all_gather | solution.py:168
  132.0 397.9 %all-gather.15.cloned.1.call-start = ((), (), s32[]{:S(2)}) async-start(), calls=%async_computation.4 | async-start | bytes 3932160 | tf_op jit(solution)/shard_map/all_gather | solution.py:210
  149.2 31.4 %collective-permute-start.13 = (bf16[256,2048]{1,0:T(8,128)(2,1)}, bf16[256,2048]{1,0:T(8,128)(2,1)}, u32[]{:S(2)}, u32[]{:S(2)}) collective-permute-start(bf16[256,2048]{1,0:T(8,128)(2,1)} %all-gather.9.cloned.1.call-done), channel_id=1, source_target_pairs={{0,2},{1,3},{2,0},{3,1},{4,6},{5,7},{6,4},{7,5},{8,10},{9,11},{10,... | collective-permute-start | bytes 3145736 | tf_op jit(solution)/shard_map/ppermute | solution.py:118
  150.3 26.3 %collective-permute-start.12 = (bf16[256,2048]{1,0:T(8,128)(2,1)}, bf16[256,2048]{1,0:T(8,128)(2,1)}, u32[]{:S(2)}, u32[]{:S(2)}) collective-permute-start(bf16[256,2048]{1,0:T(8,128)(2,1)} %all-gather.9.cloned.1.call-done), channel_id=1, source_target_pairs={{0,1},{1,0},{2,3},{3,2},{4,5},{5,4},{6,7},{7,6},{8,9},{9,8},{10,11... | collective-permute-start | bytes 3145736 | tf_op jit(solution)/shard_map/ppermute | solution.py:118
  156.9 42.7 %collective-permute-start.14 = (bf16[256,2048]{1,0:T(8,128)(2,1)}, bf16[256,2048]{1,0:T(8,128)(2,1)}, u32[]{:S(2)}, u32[]{:S(2)}) collective-permute-start(bf16[256,2048]{1,0:T(8,128)(2,1)} %all-gather.9.cloned.1.call-done), channel_id=1, source_target_pairs={{0,3},{1,2},{2,1},{3,0},{4,7},{5,6},{6,5},{7,4},{8,11},{9,10},{10,... | collective-permute-start | bytes 3145736 | tf_op jit(solution)/shard_map/ppermute | solution.py:118
  159.1 135.4 %collective-permute-start.9 = (bf16[64,2048]{1,0:T(8,128)(2,1)}, bf16[64,2048]{1,0:T(8,128)(2,1)}, u32[]{:S(2)}, u32[]{:S(2)}) collective-permute-start(bf16[64,2048]{1,0:T(8,128)(2,1)} %get-tuple-element.736), channel_id=1, source_target_pairs={{0,1},{1,0},{2,3},{3,2},{4,5},{5,4},{6,7},{7,6},{8,9},{9,8},{10,11... | collective-permute-start | bytes 786440 | tf_op jit(solution)/shard_map/ppermute | solution.py:118
  160.4 134.1 %collective-permute-start.11 = (bf16[64,2048]{1,0:T(8,128)(2,1)}, bf16[64,2048]{1,0:T(8,128)(2,1)}, u32[]{:S(2)}, u32[]{:S(2)}) collective-permute-start(bf16[64,2048]{1,0:T(8,128)(2,1)} %get-tuple-element.737), channel_id=1, source_target_pairs={{0,3},{1,2},{2,1},{3,0},{4,7},{5,6},{6,5},{7,4},{8,11},{9,10},{10,... | collective-permute-start | bytes 786440 | tf_op jit(solution)/shard_map/ppermute | solution.py:118
  176.6 56.5 %collective-permute-start.26 = (bf16[256,2048]{1,0:T(8,128)(2,1)}, bf16[256,2048]{1,0:T(8,128)(2,1)S(1)}, u32[]{:S(2)}, u32[]{:S(2)}) collective-permute-start(bf16[256,2048]{1,0:T(8,128)(2,1)} %all-gather.11.cloned.1.call-done), channel_id=1, source_target_pairs={{0,3},{1,2},{2,1},{3,0},{4,7},{5,6},{6,5},{7,4},{8,11},{9,10},{10,... | collective-permute-start | bytes 3145736 | tf_op jit(solution)/shard_map/ppermute | solution.py:118
  180.6 66.3 %collective-permute-start.25 = (bf16[256,2048]{1,0:T(8,128)(2,1)}, bf16[256,2048]{1,0:T(8,128)(2,1)S(1)}, u32[]{:S(2)}, u32[]{:S(2)}) collective-permute-start(bf16[256,2048]{1,0:T(8,128)(2,1)} %all-gather.11.cloned.1.call-done), channel_id=1, source_target_pairs={{0,2},{1,3},{2,0},{3,1},{4,6},{5,7},{6,4},{7,5},{8,10},{9,11},{10,... | collective-permute-start | bytes 3145736 | tf_op jit(solution)/shard_map/ppermute | solution.py:118
  199.6 55.6 %collective-permute-start.24 = (bf16[256,2048]{1,0:T(8,128)(2,1)S(1)}, bf16[256,2048]{1,0:T(8,128)(2,1)S(1)}, u32[]{:S(2)}, u32[]{:S(2)}) collective-permute-start(bf16[256,2048]{1,0:T(8,128)(2,1)S(1)} %copy-done.23), channel_id=1, source_target_pairs={{0,1},{1,0},{2,3},{3,2},{4,5},{5,4},{6,7},{7,6},{8,9},{9,8},{10,11... | collective-permute-start | bytes 3145736 | tf_op jit(solution)/shard_map/ppermute | solution.py:118
  233.2 27.2 %collective-permute-start.15 = (bf16[64,2048]{1,0:T(8,128)(2,1)S(1)}, bf16[64,2048]{1,0:T(8,128)(2,1)S(1)}, u32[]{:S(2)}, u32[]{:S(2)}) collective-permute-start(bf16[64,2048]{1,0:T(8,128)(2,1)S(1)} %get-tuple-element.733), channel_id=1, source_target_pairs={{0,1},{1,0},{2,3},{3,2},{4,5},{5,4},{6,7},{7,6},{8,9},{9,8},{10,11... | collective-permute-start | bytes 786440 | tf_op jit(solution)/shard_map/ppermute | solution.py:118
  255.2 35.7 %collective-permute-start.16 = (bf16[64,2048]{1,0:T(8,128)(2,1)}, bf16[64,2048]{1,0:T(8,128)(2,1)}, u32[]{:S(2)}, u32[]{:S(2)}) collective-permute-start(bf16[64,2048]{1,0:T(8,128)(2,1)} %get-tuple-element.735), channel_id=1, source_target_pairs={{0,2},{1,3},{2,0},{3,1},{4,6},{5,7},{6,4},{7,5},{8,10},{9,11},{10,... | collective-permute-start | bytes 786440 | tf_op jit(solution)/shard_map/ppermute | solution.py:118
  261.1 35.4 %collective-permute-start.10 = (bf16[64,2048]{1,0:T(8,128)(2,1)}, bf16[64,2048]{1,0:T(8,128)(2,1)}, u32[]{:S(2)}, u32[]{:S(2)}) collective-permute-start(bf16[64,2048]{1,0:T(8,128)(2,1)} %get-tuple-element.738), channel_id=1, source_target_pairs={{0,2},{1,3},{2,0},{3,1},{4,6},{5,7},{6,4},{7,5},{8,10},{9,11},{10,... | collective-permute-start | bytes 786440 | tf_op jit(solution)/shard_map/ppermute | solution.py:118
  264.1 199.4 %collective-permute-start.30 = (bf16[256,2048]{1,0:T(8,128)(2,1)}, bf16[256,2048]{1,0:T(8,128)(2,1)}, u32[]{:S(2)}, u32[]{:S(2)}) collective-permute-start(bf16[256,2048]{1,0:T(8,128)(2,1)} %all-gather.13.cloned.1.call-done), channel_id=1, source_target_pairs={{0,3},{1,2},{2,1},{3,0},{4,7},{5,6},{6,5},{7,4},{8,11},{9,10},{10,... | collective-permute-start | bytes 3145736 | tf_op jit(solution)/shard_map/ppermute | solution.py:118
  290.9 172.6 %collective-permute-start.29 = (bf16[256,2048]{1,0:T(8,128)(2,1)}, bf16[256,2048]{1,0:T(8,128)(2,1)}, u32[]{:S(2)}, u32[]{:S(2)}) collective-permute-start(bf16[256,2048]{1,0:T(8,128)(2,1)} %all-gather.13.cloned.1.call-done), channel_id=1, source_target_pairs={{0,2},{1,3},{2,0},{3,1},{4,6},{5,7},{6,4},{7,5},{8,10},{9,11},{10,... | collective-permute-start | bytes 3145736 | tf_op jit(solution)/shard_map/ppermute | solution.py:118
  301.0 25.8 %collective-permute-start.19 = (bf16[64,2048]{1,0:T(8,128)(2,1)S(1)}, bf16[64,2048]{1,0:T(8,128)(2,1)S(1)}, u32[]{:S(2)}, u32[]{:S(2)}) collective-permute-start(bf16[64,2048]{1,0:T(8,128)(2,1)S(1)} %get-tuple-element.695), channel_id=1, source_target_pairs={{0,2},{1,3},{2,0},{3,1},{4,6},{5,7},{6,4},{7,5},{8,10},{9,11},{10,... | collective-permute-start | bytes 786440 | tf_op jit(solution)/shard_map/ppermute | solution.py:118
  309.8 153.7 %collective-permute-start.28 = (bf16[256,2048]{1,0:T(8,128)(2,1)}, bf16[256,2048]{1,0:T(8,128)(2,1)}, u32[]{:S(2)}, u32[]{:S(2)}) collective-permute-start(bf16[256,2048]{1,0:T(8,128)(2,1)} %all-gather.13.cloned.1.call-done), channel_id=1, source_target_pairs={{0,1},{1,0},{2,3},{3,2},{4,5},{5,4},{6,7},{7,6},{8,9},{9,8},{10,11... | collective-permute-start | bytes 3145736 | tf_op jit(solution)/shard_map/ppermute | solution.py:118
  463.4 191.2 %all-reduce.40.cloned.1.call-start = ((), (), s32[]{:S(2)}) async-start(), calls=%async_computation.2 | async-start | bytes 4194304 | tf_op jit(solution)/shard_map/psum | solution.py:221
  516.6 178.6 %collective-permute-start.31 = (bf16[2,2048,1408]{1,2,0:T(8,128)(2,1)}, bf16[2,2048,1408]{1,2,0:T(8,128)(2,1)}, u32[]{:S(2)}, u32[]{:S(2)}) collective-permute-start(bf16[2,2048,1408]{1,2,0:T(8,128)(2,1)} %convert_bitcast_fusion.1), channel_id=1, source_target_pairs={{0,4},{4,0},{1,5},{5,1},{2,6},{6,2},{3,7},{7,3},{8,12},{12,8},{9,1... | collective-permute-start | bytes 34603016 | tf_op jit(solution)/shard_map/ppermute | solution.py:217
  529.4 129.3 %collective-permute-start.32 = (bf16[1408,2048]{1,0:T(8,128)(2,1)}, bf16[1408,2048]{1,0:T(8,128)(2,1)}, u32[]{:S(2)}, u32[]{:S(2)}) collective-permute-start(bf16[1408,2048]{1,0:T(8,128)(2,1)} %convolution_convert_fusion), channel_id=1, source_target_pairs={{0,4},{4,0},{1,5},{5,1},{2,6},{6,2},{3,7},{7,3},{8,12},{12,8},{9,1... | collective-permute-start | bytes 17301512 | tf_op jit(solution)/shard_map/ppermute | solution.py:217
  541.7 128.6 %collective-permute-start.27 = (bf16[3,2048,512]{1,2,0:T(8,128)(2,1)}, bf16[3,2048,512]{1,2,0:T(8,128)(2,1)}, u32[]{:S(2)}, u32[]{:S(2)}) collective-permute-start(bf16[3,2048,512]{1,2,0:T(8,128)(2,1)} %fusion.99), channel_id=1, source_target_pairs={{0,4},{4,0},{1,5},{5,1},{2,6},{6,2},{3,7},{7,3},{8,12},{12,8},{9,1... | collective-permute-start | bytes 18874376 | tf_op jit(solution)/shard_map/ppermute | solution.py:217
  550.1 28.0 %collective-permute-start.23 = (bf16[64,2048]{1,0:T(8,128)(2,1)}, bf16[64,2048]{1,0:T(8,128)(2,1)S(1)}, u32[]{:S(2)}, u32[]{:S(2)}) collective-permute-start(bf16[64,2048]{1,0:T(8,128)(2,1)} %get-tuple-element.731), channel_id=1, source_target_pairs={{0,3},{1,2},{2,1},{3,0},{4,7},{5,6},{6,5},{7,4},{8,11},{9,10},{10,... | collective-permute-start | bytes 786440 | tf_op jit(solution)/shard_map/ppermute | solution.py:118
  (135 other events, 1688.0 us)
Sparse Core Ops, SparseCore 0:
  9.6 30.8 all-gather.8
  42.0 27.2 all-gather.10
  132.2 28.3 all-gather.12
  463.5 64.0 all-gather.14
  578.2 66.6 all-reduce.39

commit v2 on v1

v2 whole, which is shorter than its diff:
```python
import functools
import jax
import jax.numpy as jnp
from jax import lax
from jax.experimental import pallas as pl
from jax.experimental.pallas import tpu as pltpu
from jax.sharding import Mesh, PartitionSpec as P

f32 = jnp.float32
bf16 = jnp.bfloat16

DIMS = {"nn": (((1,), (0,)), ((), ())), "nt": (((1,), (1,)), ((), ())), "tn": (((0,), (0,)), ((), ()))}


def mm(left, right, form="nn"):
    return lax.dot_general(left.astype(bf16), right.astype(bf16), DIMS[form], preferred_element_type=f32)


def halves(value):
    high = value.astype(bf16)
    return high, (value - high.astype(f32)).astype(bf16)


def mm3(left, right, form="nn"):
    lh, ll = halves(left)
    rh, rl = halves(right)
    return mm(lh, rh, form) + (mm(lh, rl, form) + mm(ll, rh, form))


def sigmoid(value):
    return 1.0 / (1.0 + jnp.exp(-value))


def block_masks(length, size):
    row = lax.broadcasted_iota(jnp.int32, (length, length), 0)
    col = lax.broadcasted_iota(jnp.int32, (length, length), 1)
    same = (row ^ col) < size
    return (same & (row > col)), (same & (row >= col))


def keep_rows(info_ref, length, size):
    row = lax.broadcasted_iota(jnp.int32, (length, 1), 0)
    keep = jnp.zeros((length, 1), f32)
    for b in range(length // size):
        keep = jnp.where((row >= b * size) & (row < (b + 1) * size), info_ref[1 + b].astype(f32), keep)
    within = row & (size - 1)
    return [None] + [jnp.where(within >= shift, 1.0, keep) for shift in range(1, 4)]


def taken(ref, lead, me, rows, shards, cols):
    parts = []
    for j in range(shards):
        at = pl.ds(pl.multiple_of((me ^ j) * rows, rows), rows)
        parts.append(ref[lead + (at, cols)] if lead is not None else ref[at, cols])
    return jnp.concatenate(parts, 0)


def put(ref, lead, me, rows, shards, cols, value):
    for j in range(shards):
        at = pl.ds(pl.multiple_of((me ^ j) * rows, rows), rows)
        ref[lead + (at, cols)] = value[j * rows:(j + 1) * rows].astype(ref.dtype)


def forward_kernel(rows, shards, blocks, info_ref, proj_ref, logit_ref, taps_ref, gain_ref,
                   mixed_ref, conv_ref, o_ref, fresh_ref, state_ref, inv_ref,
                   q_s, k_s, u_s, w_s):
    length = rows * shards
    size = length // blocks
    heads = logit_ref.shape[1]
    width = proj_ref.shape[2] // heads
    me = info_ref[0]
    masks = keep_rows(info_ref, length, size)
    strict, inclusive = block_masks(length, size)
    logit = taken(logit_ref, (), me, rows, shards, slice(None))
    beta_all = sigmoid(logit)
    for h in range(heads):
        cols = slice(h * width, (h + 1) * width)
        beta = beta_all[:, h:h + 1]
        acts = []
        for s in range(3):
            x = taken(proj_ref, (s,), me, rows, shards, cols)
            z = x * taps_ref[4 * s:4 * s + 1, cols]
            for j in range(1, 4):
                z = z + pltpu.roll(x, j, 0) * (taps_ref[4 * s + j:4 * s + j + 1, cols] * masks[j])
            conv_ref[s, :, cols] = z
            acts.append(z * sigmoid(z))
        q0, k0, v = acts
        q = q0 * (lax.rsqrt(jnp.sum(q0 * q0, axis=-1, keepdims=True) + 1e-06) * width ** -0.5)
        k = k0 * lax.rsqrt(jnp.sum(k0 * k0, axis=-1, keepdims=True) + 1e-06)
        q_s[:, cols] = q
        k_s[:, cols] = k
        power = jnp.where(strict, mm3(k * -beta, k, "nt"), 0.0)
        inverse = power
        step = 1
        while 2 * step < size:
            power = mm3(power, power)
            inverse = inverse + power + mm3(inverse, power)
            step *= 2
        inv_ref[h] = inverse
        bk, bv = beta * k, beta * v
        w_s[:, cols] = bk + mm(inverse, bk)
        u_s[:, cols] = bv + mm(inverse, bv)
    states = [jnp.zeros((width, width), f32)] * heads
    for b in range(blocks):
        at = slice(b * size, (b + 1) * size)
        keep = info_ref[1 + b].astype(f32)
        for h in range(heads):
            cols = slice(h * width, (h + 1) * width)
            state = states[h] * keep
            state_ref[h, b] = state
            fresh = u_s[at, cols] - mm(w_s[at, cols], state)
            fresh_ref[at, cols] = fresh
            states[h] = state + mm(k_s[at, cols], fresh, "tn")
            o_ref[at, cols] = mm(q_s[at, cols], state)
    for h in range(heads):
        cols = slice(h * width, (h + 1) * width)
        scores = jnp.where(inclusive, mm(q_s[:, cols], k_s[:, cols], "nt"), 0.0)
        o = o_ref[:, cols] + mm(scores, fresh_ref[:, cols])
        o_ref[:, cols] = o
        mixed = o * lax.rsqrt(jnp.mean(o * o, axis=-1, keepdims=True) + 1e-05) * gain_ref[0:1, :]
        put(mixed_ref, (), me, rows, shards, cols, mixed)


def backward_kernel(rows, shards, blocks, info_ref, grad_ref, proj_ref, logit_ref, taps_ref, gain_ref,
                    conv_ref, o_ref, fresh_ref, state_ref, inv_ref,
                    proj_grad_ref, logit_grad_ref, taps_grad_ref, gain_grad_ref,
                    q_s, k_s, w_s, do_s, df_s, dq_s, dk_s):
    length = rows * shards
    size = length // blocks
    heads = logit_ref.shape[1]
    width = proj_ref.shape[2] // heads
    me = info_ref[0]
    masks = keep_rows(info_ref, length, size)
    strict, inclusive = block_masks(length, size)
    logit = taken(logit_ref, (), me, rows, shards, slice(None))
    beta_all = sigmoid(logit)
    gain_total = jnp.zeros((1, width), f32)
    lane = lax.broadcasted_iota(jnp.int32, (length, logit_grad_ref.shape[1]), 1)
    logit_grad = jnp.zeros((length, logit_grad_ref.shape[1]), f32)
    for h in range(heads):
        cols = slice(h * width, (h + 1) * width)
        beta = beta_all[:, h:h + 1]
        zq, zk = conv_ref[0, :, cols], conv_ref[1, :, cols]
        q0, k0 = zq * sigmoid(zq), zk * sigmoid(zk)
        q = q0 * (lax.rsqrt(jnp.sum(q0 * q0, axis=-1, keepdims=True) + 1e-06) * width ** -0.5)
        k = k0 * lax.rsqrt(jnp.sum(k0 * k0, axis=-1, keepdims=True) + 1e-06)
        q_s[:, cols] = q
        k_s[:, cols] = k
        bk = beta * k
        w_s[:, cols] = bk + mm(inv_ref[h], bk)
        g = taken(grad_ref, (), me, rows, shards, cols)
        o = o_ref[:, cols]
        r = lax.rsqrt(jnp.mean(o * o, axis=-1, keepdims=True) + 1e-05)
        on = o * r
        gain_total = gain_total + jnp.sum(g * on, axis=0, keepdims=True)
        dn = g * gain_ref[0:1, :]
        do = r * (dn - on * jnp.mean(dn * on, axis=-1, keepdims=True))
        do_s[:, cols] = do
        scores = jnp.where(inclusive, mm(q, k, "nt"), 0.0)
        df_s[:, cols] = mm(scores, do, "tn")
        dscores = jnp.where(inclusive, mm(do, fresh_ref[:, cols], "nt"), 0.0)
        dq_s[:, cols] = mm(dscores, k)
        dk_s[:, cols] = mm(dscores, q, "tn")
    gain_grad_ref[...] = jnp.broadcast_to(gain_total, gain_grad_ref.shape)
    carried = [jnp.zeros((width, width), f32)] * heads
    for b in reversed(range(blocks)):
        at = slice(b * size, (b + 1) * size)
        keep = info_ref[1 + b].astype(f32)
        for h in range(heads):
            cols = slice(h * width, (h + 1) * width)
            after = carried[h]
            df = df_s[at, cols] + mm(k_s[at, cols], after)
            df_s[at, cols] = df
            do = do_s[at, cols]
            carried[h] = keep * (after + mm(q_s[at, cols], do, "tn") - mm(w_s[at, cols], df, "tn"))
            dq_s[at, cols] = dq_s[at, cols] + mm(do, state_ref[h, b], "nt")
            dk_s[at, cols] = dk_s[at, cols] + mm(fresh_ref[at, cols], after, "nt")
    for h in range(heads):
        cols = slice(h * width, (h + 1) * width)
        beta = beta_all[:, h:h + 1]
        k = k_s[:, cols]
        df = df_s[:, cols]
        dr = df + mm(inv_ref[h], df, "tn")
        bdr = beta * dr
        fresh = fresh_ref[:, cols]
        lower = jnp.where(strict, mm(dr, fresh, "nt"), 0.0)
        blower = beta * lower
        zv = conv_ref[2, :, cols]
        sv = sigmoid(zv)
        held, back = [], []
        for b in range(blocks):
            at = slice(b * size, (b + 1) * size)
            held.append(mm(k[at], state_ref[h, b]))
            back.append(mm(bdr[at], state_ref[h, b], "nt"))
        excess = zv * sv - jnp.concatenate(held, 0)
        gram = mm(k, k, "nt")
        dbeta = jnp.sum(dr * excess, axis=-1, keepdims=True) - jnp.sum(lower * gram, axis=-1, keepdims=True)
        logit_grad = jnp.where(lane == h, dbeta * beta * (1.0 - beta), logit_grad)
        dk = dk_s[:, cols] - jnp.concatenate(back, 0) - (mm(blower, k) + mm(blower, k, "tn"))
        dq = dq_s[:, cols]
        for s, dy in ((0, dq), (1, dk), (2, bdr)):
            z = conv_ref[s, :, cols]
            sz = sigmoid(z)
            if s < 2:
                y = z * sz
                r = lax.rsqrt(jnp.sum(y * y, axis=-1, keepdims=True) + 1e-06)
                yn = y * r
                if s == 0:
                    r = r * width ** -0.5
                dy = r * (dy - yn * jnp.sum(dy * yn, axis=-1, keepdims=True))
            dz = dy * sz * (1.0 + z * (1.0 - sz))
            x = taken(proj_ref, (s,), me, rows, shards, cols)
            dx = dz * taps_ref[4 * s:4 * s + 1, cols]
            taps_grad_ref[4 * s:4 * s + 1, cols] = jnp.sum(dz * x, axis=0, keepdims=True)
            for j in range(1, 4):
                moved = dz * masks[j]
                taps_grad_ref[4 * s + j:4 * s + j + 1, cols] = jnp.sum(moved * pltpu.roll(x, j, 0), axis=0, keepdims=True)
                dx = dx + pltpu.roll(moved, length - j, 0) * taps_ref[4 * s + j:4 * s + j + 1, cols]
            put(proj_grad_ref, (s,), me, rows, shards, cols, dx)
    put(logit_grad_ref, (), me, rows, shards, slice(None), logit_grad)


SMEM = pl.BlockSpec(memory_space=pltpu.SMEM)
VMEM = pl.BlockSpec(memory_space=pltpu.VMEM)


def mixer_forward(info, projected, logit, taps, gain, rows, shards, blocks):
    _, length, span = projected.shape
    heads = logit.shape[1]
    width = span // heads
    shape = jax.ShapeDtypeStruct
    return pl.pallas_call(
        functools.partial(forward_kernel, rows, shards, blocks),
        out_shape=(
            shape((length, span), bf16),
            shape((3, length, span), f32),
            shape((length, span), f32),
            shape((length, span), f32),
            shape((heads, blocks, width, width), f32),
            shape((heads, length, length), f32),
        ),
        in_specs=[SMEM] + [VMEM] * 4,
        out_specs=(VMEM,) * 6,
        scratch_shapes=[pltpu.VMEM((length, span), f32)] * 4,
        compiler_params=pltpu.CompilerParams(vmem_limit_bytes=48 * 1024 * 1024),
        cost_estimate=pl.CostEstimate(flops=10**10, bytes_accessed=10 * 2**20, transcendentals=10**6),
        name="mixer_forward",
    )(info, projected, logit, taps, gain)


def mixer_backward(info, grad, projected, logit, taps, gain, saved, rows, shards, blocks):
    _, length, span = projected.shape
    heads = logit.shape[1]
    width = span // heads
    shape = jax.ShapeDtypeStruct
    return pl.pallas_call(
        functools.partial(backward_kernel, rows, shards, blocks),
        out_shape=(
            shape((3, length, span), bf16),
            shape((length, 128), f32),
            shape((16, span), f32),
            shape((8, width), f32),
        ),
        in_specs=[SMEM] + [VMEM] * 10,
        out_specs=(VMEM,) * 4,
        scratch_shapes=[pltpu.VMEM((length, span), f32)] * 7,
        compiler_params=pltpu.CompilerParams(vmem_limit_bytes=48 * 1024 * 1024),
        cost_estimate=pl.CostEstimate(flops=2 * 10**10, bytes_accessed=14 * 2**20, transcendentals=10**6),
        name="mixer_backward",
    )(info, grad, projected, logit, taps, gain, *saved)


def norm_rows(values, gain):
    return values * lax.rsqrt(jnp.mean(values * values, axis=-1, keepdims=True) + 1e-06) * gain


def norm_back(grad, values, gain):
    scale = lax.rsqrt(jnp.mean(values * values, axis=-1, keepdims=True) + 1e-06)
    unit = values * scale
    inner = grad * gain
    back = scale * (inner - unit * jnp.mean(inner * unit, axis=-1, keepdims=True))
    return back, jnp.sum(grad * unit, axis=0)


def dot(equation, left, right):
    return jnp.einsum(equation, left, right, preferred_element_type=f32)


def after(value, *others):
    return lax.optimization_barrier((value, *others))[0]


def per_device(shards, hidden_in, norm1_gain, qkv_weight, beta_weight, conv_weight, out_gain,
               out_weight, norm2_gain, gate_up_weight, down_weight, block_segments, cotangent):
    segments = block_segments[0]
    blocks = segments.shape[0]
    rows, model = hidden_in.shape
    length = rows * shards
    me = lax.axis_index("head")
    mine_z = lax.axis_index("z")

    def exchange(parts):
        return [parts[0]] + [
            lax.ppermute(parts[k], "head", [(i, i ^ k) for i in range(shards)])
            for k in range(1, shards)
        ]

    def gather_rows(own):
        return exchange([own] * shards)

    def scatter_sum(product):
        pieces = exchange([product[k * rows:(k + 1) * rows] for k in range(shards)])
        total = pieces[0].astype(f32)
        for piece in pieces[1:]:
            total = total + piece.astype(f32)
        return total

    keep = jnp.concatenate([jnp.zeros((1,), bool), segments[1:] == segments[:-1]])
    info = jnp.concatenate([me[None], keep]).astype(jnp.int32)
    taps = conv_weight.astype(f32).reshape(-1, conv_weight.shape[2])
    taps = jnp.pad(taps, ((0, 16 - taps.shape[0]), (0, 0)))
    gain = out_gain[None]

    hidden_parts = gather_rows(hidden_in)
    normed_all = jnp.concatenate(
        [norm_rows(part.astype(f32), norm1_gain).astype(bf16) for part in hidden_parts]
    )
    rows_in = hidden_in.astype(f32)
    cot_all = jnp.concatenate(gather_rows(cotangent))
    cot_line = lax.all_gather(cotangent, "z", axis=0, tiled=True)
    hidden_line = lax.all_gather(hidden_in, "z", axis=0, tiled=True)
    line = cot_line.shape[0] // rows

    projected = dot("td,sde->ste", normed_all, qkv_weight)
    beta_logit = dot("td,dh->th", normed_all, beta_weight)
    mixer_low, *saved = mixer_forward(info, projected, beta_logit, taps, gain, rows, shards, blocks)
    attn_rows = scatter_sum(dot("tc,cd->td", mixer_low, out_weight).astype(bf16))
    middle = rows_in + attn_rows
    second_low = norm_rows(middle, norm2_gain).astype(bf16)
    second_all = jnp.concatenate(gather_rows(second_low))
    second_line = lax.all_gather(second_low, "z", axis=0, tiled=True)

    def feed_forward(second, cot):
        gate_up = dot("td,sdf->stf", second, gate_up_weight)
        sigmoid_gate = jax.nn.sigmoid(gate_up[0])
        silu_gate = gate_up[0] * sigmoid_gate
        hidden_low = (silu_gate * gate_up[1]).astype(bf16)
        hidden_grad = dot("td,fd->tf", cot, down_weight)
        gate_grad = hidden_grad * gate_up[1] * sigmoid_gate * (1.0 + gate_up[0] * (1.0 - sigmoid_gate))
        up_grad = hidden_grad * silu_gate
        return hidden_low, jnp.stack([gate_grad, up_grad]).astype(bf16)

    hidden_low, gate_up_low = feed_forward(second_all, cot_all)
    second_grad = scatter_sum(dot("stf,sdf->td", gate_up_low, gate_up_weight).astype(bf16))
    ffn_rows = scatter_sum(dot("tf,fd->td", hidden_low, down_weight).astype(bf16))
    block_out = (middle + ffn_rows).astype(bf16)
    middle_part, norm2_gain_grad = norm_back(second_grad, middle, norm2_gain)
    middle_grad = cotangent.astype(f32) + middle_part
    attn_grad_all = jnp.concatenate(gather_rows(middle_grad.astype(bf16)))
    mixer_in_grad = dot("td,cd->tc", attn_grad_all, out_weight)
    out_grad = dot("tc,td->cd", mixer_low, attn_grad_all).astype(bf16)
    mixer_in_grad = after(mixer_in_grad, out_grad)

    projected_low, beta_logit_grad, conv_grad, out_gain_grad = mixer_backward(
        info, mixer_in_grad, projected, beta_logit, taps, gain, saved, rows, shards, blocks
    )
    beta_low = beta_logit_grad[:, :beta_weight.shape[1]].astype(bf16)
    first_grad = scatter_sum(
        (dot("ste,sde->td", projected_low, qkv_weight) + dot("th,dh->td", beta_low, beta_weight)).astype(bf16)
    )
    rows_part, norm1_gain_grad = norm_back(first_grad, rows_in, norm1_gain)
    input_grad = middle_grad + rows_part
    projected_line = lax.all_gather(projected_low, "z", axis=0)
    beta_grad = dot("td,th->dh", normed_all, beta_low)

    cot_every = jnp.concatenate(gather_rows(cot_line))
    second_every = jnp.concatenate(gather_rows(second_line))
    hidden_every_low, gate_up_every = feed_forward(second_every, cot_every)

    def pair_sum(partial):
        other = lax.ppermute(partial, "core", [(0, 1), (1, 0)])
        return partial.astype(f32) + other.astype(f32)

    gate_up_grad = jnp.stack(
        [pair_sum(dot("td,tf->df", second_every, gate_up_every[s]).astype(bf16)) for s in range(2)]
    )
    down_grad = pair_sum(dot("tf,td->fd", hidden_every_low, cot_every).astype(bf16))
    hidden_every = jnp.stack(gather_rows(hidden_line)).reshape(shards, line, rows, model)
    normed_every = norm_rows(hidden_every.astype(f32), norm1_gain).astype(bf16)
    normed_every = normed_every.transpose(1, 0, 2, 3).reshape(line, length, model)
    qkv_grad = jnp.stack(
        [pair_sum(dot("ztd,zte->de", normed_every, projected_line[:, s]).astype(bf16)) for s in range(3)]
    )
    out_grad = lax.psum(out_grad, ("z", "core")).astype(f32)

    gains = jnp.concatenate([norm1_gain_grad, norm2_gain_grad, out_gain_grad[0]])
    small = jnp.concatenate([gains, beta_grad.T.reshape(-1), conv_grad[:12].reshape(-1)])
    small = small.reshape(-1, 128)

    def butterfly(value, axis, size):
        step = 1
        while step < size:
            value = value + lax.ppermute(value, axis, [(i, i ^ step) for i in range(size)])
            step *= 2
        return value

    small = butterfly(butterfly(small, "core", 2), "z", line).reshape(-1)
    gain_size = gains.size
    gains = butterfly(small[:gain_size].reshape(-1, 128), "head", shards).reshape(-1)
    beta_size = beta_grad.size
    beta_grad = small[gain_size:gain_size + beta_size].reshape(beta_grad.shape[::-1]).T
    conv_grad = small[gain_size + beta_size:].reshape(conv_weight.shape)
    return (
        block_out,
        input_grad,
        gains[:model],
        qkv_grad,
        beta_grad,
        conv_grad,
        gains[2 * model:],
        out_grad,
        gains[model:2 * model],
        gate_up_grad,
        down_grad,
    )


def solution(mesh):
    groups, shards = mesh.devices.shape
    split = Mesh(mesh.devices.reshape(groups // 2, 2, shards), ("z", "core", "head"))
    tokens = P(("z", "core", "head"), None)
    placed = (
        tokens,
        P(),
        P(None, None, "head"),
        P(None, "head"),
        P(None, None, "head"),
        P(),
        P("head", None),
        P(),
        P(None, None, "head"),
        P("head", None),
        P(("z", "core"), None),
        tokens,
    )
    return jax.shard_map(
        lambda *args: per_device(shards, *args),
        mesh=split,
        in_specs=placed,
        out_specs=(
            tokens,
            tokens,
            P(),
            P(None, None, "head"),
            P(None, "head"),
            P(None, None, "head"),
            P(),
            P("head", None),
            P(),
            P(None, None, "head"),
            P("head", None),
        ),
        check_vma=False,
    )
```

time: 751 us -> 497 us (0.66)
  matrix products: 254 us -> 115 us
  blocking collectives: 88.5 us -> 0 us
  local copies, waits for them, and re-layouts: 109 us -> 21.6 us
  waiting for transfers between devices: 146 us -> 195 us
  Pallas kernels: 0 us -> 24.1 us
  other arithmetic: 89.2 us -> 69.7 us
  starting transfers between devices: 37.7 us -> 46.6 us
    dot_general x276 -> x0, matrix products: 133 us -> none  [the longest x80 25 us: block_step(): jnp.einsum('hcd,hde->hce', inverse, power, precision=highest_precision)]
    all_gather x2 -> x0, blocking collectives: 88.5 us -> none  [the longest x1 73.6 us: per_device(): lax.all_gather(gains, ('z', 'core', 'head'), axis=0, tiled=True)]
    ppermute x0 -> x5, waiting for transfers between devices: none -> 56.2 us  [butterfly(): lax.ppermute(value, axis, [(i, i ^ step) for i in range(size)])]
    another operation x4 -> x7, other arithmetic: 0.09 us -> 42.8 us  [the longest x3 35.8 us: per_device(): jnp.stack([pair_sum(dot('td,tf->df', second_every, gate_up_every[s]).asty...]
    ppermute x30 -> x33, waiting for transfers between devices: 145 us -> 102 us  [exchange(): lax.ppermute(parts[k], 'head', [(i, i ^ k) for i in range(shards)])]
    psum x1, waiting for transfers between devices: 0.01 us -> 36 us  [per_device(): out_grad = lax.psum(out_grad, ('z', 'core')).astype(f32)]
    unnamed x243 -> x95, local copies, waits for them, and re-layouts: 50.2 us -> 16.1 us
    add x3 -> x1, other arithmetic: 41.3 us -> 9.8 us  [pair_sum(): return partial.astype(f32) + other.astype(f32)]
  transfers between devices with their start and end apart: 38 -> 49, of which waited for: 19 -> 23; matrix products, arithmetic and copies ran while one was open for 55% -> 39% of each run, Pallas kernels for 0% -> 5%
where the time goes in v2:
time: 497 us; the launch traced here: 488 us
  waiting for transfers between devices  195 us (39%)
  matrix products  115 us (23%)
  other arithmetic  69.7 us (14%)
  starting transfers between devices  46.6 us (9%)
  Pallas kernels  24.1 us (5%)
  local copies, waits for them, and re-layouts  21.6 us (4%)
  between operations  16.4 us (3%)
    dot_general x20, matrix products, dot(): return jnp.einsum(equation, left, right, preferred_element_type=f32)  115 us
    ppermute x33, waiting for transfers between devices, exchange(): lax.ppermute(parts[k], 'head', [(i, i ^ k) for i in range(shards)])  102 us
    ppermute x5, waiting for transfers between devices, butterfly(): lax.ppermute(value, axis, [(i, i ^ step) for i in range(size)])  56.2 us
    ppermute x33, starting transfers between devices, exchange(): lax.ppermute(parts[k], 'head', [(i, i ^ k) for i in range(shards)])  41.2 us
    psum x1, waiting for transfers between devices, per_device(): out_grad = lax.psum(out_grad, ('z', 'core')).astype(f32)  36 us
    another operation x3, other arithmetic, per_device(): jnp.stack([pair_sum(dot('td,tf->df', second_every, gate_up_every[s]).asty...  35.8 us
    unnamed x95, local copies, waits for them, and re-layouts  16.1 us
    pallas_call x1, Pallas kernels, mixer_forward(): pl.pallas_call(functools.partial(forward_kernel, rows, shards, blocks), o...  14.2 us
  transfers between devices with their start and end apart: 49, of which 23 were waited for; matrix products, arithmetic and copies ran while one was open for 39% of the time, Pallas kernels for 5%

profile of v2, /device:TPU:0, one launch (start us, length us, event | category | flops | bytes accessed | tf_op | source)
XLA Modules:
  0.0 487.6 jit_solution(14016951839189430079)
XLA Ops:
  30.1 14.2 %mixer_forward.1 = (bf16[256,512]{1,0:T(8,128)(2,1)S(1)}, f32[3,256,512]{2,1,0:T(8,128)S(1)}, f32[256,512]{1,0:T(8,128)S(1)}, f32[256,512]{1,0:T(8,128)S(1)}, f3...) custom-call(s32[5]{0:T(128)S(1)} %pad_add_fusion.info_ref, f32[3,256,512]{2,1,0:T(8,128)} %convolution_bitcast_fusion.4.proj_ref, ...), custom_call_target="tpu_custom_call" | custom-call | flops 10000000000 | bytes 10485760 | tf_op jit(solution)/shard_map/mixer_forward/pallas_call | solution.py:232
  52.6 5.7 %collective-permute-done.3 = bf16[64,2048]{1,0:T(8,128)(2,1)S(1)} collective-permute-done((bf16[64,2048]{1,0:T(8,128)(2,1)S(1)}, bf16[64,2048]{1,0:T(8,128)(2,1)S(1)}, u32[]{:S(2)}, u32[]{:S(2)}) %collective-permute-start.3) | collective-permute-done | bytes 262176 | tf_op jit(solution)/shard_map/ppermute | solution.py:304
  58.3 5.9 %collective-permute-done.4 = bf16[64,2048]{1,0:T(8,128)(2,1)S(1)} collective-permute-done((bf16[64,2048]{1,0:T(8,128)(2,1)S(1)}, bf16[64,2048]{1,0:T(8,128)(2,1)S(1)}, u32[]{:S(2)}, u32[]{:S(2)}) %collective-permute-start.4) | collective-permute-done | bytes 262176 | tf_op jit(solution)/shard_map/ppermute | solution.py:304
  81.6 6.5 %convolution_bitcast_fusion.1 = f32[2,256,1408]{2,1,0:T(8,128)S(1)} fusion(bf16[2,2048,1408]{2,1,0:T(8,128)(2,1)} %param.20, bf16[64,2048]{1,0:T(8,128)(2,1)} %collective-permute-done.8, bf16[64,2048]{1,0:T(8,128)(2,1)} %collective-permute-done.7, bf16[64,2048]{1,0:T(8,128)(2,1)} %collective-permute-done.6, bf16[64,2048]{1,0:T(8,128)(2,1)} %multiply_convert_fusion.10), kind=kOutput, calls=%fused_computation.29 | convolution fusion | flops 2956984320 | bytes 15466496 | tf_op jit(solution)/shard_map/td,sdf->stf/dot_general | solution.py:286
  92.8 5.1 %fusion.31 = (bf16[1,256,1408]{2,1,0:T(8,128)(2,1)S(1)}, bf16[1,256,1408]{2,1,0:T(8,128)(2,1)S(1)}) fusion(f32[2,256,1408]{2,1,0:T(8,128)S(1)} %convolution_bitcast_fusion.1, bf16[1408,2048]{1,0:T(8,128)(2,1)} %param.21, bf16[64,2048]{1,0:T(8,128)(2,1)S(1)} %collective-permute-done.14, bf16[64,2048]{1,0:T(8,128)(2,1)} %collective-permute-done.13, ...), kind=kOutput, calls=%fused_computation.79 | convolution fusion | flops 1485275136 | bytes 11141120 | tf_op jit(solution)/shard_map/td,fd->tf/dot_general | solution.py:286
  97.9 7.5 %fusion.5 = bf16[256,2048]{1,0:T(8,128)(2,1)S(1)} fusion(bf16[2,2048,1408]{2,1,0:T(8,128)(2,1)} %param.20, bf16[1,256,1408]{2,1,0:T(8,128)(2,1)S(1)} %get-tuple-element.42, bf16[1,256,1408]{2,1,0:T(8,128)(2,1)S(1)} %get-tuple-element.41), kind=kOutput, calls=%fused_computation.34 | convolution fusion | flops 2954035200 | bytes 14024704 | tf_op jit(solution)/shard_map/stf,sdf->td/dot_general | solution.py:286
  116.4 8.5 %collective-permute-done.16 = bf16[64,2048]{1,0:T(8,128)(2,1)S(1)} collective-permute-done((bf16[64,2048]{1,0:T(8,128)(2,1)S(1)}, bf16[64,2048]{1,0:T(8,128)(2,1)S(1)}, u32[]{:S(2)}, u32[]{:S(2)}) %collective-permute-start.16) | collective-permute-done | bytes 262176 | tf_op jit(solution)/shard_map/ppermute | solution.py:304
  149.3 9.9 %mixer_backward.1 = (bf16[3,256,512]{2,1,0:T(8,128)(2,1)}, f32[256,128]{1,0:T(8,128)S(1)}, f32[16,512]{1,0:T(8,128)S(1)}, f32[8,128]{1,0:T(8,128)S(1)}) custom-call(s32[5]{0:T(128)S(1)} %pad_add_fusion.info_ref, f32[256,512]{1,0:T(8,128)S(1)} %fusion.50.grad_ref, f32[3,256,512]{2,1,0:T(8,128)} %convolution_bitcast_fusion.4.proj_ref, ...), custom_call_target="tpu_custom_call" | custom-call | flops 20000000000 | bytes 14680064 | tf_op jit(solution)/shard_map/mixer_backward/pallas_call | solution.py:256
  181.2 6.2 %collective-permute-done.25 = f32[145,128]{1,0:T(8,128)S(1)} collective-permute-done((f32[145,128]{1,0:T(8,128)S(1)}, f32[145,128]{1,0:T(8,128)S(1)}, u32[]{:S(2)}, u32[]{:S(2)}) %collective-permute-start.25) | collective-permute-done | bytes 74272 | tf_op jit(solution)/shard_map/ppermute | solution.py:403
  190.7 7.3 %collective-permute-done.26 = f32[145,128]{1,0:T(8,128)S(1)} collective-permute-done((f32[145,128]{1,0:T(8,128)S(1)}, f32[145,128]{1,0:T(8,128)S(1)}, u32[]{:S(2)}, u32[]{:S(2)}) %collective-permute-start.26) | collective-permute-done | bytes 74272 | tf_op jit(solution)/shard_map/ppermute | solution.py:403
  207.8 41.5 %collective-permute-done.28 = f32[33,128]{1,0:T(8,128)S(1)} collective-permute-done((f32[33,128]{1,0:T(8,128)S(1)}, f32[33,128]{1,0:T(8,128)S(1)}, u32[]{:S(2)}, u32[]{:S(2)}) %collective-permute-start.28) | collective-permute-done | bytes 16928 | tf_op jit(solution)/shard_map/ppermute | solution.py:403
  252.8 36.0 %all-reduce.3.cloned.1.call-done = bf16[512,2048]{1,0:T(8,128)(2,1)} async-done(((bf16[512,2048]{1,0:T(8,128)(2,1)}), bf16[512,2048]{1,0:T(8,128)(2,1)}) %all-reduce.3.cloned.1.call-update) | async-done | bytes 2097168 | tf_op jit(solution)/shard_map/psum | solution.py:394
  300.8 12.2 %fusion.69 = f32[1024,1408]{1,0:T(8,128)} fusion(bf16[1024,2048]{1,0:T(8,128)(2,1)S(1)} %constant_dynamic-update-slice_fusion.5, bf16[1408,2048]{1,0:T(8,128)(2,1)} %param.21), kind=kOutput, calls=%fused_computation.157 | convolution fusion | flops 5905580032 | bytes 15728640 | tf_op jit(solution)/shard_map/td,fd->tf/dot_general | solution.py:286
  323.8 18.8 %collective-permute-done.35 = bf16[256,2048]{1,0:T(8,128)(2,1)S(1)} collective-permute-done((bf16[256,2048]{1,0:T(8,128)(2,1)S(1)}, bf16[256,2048]{1,0:T(8,128)(2,1)S(1)}, u32[]{:S(2)}, u32[]{:S(2)}) %collective-permute-start.35) | collective-permute-done | bytes 1048608 | tf_op jit(solution)/shard_map/ppermute | solution.py:304
  342.8 19.4 %collective-permute-done.37 = bf16[256,2048]{1,0:T(8,128)(2,1)S(1)} collective-permute-done((bf16[256,2048]{1,0:T(8,128)(2,1)S(1)}, bf16[256,2048]{1,0:T(8,128)(2,1)S(1)}, u32[]{:S(2)}, u32[]{:S(2)}) %collective-permute-start.37) | collective-permute-done | bytes 1048608 | tf_op jit(solution)/shard_map/ppermute | solution.py:304
  362.3 14.9 %convolution_bitcast_fusion = f32[2,1024,1408]{2,1,0:T(8,128)} fusion(bf16[2,2048,1408]{2,1,0:T(8,128)(2,1)S(1)} %bitcast.168, bf16[1024,2048]{1,0:T(8,128)(2,1)S(1)} %constant_dynamic-update-slice_fusion.1), kind=kOutput, calls=%fused_computation.13 | convolution fusion | flops 11811160064 | bytes 27262976 | tf_op jit(solution)/shard_map/td,sdf->stf/dot_general | solution.py:286
  377.2 15.3 %convolution_convert_fusion.2 = bf16[2048,1408]{1,0:T(8,128)(2,1)} fusion(bf16[1024,2048]{1,0:T(8,128)(2,1)S(1)} %constant_dynamic-update-slice_fusion.1, f32[1024,1408]{1,0:T(8,128)} %fusion.69, f32[2,1024,1408]{2,1,0:T(8,128)} %convolution_bitcast_fusion), kind=kOutput, calls=%fused_computation.12 | convolution fusion | flops 5922881536 | bytes 27262976 | tf_op jit(solution)/shard_map/td,tf->df/dot_general | solution.py:286
  392.5 11.9 %convolution_convert_fusion.1 = bf16[2048,1408]{1,0:T(8,128)(2,1)} fusion(bf16[1024,2048]{1,0:T(8,128)(2,1)S(1)} %constant_dynamic-update-slice_fusion.1, f32[1024,1408]{1,0:T(8,128)} %fusion.69, f32[2,1024,1408]{2,1,0:T(8,128)S(1)} %copy-done.38), kind=kOutput, calls=%fused_computation.11 | convolution fusion | flops 5917114368 | bytes 21495808 | tf_op jit(solution)/shard_map/td,tf->df/dot_general | solution.py:286
  415.6 11.3 %convolution_convert_fusion = bf16[1408,2048]{1,0:T(8,128)(2,1)S(1)} fusion(bf16[1024,2048]{1,0:T(8,128)(2,1)S(1)} %copy-done.31, f32[2,1024,1408]{2,1,0:T(8,128)} %convolution_bitcast_fusion), kind=kOutput, calls=%fused_computation.10 | convolution fusion | flops 5917114368 | bytes 21495808 | tf_op jit(solution)/shard_map/tf,td->fd/dot_general | solution.py:286
  429.3 5.2 %pad_maximum_fusion.1 = f32[3,2048,512]{2,1,0:T(8,128)} fusion(f32[1,2048,512]{2,1,0:T(8,128)S(1)} %add_bitcast_fusion.2, f32[1,2048,512]{2,1,0:T(8,128)S(1)} %add_bitcast_fusion.3, f32[1,2048,512]{2,1,0:T(8,128)S(1)} %add_bitcast_fusion.4), kind=kLoop, calls=%fused_computation.1 | loop fusion | flops 6291456 | bytes 25165824 | tf_op jit(solution)/shard_map/stack | solution.py:391
  434.4 9.7 %add_bitcast_fusion.1 = f32[1,2048,1408]{2,1,0:T(8,128)} fusion(bf16[2048,1408]{1,0:T(8,128)(2,1)} %collective-permute-done.41, bf16[2048,1408]{1,0:T(8,128)(2,1)} %convolution_convert_fusion.2), kind=kLoop, calls=%fused_computation.4 | loop fusion | flops 8650752 | bytes 23068672 | tf_op jit(solution)/shard_map/stack | solution.py:384
  444.1 9.9 %add_bitcast_fusion = f32[1,2048,1408]{2,1,0:T(8,128)} fusion(bf16[2048,1408]{1,0:T(8,128)(2,1)} %collective-permute-done.42, bf16[2048,1408]{1,0:T(8,128)(2,1)} %convolution_convert_fusion.1), kind=kLoop, calls=%fused_computation.3 | loop fusion | flops 8650752 | bytes 23068672 | tf_op jit(solution)/shard_map/stack | solution.py:384
  454.0 16.2 %pad_maximum_fusion = f32[2,2048,1408]{2,1,0:T(8,128)} fusion(f32[1,2048,1408]{2,1,0:T(8,128)} %add_bitcast_fusion, f32[1,2048,1408]{2,1,0:T(8,128)} %add_bitcast_fusion.1), kind=kLoop, calls=%fused_computation | loop fusion | flops 5767168 | bytes 46137344 | tf_op jit(solution)/shard_map/stack | solution.py:384
  470.2 9.8 %convert_add_fusion = f32[1408,2048]{1,0:T(8,128)} fusion(bf16[1408,2048]{1,0:T(8,128)(2,1)} %collective-permute-done.43, bf16[1408,2048]{1,0:T(8,128)(2,1)S(1)} %convolution_convert_fusion), kind=kLoop, calls=%fused_computation.2 | loop fusion | flops 8650752 | bytes 23068672 | tf_op jit(solution)/shard_map/add | solution.py:382
  (252 shorter events, 162.4 us)
Async XLA Ops:
  8.0 180.3 %all-gather.10.cloned.1.call-start = ((), (), s32[]{:S(2)}) async-start(), calls=%async_computation.3 | async-start | bytes 1310720 | tf_op jit(solution)/shard_map/all_gather | solution.py:330
  12.7 189.7 %all-gather.6.cloned.1.call-start = ((), (), s32[]{:S(2)}) async-start(), calls=%async_computation | async-start | bytes 1310720 | tf_op jit(solution)/shard_map/all_gather | solution.py:331
  69.6 23.1 %collective-permute-start.12 = (bf16[64,2048]{1,0:T(8,128)(2,1)S(1)}, bf16[64,2048]{1,0:T(8,128)(2,1)}, u32[]{:S(2)}, u32[]{:S(2)}) collective-permute-start(bf16[64,2048]{1,0:T(8,128)(2,1)S(1)} %copy-done.17), channel_id=1, source_target_pairs={{0,1},{1,0},{2,3},{3,2},{4,5},{5,4},{6,7},{7,6},{8,9},{9,8},{10,11... | collective-permute-start | bytes 786440 | tf_op jit(solution)/shard_map/ppermute | solution.py:304
  70.0 22.7 %collective-permute-start.13 = (bf16[64,2048]{1,0:T(8,128)(2,1)S(1)}, bf16[64,2048]{1,0:T(8,128)(2,1)}, u32[]{:S(2)}, u32[]{:S(2)}) collective-permute-start(bf16[64,2048]{1,0:T(8,128)(2,1)S(1)} %copy-done.17), channel_id=1, source_target_pairs={{0,2},{1,3},{2,0},{3,1},{4,6},{5,7},{6,4},{7,5},{8,10},{9,11},{10,... | collective-permute-start | bytes 786440 | tf_op jit(solution)/shard_map/ppermute | solution.py:304
  71.7 178.6 %all-gather.8.cloned.1.call-start = ((), (), s32[]{:S(2)}) async-start(), calls=%async_computation.2 | async-start | bytes 1310720 | tf_op jit(solution)/shard_map/all_gather | solution.py:341
  75.7 17.1 %collective-permute-start.14 = (bf16[64,2048]{1,0:T(8,128)(2,1)S(1)}, bf16[64,2048]{1,0:T(8,128)(2,1)S(1)}, u32[]{:S(2)}, u32[]{:S(2)}) collective-permute-start(bf16[64,2048]{1,0:T(8,128)(2,1)S(1)} %copy-done.17), channel_id=1, source_target_pairs={{0,3},{1,2},{2,1},{3,0},{4,7},{5,6},{6,5},{7,4},{8,11},{9,10},{10,... | collective-permute-start | bytes 786440 | tf_op jit(solution)/shard_map/ppermute | solution.py:304
  107.2 17.7 %collective-permute-start.16 = (bf16[64,2048]{1,0:T(8,128)(2,1)S(1)}, bf16[64,2048]{1,0:T(8,128)(2,1)S(1)}, u32[]{:S(2)}, u32[]{:S(2)}) collective-permute-start(bf16[64,2048]{1,0:T(8,128)(2,1)S(1)} %get-tuple-element.48), channel_id=1, source_target_pairs={{0,2},{1,3},{2,0},{3,1},{4,6},{5,7},{6,4},{7,5},{8,10},{9,11},{10,... | collective-permute-start | bytes 786440 | tf_op jit(solution)/shard_map/ppermute | solution.py:304
  107.6 17.3 %collective-permute-start.17 = (bf16[64,2048]{1,0:T(8,128)(2,1)S(1)}, bf16[64,2048]{1,0:T(8,128)(2,1)S(1)}, u32[]{:S(2)}, u32[]{:S(2)}) collective-permute-start(bf16[64,2048]{1,0:T(8,128)(2,1)S(1)} %get-tuple-element.47), channel_id=1, source_target_pairs={{0,3},{1,2},{2,1},{3,0},{4,7},{5,6},{6,5},{7,4},{8,11},{9,10},{10,... | collective-permute-start | bytes 786440 | tf_op jit(solution)/shard_map/ppermute | solution.py:304
  109.1 18.6 %collective-permute-start.10 = (bf16[64,2048]{1,0:T(8,128)(2,1)S(1)}, bf16[64,2048]{1,0:T(8,128)(2,1)S(1)}, u32[]{:S(2)}, u32[]{:S(2)}) collective-permute-start(bf16[64,2048]{1,0:T(8,128)(2,1)S(1)} %get-tuple-element.51), channel_id=1, source_target_pairs={{0,2},{1,3},{2,0},{3,1},{4,6},{5,7},{6,4},{7,5},{8,10},{9,11},{10,... | collective-permute-start | bytes 786440 | tf_op jit(solution)/shard_map/ppermute | solution.py:304
  132.5 156.3 %all-reduce.3.cloned.1.call-start = ((), (), s32[]{:S(2)}) async-start(), calls=%async_computation.1 | async-start | bytes 4194304 | tf_op jit(solution)/shard_map/psum | solution.py:394
  169.3 235.6 %all-gather.12.cloned.1.call-start = ((), (), s32[]{:S(2)}) async-start(), calls=%async_computation.4 | async-start | bytes 3932160 | tf_op jit(solution)/shard_map/all_gather | solution.py:373
  199.0 94.1 %collective-permute-start.38 = (bf16[256,2048]{1,0:T(8,128)(2,1)}, bf16[256,2048]{1,0:T(8,128)(2,1)}, u32[]{:S(2)}, u32[]{:S(2)}) collective-permute-start(bf16[256,2048]{1,0:T(8,128)(2,1)} %all-gather.10.cloned.1.call-done), channel_id=1, source_target_pairs={{0,1},{1,0},{2,3},{3,2},{4,5},{5,4},{6,7},{7,6},{8,9},{9,8},{10,11... | collective-permute-start | bytes 3145736 | tf_op jit(solution)/shard_map/ppermute | solution.py:304
  200.1 96.7 %collective-permute-start.39 = (bf16[256,2048]{1,0:T(8,128)(2,1)}, bf16[256,2048]{1,0:T(8,128)(2,1)}, u32[]{:S(2)}, u32[]{:S(2)}) collective-permute-start(bf16[256,2048]{1,0:T(8,128)(2,1)} %all-gather.10.cloned.1.call-done), channel_id=1, source_target_pairs={{0,2},{1,3},{2,0},{3,1},{4,6},{5,7},{6,4},{7,5},{8,10},{9,11},{10,... | collective-permute-start | bytes 3145736 | tf_op jit(solution)/shard_map/ppermute | solution.py:304
  200.8 98.0 %collective-permute-start.40 = (bf16[256,2048]{1,0:T(8,128)(2,1)}, bf16[256,2048]{1,0:T(8,128)(2,1)}, u32[]{:S(2)}, u32[]{:S(2)}) collective-permute-start(bf16[256,2048]{1,0:T(8,128)(2,1)} %all-gather.10.cloned.1.call-done), channel_id=1, source_target_pairs={{0,3},{1,2},{2,1},{3,0},{4,7},{5,6},{6,5},{7,4},{8,11},{9,10},{10,... | collective-permute-start | bytes 3145736 | tf_op jit(solution)/shard_map/ppermute | solution.py:304
  202.4 110.6 %collective-permute-start.29 = (bf16[256,2048]{1,0:T(8,128)(2,1)}, bf16[256,2048]{1,0:T(8,128)(2,1)S(1)}, u32[]{:S(2)}, u32[]{:S(2)}) collective-permute-start(bf16[256,2048]{1,0:T(8,128)(2,1)} %all-gather.6.cloned.1.call-done), channel_id=1, source_target_pairs={{0,1},{1,0},{2,3},{3,2},{4,5},{5,4},{6,7},{7,6},{8,9},{9,8},{10,11... | collective-permute-start | bytes 3145736 | tf_op jit(solution)/shard_map/ppermute | solution.py:304
  203.6 45.6 %collective-permute-start.28 = (f32[33,128]{1,0:T(8,128)S(1)}, f32[33,128]{1,0:T(8,128)S(1)}, u32[]{:S(2)}, u32[]{:S(2)}) collective-permute-start(f32[33,128]{1,0:T(8,128)S(1)} %slice_add_fusion), channel_id=1, source_target_pairs={{0,2},{1,3},{2,0},{3,1},{4,6},{5,7},{6,4},{7,5},{8,10},{9,11},{10,... | collective-permute-start | bytes 50696 | tf_op jit(solution)/shard_map/ppermute | solution.py:403
  249.2 66.2 %collective-permute-start.30 = (bf16[256,2048]{1,0:T(8,128)(2,1)}, bf16[256,2048]{1,0:T(8,128)(2,1)S(1)}, u32[]{:S(2)}, u32[]{:S(2)}) collective-permute-start(bf16[256,2048]{1,0:T(8,128)(2,1)} %all-gather.6.cloned.1.call-done), channel_id=1, source_target_pairs={{0,2},{1,3},{2,0},{3,1},{4,6},{5,7},{6,4},{7,5},{8,10},{9,11},{10,... | collective-permute-start | bytes 3145736 | tf_op jit(solution)/shard_map/ppermute | solution.py:304
  293.1 27.0 %collective-permute-start.31 = (bf16[256,2048]{1,0:T(8,128)(2,1)S(1)}, bf16[256,2048]{1,0:T(8,128)(2,1)S(1)}, u32[]{:S(2)}, u32[]{:S(2)}) collective-permute-start(bf16[256,2048]{1,0:T(8,128)(2,1)S(1)} %copy-done.15), channel_id=1, source_target_pairs={{0,3},{1,2},{2,1},{3,0},{4,7},{5,6},{6,5},{7,4},{8,11},{9,10},{10,... | collective-permute-start | bytes 3145736 | tf_op jit(solution)/shard_map/ppermute | solution.py:304
  296.8 45.8 %collective-permute-start.35 = (bf16[256,2048]{1,0:T(8,128)(2,1)S(1)}, bf16[256,2048]{1,0:T(8,128)(2,1)S(1)}, u32[]{:S(2)}, u32[]{:S(2)}) collective-permute-start(bf16[256,2048]{1,0:T(8,128)(2,1)S(1)} %copy-done.18), channel_id=1, source_target_pairs={{0,1},{1,0},{2,3},{3,2},{4,5},{5,4},{6,7},{7,6},{8,9},{9,8},{10,11... | collective-permute-start | bytes 3145736 | tf_op jit(solution)/shard_map/ppermute | solution.py:304
  298.9 43.8 %collective-permute-start.36 = (bf16[256,2048]{1,0:T(8,128)(2,1)S(1)}, bf16[256,2048]{1,0:T(8,128)(2,1)S(1)}, u32[]{:S(2)}, u32[]{:S(2)}) collective-permute-start(bf16[256,2048]{1,0:T(8,128)(2,1)S(1)} %copy-done.18), channel_id=1, source_target_pairs={{0,2},{1,3},{2,0},{3,1},{4,6},{5,7},{6,4},{7,5},{8,10},{9,11},{10,... | collective-permute-start | bytes 3145736 | tf_op jit(solution)/shard_map/ppermute | solution.py:304
  313.1 49.1 %collective-permute-start.37 = (bf16[256,2048]{1,0:T(8,128)(2,1)S(1)}, bf16[256,2048]{1,0:T(8,128)(2,1)S(1)}, u32[]{:S(2)}, u32[]{:S(2)}) collective-permute-start(bf16[256,2048]{1,0:T(8,128)(2,1)S(1)} %copy-done.18), channel_id=1, source_target_pairs={{0,3},{1,2},{2,1},{3,0},{4,7},{5,6},{6,5},{7,4},{8,11},{9,10},{10,... | collective-permute-start | bytes 3145736 | tf_op jit(solution)/shard_map/ppermute | solution.py:304
  392.5 42.0 %collective-permute-start.41 = (bf16[2048,1408]{1,0:T(8,128)(2,1)}, bf16[2048,1408]{1,0:T(8,128)(2,1)}, u32[]{:S(2)}, u32[]{:S(2)}) collective-permute-start(bf16[2048,1408]{1,0:T(8,128)(2,1)} %convolution_convert_fusion.2), channel_id=1, source_target_pairs={{0,4},{4,0},{1,5},{5,1},{2,6},{6,2},{3,7},{7,3},{8,12},{12,8},{9,1... | collective-permute-start | bytes 17301512 | tf_op jit(solution)/shard_map/ppermute | solution.py:381
  404.4 39.7 %collective-permute-start.42 = (bf16[2048,1408]{1,0:T(8,128)(2,1)}, bf16[2048,1408]{1,0:T(8,128)(2,1)}, u32[]{:S(2)}, u32[]{:S(2)}) collective-permute-start(bf16[2048,1408]{1,0:T(8,128)(2,1)} %convolution_convert_fusion.1), channel_id=1, source_target_pairs={{0,4},{4,0},{1,5},{5,1},{2,6},{6,2},{3,7},{7,3},{8,12},{12,8},{9,1... | collective-permute-start | bytes 17301512 | tf_op jit(solution)/shard_map/ppermute | solution.py:381
  426.8 43.4 %collective-permute-start.43 = (bf16[1408,2048]{1,0:T(8,128)(2,1)S(1)}, bf16[1408,2048]{1,0:T(8,128)(2,1)}, u32[]{:S(2)}, u32[]{:S(2)}) collective-permute-start(bf16[1408,2048]{1,0:T(8,128)(2,1)S(1)} %convolution_convert_fusion), channel_id=1, source_target_pairs={{0,4},{4,0},{1,5},{5,1},{2,6},{6,2},{3,7},{7,3},{8,12},{12,8},{9,1... | collective-permute-start | bytes 17301512 | tf_op jit(solution)/shard_map/ppermute | solution.py:381
  (67 other events, 890.7 us)
Sparse Core Ops, SparseCore 0:
  12.8 29.6 all-gather.9
  71.9 28.3 all-gather.5
  132.6 28.6 all-gather.7
  181.3 72.0 all-gather.11
Sparse Core Ops, SparseCore 1:
  169.4 119.4 all-reduce.2

commit v3 on v2

--- a/solution.py
+++ b/solution.py
@@ -270,6 +270,213 @@
     )(info, grad, projected, logit, taps, gain, *saved)
 
 
+def rows_kernel(second_ref, cot_ref, gate_up_ref, down_ref, out_ref, gate_s, up_s, grad_s):
+    step = pl.program_id(0)
+    second = second_ref[...]
+    cot = cot_ref[...]
+    cot = cot.reshape(-1, cot.shape[-1])
+    gate = jnp.dot(second, gate_up_ref[0], preferred_element_type=f32)
+    up = jnp.dot(second, gate_up_ref[1], preferred_element_type=f32)
+    grad = lax.dot_general(cot, down_ref[...], DIMS["nt"], preferred_element_type=f32)
+
+    @pl.when(step == 0)
+    def _():
+        gate_s[...] = gate
+        up_s[...] = up
+        grad_s[...] = grad
+
+    @pl.when(step > 0)
+    def _():
+        gate_s[...] += gate
+        up_s[...] += up
+        grad_s[...] += grad
+
+    @pl.when(step == pl.num_programs(0) - 1)
+    def _():
+        chunk = 32
+
+        def body(r, carry):
+            at = pl.ds(pl.multiple_of(r * chunk, chunk), chunk)
+            gate, up, grad = gate_s[at], up_s[at], grad_s[at]
+            sg = sigmoid(gate)
+            silu = gate * sg
+            out_ref[0, at] = (grad * up * sg * (1.0 + gate * (1.0 - sg))).astype(bf16)
+            out_ref[1, at] = (grad * silu).astype(bf16)
+            out_ref[2, at] = (silu * up).astype(bf16)
+            return carry
+
+        lax.fori_loop(0, gate_s.shape[0] // chunk, body, 0)
+
+
+def feed_forward_rows(second, cot, part, gate_up_weight, down_weight, tile=512):
+    length, model = second.shape
+    line, _, rows, _ = cot.shape
+    hidden = down_weight.shape[0]
+    return pl.pallas_call(
+        rows_kernel,
+        grid=(model // tile,),
+        in_specs=[
+            pl.BlockSpec((length, tile), lambda i: (0, i)),
+            pl.BlockSpec((line, None, rows, tile), lambda i: (0, part, 0, i)),
+            pl.BlockSpec((2, tile, hidden), lambda i: (0, i, 0)),
+            pl.BlockSpec((hidden, tile), lambda i: (0, i)),
+        ],
+        out_specs=pl.BlockSpec((3, length, hidden), lambda i: (0, 0, 0), pipeline_mode=pl.Buffered(1)),
+        out_shape=jax.ShapeDtypeStruct((3, length, hidden), bf16),
+        scratch_shapes=[pltpu.VMEM((length, hidden), f32)] * 3,
+        compiler_params=pltpu.CompilerParams(vmem_limit_bytes=56 * 1024 * 1024),
+        cost_estimate=pl.CostEstimate(
+            flops=6 * length * model * hidden, bytes_accessed=6 * model * hidden, transcendentals=length * hidden),
+        name="feed_forward_rows",
+    )(second, cot, gate_up_weight, down_weight)
+
+
+def swap(value):
+    return lax.ppermute(value, "core", [(0, 1), (1, 0)])
+
+
+def planes_kernel(pieces, core_ref, *refs):
+    out_ref, sent_ref = refs[2 * pieces:]
+    lefts = [refs[p][...].T for p in range(pieces)]
+    for s in range(out_ref.shape[0]):
+        total = None
+        for p in range(pieces):
+            term = jnp.dot(lefts[p], refs[pieces + p][s], preferred_element_type=f32)
+            total = term if total is None else total + term
+        low = total.astype(bf16)
+        sent_ref[s] = low
+        out_ref[s] = low.astype(f32)
+
+
+def planes_fill(core_ref, whole_ref, part_ref, out_ref):
+    out_ref[...] = part_ref[...].astype(f32)
+
+
+def planes_grad(core, lefts, rights, planes, tile=256):
+    pieces = len(lefts)
+    height = lefts[0].shape[1]
+    _, depth, span = rights[0].shape
+    steps = height // 2 // tile
+    whole = jax.ShapeDtypeStruct((planes, height, span), f32)
+    params = pltpu.CompilerParams(vmem_limit_bytes=48 * 1024 * 1024)
+    own, sent = pl.pallas_call(
+        functools.partial(planes_kernel, pieces),
+        grid_spec=pltpu.PrefetchScalarGridSpec(
+            num_scalar_prefetch=1,
+            grid=(steps,),
+            in_specs=[pl.BlockSpec((depth, tile), lambda i, c: (0, c[0] * steps + i))] * pieces
+            + [pl.BlockSpec((planes, depth, span), lambda i, c: (0, 0, 0), pipeline_mode=pl.Buffered(1))] * pieces,
+            out_specs=(
+                pl.BlockSpec((planes, tile, span), lambda i, c: (0, c[0] * steps + i, 0)),
+                pl.BlockSpec((planes, tile, span), lambda i, c: (0, i, 0)),
+            ),
+        ),
+        out_shape=(whole, jax.ShapeDtypeStruct((planes, height // 2, span), bf16)),
+        compiler_params=params,
+        cost_estimate=pl.CostEstimate(
+            flops=pieces * depth * planes * height * span // 4,
+            bytes_accessed=planes * height * span, transcendentals=0),
+        name="planes_grad",
+    )(core, *lefts, *rights)
+
+    def finish(part):
+        return pl.pallas_call(
+            planes_fill,
+            grid_spec=pltpu.PrefetchScalarGridSpec(
+                num_scalar_prefetch=1,
+                grid=(planes, steps),
+                in_specs=[
+                    pl.BlockSpec(memory_space=pl.ANY),
+                    pl.BlockSpec((1, tile, span), lambda s, i, c: (s, i, 0)),
+                ],
+                out_specs=pl.BlockSpec((1, tile, span), lambda s, i, c: (s, (1 - c[0]) * steps + i, 0)),
+            ),
+            out_shape=whole,
+            input_output_aliases={1: 0},
+            compiler_params=params,
+            cost_estimate=pl.CostEstimate(
+                flops=planes * height * span // 2, bytes_accessed=3 * planes * height * span, transcendentals=0),
+            name="planes_fill",
+        )(core, own, part)
+
+    return sent, finish
+
+
+def turned_kernel(pieces, core_ref, *refs):
+    out_ref, sent_ref = refs[2 * pieces:2 * pieces + 2]
+    turned = refs[2 * pieces + 2:]
+
+    @pl.when(pl.program_id(0) == 0)
+    def _():
+        for p in range(pieces):
+            turned[p][...] = refs[p][...].T
+
+    total = None
+    for p in range(pieces):
+        right = refs[pieces + p][...]
+        right = right.reshape(-1, right.shape[-1])
+        term = jnp.dot(turned[p][...], right, preferred_element_type=f32)
+        total = term if total is None else total + term
+    low = total.astype(bf16)
+    sent_ref[...] = low
+    out_ref[...] = low.astype(f32)
+
+
+def turned_grad(core, lefts, rights, tile=256):
+    pieces = len(lefts)
+    _, depth, height = lefts[0].shape
+    line, parts, rows, span = rights[0].shape
+
+    def right_spec(h):
+        return pl.BlockSpec((line, None, rows, tile), lambda i, c: (0, h, 0, c[0] * steps + i))
+
+    steps = span // 2 // tile
+    whole = jax.ShapeDtypeStruct((height, span), f32)
+    params = pltpu.CompilerParams(vmem_limit_bytes=48 * 1024 * 1024)
+    own, sent = pl.pallas_call(
+        functools.partial(turned_kernel, pieces),
+        grid_spec=pltpu.PrefetchScalarGridSpec(
+            num_scalar_prefetch=1,
+            grid=(steps,),
+            in_specs=[pl.BlockSpec((None, depth, height), lambda i, c: (2, 0, 0), pipeline_mode=pl.Buffered(1))] * pieces
+            + [right_spec(p % parts) for p in range(pieces)],
+            out_specs=(
+                pl.BlockSpec((height, tile), lambda i, c: (0, c[0] * steps + i)),
+                pl.BlockSpec((height, tile), lambda i, c: (0, i)),
+            ),
+            scratch_shapes=[pltpu.VMEM((height, depth), bf16)] * pieces,
+        ),
+        out_shape=(whole, jax.ShapeDtypeStruct((height, span // 2), bf16)),
+        compiler_params=params,
+        cost_estimate=pl.CostEstimate(
+            flops=pieces * depth * height * span // 4,
+            bytes_accessed=height * span, transcendentals=0),
+        name="turned_grad",
+    )(core, *lefts, *[right for right in rights for _ in range(parts)])
+
+    def finish(part):
+        return pl.pallas_call(
+            planes_fill,
+            grid_spec=pltpu.PrefetchScalarGridSpec(
+                num_scalar_prefetch=1,
+                grid=(steps,),
+                in_specs=[
+                    pl.BlockSpec(memory_space=pl.ANY),
+                    pl.BlockSpec((height, tile), lambda i, c: (0, i)),
+                ],
+                out_specs=pl.BlockSpec((height, tile), lambda i, c: (0, (1 - c[0]) * steps + i)),
+            ),
+            out_shape=whole,
+            input_output_aliases={1: 0},
+            compiler_params=params,
+            cost_estimate=pl.CostEstimate(
+                flops=height * span // 2, bytes_accessed=3 * height * span, transcendentals=0),
+            name="turned_fill",
+        )(core, own, part)
+
+    return sent, finish
+
+
 def norm_rows(values, gain):
     return values * lax.rsqrt(jnp.mean(values * values, axis=-1, keepdims=True) + 1e-06) * gain
 
@@ -299,11 +506,24 @@
     me = lax.axis_index("head")
     mine_z = lax.axis_index("z")
 
+    half = shards // 2
+
     def exchange(parts):
         return [parts[0]] + [
             lax.ppermute(parts[k], "head", [(i, i ^ k) for i in range(shards)])
             for k in range(1, shards)
         ]
+
+    def move(value, k):
+        return lax.ppermute(value, "head", [(i, i ^ k) for i in range(shards)])
+
+    def relay(pieces):
+        far = []
+        for k in range(half + 1, shards):
+            via = k ^ half
+            cut = pieces[0].shape[0] // 2
+            far.append(jnp.concatenate([move(pieces[half][:cut], via), move(pieces[via][cut:], half)]))
+        return far
 
     def gather_rows(own):
         return exchange([own] * shards)
@@ -321,24 +541,28 @@
     taps = jnp.pad(taps, ((0, 16 - taps.shape[0]), (0, 0)))
     gain = out_gain[None]
 
+    core = lax.axis_index("core")
     hidden_parts = gather_rows(hidden_in)
     normed_all = jnp.concatenate(
         [norm_rows(part.astype(f32), norm1_gain).astype(bf16) for part in hidden_parts]
     )
     rows_in = hidden_in.astype(f32)
-    cot_all = jnp.concatenate(gather_rows(cotangent))
-    cot_line = lax.all_gather(cotangent, "z", axis=0, tiled=True)
-    hidden_line = lax.all_gather(hidden_in, "z", axis=0, tiled=True)
-    line = cot_line.shape[0] // rows
-
+    hidden_line = lax.all_gather(hidden_in, "z", axis=0)
+    line = hidden_line.shape[0]
     projected = dot("td,sde->ste", normed_all, qkv_weight)
+    cot_all = jnp.concatenate([after(part, projected) for part in gather_rows(cotangent)])
+    cot_line = lax.all_gather(cot_all, "z", axis=0)
     beta_logit = dot("td,dh->th", normed_all, beta_weight)
-    mixer_low, *saved = mixer_forward(info, projected, beta_logit, taps, gain, rows, shards, blocks)
-    attn_rows = scatter_sum(dot("tc,cd->td", mixer_low, out_weight).astype(bf16))
+    mixer_low, *saved = mixer_forward(
+        info, after(projected, cot_all), beta_logit, taps, gain, rows, shards, blocks
+    )
+    attn_rows = scatter_sum(after(dot("tc,cd->td", mixer_low, out_weight).astype(bf16), hidden_line))
     middle = rows_in + attn_rows
     second_low = norm_rows(middle, norm2_gain).astype(bf16)
     second_all = jnp.concatenate(gather_rows(second_low))
-    second_line = lax.all_gather(second_low, "z", axis=0, tiled=True)
+    second_line = lax.all_gather(after(second_low, cot_line), "z", axis=0)
+    hidden_ready = after(hidden_line, second_all)
+    hidden_near = [move(hidden_ready, k) for k in range(1, half + 1)]
 
     def feed_forward(second, cot):
         gate_up = dot("td,sdf->stf", second, gate_up_weight)
@@ -351,62 +575,99 @@
         return hidden_low, jnp.stack([gate_grad, up_grad]).astype(bf16)
 
     hidden_low, gate_up_low = feed_forward(second_all, cot_all)
-    second_grad = scatter_sum(dot("stf,sdf->td", gate_up_low, gate_up_weight).astype(bf16))
-    ffn_rows = scatter_sum(dot("tf,fd->td", hidden_low, down_weight).astype(bf16))
-    block_out = (middle + ffn_rows).astype(bf16)
-    middle_part, norm2_gain_grad = norm_back(second_grad, middle, norm2_gain)
+    second_grad = scatter_sum(after(dot("stf,sdf->td", gate_up_low, gate_up_weight).astype(bf16), *hidden_near))
+    ffn_product = dot("tf,fd->td", hidden_low, down_weight).astype(bf16)
+    middle_part, norm2_gain_grad = norm_back(after(second_grad, cot_line, ffn_product), middle, norm2_gain)
     middle_grad = cotangent.astype(f32) + middle_part
     attn_grad_all = jnp.concatenate(gather_rows(middle_grad.astype(bf16)))
     mixer_in_grad = dot("td,cd->tc", attn_grad_all, out_weight)
-    out_grad = dot("tc,td->cd", mixer_low, attn_grad_all).astype(bf16)
-    mixer_in_grad = after(mixer_in_grad, out_grad)
 
     projected_low, beta_logit_grad, conv_grad, out_gain_grad = mixer_backward(
         info, mixer_in_grad, projected, beta_logit, taps, gain, saved, rows, shards, blocks
     )
+    projected_line = lax.all_gather(projected_low, "z", axis=1, tiled=True)
+    second_ready = after(second_line, projected_low)
+    second_parts = [second_ready] + [move(second_ready, k) for k in range(1, half + 1)]
     beta_low = beta_logit_grad[:, :beta_weight.shape[1]].astype(bf16)
-    first_grad = scatter_sum(
-        (dot("ste,sde->td", projected_low, qkv_weight) + dot("th,dh->td", beta_low, beta_weight)).astype(bf16)
-    )
+    first_product = dot("ste,sde->td", projected_low, qkv_weight) + dot("th,dh->td", beta_low, beta_weight)
+    beta_grad = dot("td,th->dh", normed_all, beta_low)
+
+    both = jnp.stack([first_product.astype(bf16), ffn_product]).reshape(2, shards, rows, model)
+
+    out_partial = dot("tc,td->cd", mixer_low, attn_grad_all).astype(bf16)
+    span = out_partial.shape[0] // 2
+    out_half = lax.dynamic_slice_in_dim(out_partial, core * span, span).astype(f32)
+    out_half = out_half + swap(lax.dynamic_slice_in_dim(out_partial, (1 - core) * span, span)).astype(f32)
+    out_half = out_half.astype(bf16)
+
+    cot_other = swap(cot_line)
+    cot_line = cot_line.reshape(line, 2, half * rows, model)
+    second_lines, line_rows, others = [], [], []
+    second_parts = second_parts + relay(second_parts)
+    hidden_near = [after(piece, second_parts[half]) for piece in hidden_near]
+    hidden_far = relay([hidden_line, *hidden_near])
+    for h in range(2):
+        pieces = second_parts[h * half:(h + 1) * half]
+        if h == 1:
+            pieces = [after(piece, line_rows[0], out_half) for piece in pieces]
+        piece = jnp.stack(pieces, 1).reshape(line * half * rows, model)
+        if h == 0:
+            piece = after(piece, both, cot_other, second_parts[half])
+        else:
+            piece = after(piece, *hidden_far, *others)
+        second_lines.append(piece)
+        others.append(swap(piece))
+        line_rows.append(feed_forward_rows(piece, cot_line, h, gate_up_weight, down_weight))
+    out_every = lax.all_gather(after(out_half, line_rows[0]), "z", axis=0)
+    hidden_every = jnp.stack([hidden_line, *hidden_near, *hidden_far])
+    row_others = [swap(part) for part in line_rows]
+    down_part, down_finish = turned_grad(
+        core[None], [after(line_rows[0], row_others[0], projected_line, *others), line_rows[1], *row_others],
+        [cot_line, cot_other.reshape(cot_line.shape)],
+    )
+    normed_every = norm_rows(hidden_every.astype(f32), norm1_gain).astype(bf16)
+    normed_every = normed_every.transpose(1, 0, 2, 3).reshape(line * length, model)
+
+    both_parts = after(both, line_rows[1])
+    first_grad, ffn_rows = sum(
+        piece.astype(f32) for piece in exchange([both_parts[:, k] for k in range(shards)])
+    )
+    first_grad = after(first_grad, down_part)
+    block_out = (middle + ffn_rows).astype(bf16)
     rows_part, norm1_gain_grad = norm_back(first_grad, rows_in, norm1_gain)
     input_grad = middle_grad + rows_part
-    projected_line = lax.all_gather(projected_low, "z", axis=0)
-    beta_grad = dot("td,th->dh", normed_all, beta_low)
-
-    cot_every = jnp.concatenate(gather_rows(cot_line))
-    second_every = jnp.concatenate(gather_rows(second_line))
-    hidden_every_low, gate_up_every = feed_forward(second_every, cot_every)
-
-    def pair_sum(partial):
-        other = lax.ppermute(partial, "core", [(0, 1), (1, 0)])
-        return partial.astype(f32) + other.astype(f32)
-
-    gate_up_grad = jnp.stack(
-        [pair_sum(dot("td,tf->df", second_every, gate_up_every[s]).astype(bf16)) for s in range(2)]
-    )
-    down_grad = pair_sum(dot("tf,td->fd", hidden_every_low, cot_every).astype(bf16))
-    hidden_every = jnp.stack(gather_rows(hidden_line)).reshape(shards, line, rows, model)
-    normed_every = norm_rows(hidden_every.astype(f32), norm1_gain).astype(bf16)
-    normed_every = normed_every.transpose(1, 0, 2, 3).reshape(line, length, model)
-    qkv_grad = jnp.stack(
-        [pair_sum(dot("ztd,zte->de", normed_every, projected_line[:, s]).astype(bf16)) for s in range(3)]
-    )
-    out_grad = lax.psum(out_grad, ("z", "core")).astype(f32)
-
     gains = jnp.concatenate([norm1_gain_grad, norm2_gain_grad, out_gain_grad[0]])
-    small = jnp.concatenate([gains, beta_grad.T.reshape(-1), conv_grad[:12].reshape(-1)])
-    small = small.reshape(-1, 128)
-
-    def butterfly(value, axis, size):
-        step = 1
-        while step < size:
-            value = value + lax.ppermute(value, axis, [(i, i ^ step) for i in range(size)])
-            step *= 2
-        return value
-
-    small = butterfly(butterfly(small, "core", 2), "z", line).reshape(-1)
+    small = jnp.concatenate([gains, beta_grad.T.reshape(-1), conv_grad[:12].reshape(-1)]).reshape(-1, 128)
+
+    def total(value, axis, size):
+        values = [value] + [
+            lax.ppermute(value, axis, [(i, i ^ k) for i in range(size)]) for k in range(1, size)
+        ]
+        while len(values) > 1:
+            values = [left + right for left, right in zip(values[::2], values[1::2])]
+        return values[0]
+
+    gate_up_part, gate_up_finish = planes_grad(
+        core[None], [after(second_lines[0], normed_every, down_part), second_lines[1], *others],
+        [*line_rows, *row_others], 2,
+    )
+    small = total(small, "core", 2)
+    qkv_part, qkv_finish = planes_grad(
+        core[None], [after(normed_every, small, gate_up_part), swap(normed_every)],
+        [projected_line, swap(projected_line)], 3,
+    )
+    down_grad = down_finish(after(swap(down_part), qkv_part, out_every))
+    small = total(small, "z", line)
+    small = small.reshape(-1)
     gain_size = gains.size
-    gains = butterfly(small[:gain_size].reshape(-1, 128), "head", shards).reshape(-1)
+    gains = total(small[:gain_size].reshape(-1, 128), "head", shards).reshape(-1)
+    out_rows = jnp.sum(out_every.astype(f32), axis=0).astype(bf16)
+    out_other = swap(out_rows)
+    out_grad = jnp.where(
+        core == 0, jnp.concatenate([out_rows, out_other]), jnp.concatenate([out_other, out_rows])
+    ).astype(f32)
+    gate_up_grad = gate_up_finish(after(swap(gate_up_part), down_grad, small))
+    qkv_grad = qkv_finish(after(swap(qkv_part), gate_up_grad))
     beta_size = beta_grad.size
     beta_grad = small[gain_size:gain_size + beta_size].reshape(beta_grad.shape[::-1]).T
     conv_grad = small[gain_size + beta_size:].reshape(conv_weight.shape)

time: 497 us -> 413 us (0.83); the launches traced: 488 us -> 409 us
  Pallas kernels: 24.1 us -> 129 us
  waiting for transfers between devices: 195 us -> 98.8 us
  matrix products: 115 us -> 47.2 us
  other arithmetic: 69.7 us -> 43.2 us
  local copies, waits for them, and re-layouts: 21.6 us -> 27.5 us
    pallas_call x0 -> x8, Pallas kernels: none -> 105 us  [the longest x2 40 us: feed_forward_rows(): pl.pallas_call(rows_kernel, grid=(model // tile,), in_specs=[pl.BlockSpec...]
    dot_general x20 -> x12, matrix products: 115 us -> 47.2 us  [dot(): return jnp.einsum(equation, left, right, preferred_element_type=f32)]
    ppermute x33 -> x21, waiting for transfers between devices: 102 us -> 44.2 us  [exchange(): lax.ppermute(parts[k], 'head', [(i, i ^ k) for i in range(shards)])]
    another operation x7 -> x3, other arithmetic: 42.8 us -> 3.25 us  [the longest x2 1.69 us: per_device(): piece = jnp.stack(pieces, 1).reshape(line * half * rows, model)]
    psum x1 -> x0, waiting for transfers between devices: 36 us -> none  [per_device(): out_grad = lax.psum(out_grad, ('z', 'core')).astype(f32)]
    ppermute x11 -> x27, starting transfers between devices: 4.55 us -> 19.3 us  [the longest x8 9.63 us: move(): return lax.ppermute(value, 'head', [(i, i ^ k) for i in range(shards)])]
    ppermute x33 -> x21, starting transfers between devices: 41.2 us -> 28.1 us  [exchange(): lax.ppermute(parts[k], 'head', [(i, i ^ k) for i in range(shards)])]
    ppermute x11 -> x27, waiting for transfers between devices: 56.3 us -> 49.7 us  [the longest x8 28.2 us: move(): return lax.ppermute(value, 'head', [(i, i ^ k) for i in range(shards)])]
  transfers between devices with their start and end apart: 49 -> 53, of which waited for: 23 -> 21; matrix products, arithmetic and copies ran while one was open for 39% -> 26% of each run, Pallas kernels for 5% -> 30%
where the time goes in v3:
time: 413 us; the launch traced here: 409 us
  Pallas kernels  129 us (31%)
  waiting for transfers between devices  98.8 us (24%)
  starting transfers between devices  48 us (12%)
  matrix products  47.2 us (11%)
  other arithmetic  43.2 us (10%)
  local copies, waits for them, and re-layouts  27.5 us (7%)
  between operations  14.8 us (4%)
    dot_general x12, matrix products, dot(): return jnp.einsum(equation, left, right, preferred_element_type=f32)  47.2 us
    ppermute x21, waiting for transfers between devices, exchange(): lax.ppermute(parts[k], 'head', [(i, i ^ k) for i in range(shards)])  44.2 us
    pallas_call x2, Pallas kernels, feed_forward_rows(): pl.pallas_call(rows_kernel, grid=(model // tile,), in_specs=[pl.BlockSpec...  40 us
    pallas_call x2, Pallas kernels, planes_grad(): pl.pallas_call(functools.partial(planes_kernel, pieces), grid_spec=pltpu....  33.5 us
    ppermute x8, waiting for transfers between devices, move(): return lax.ppermute(value, 'head', [(i, i ^ k) for i in range(shards)])  28.2 us
    ppermute x21, starting transfers between devices, exchange(): lax.ppermute(parts[k], 'head', [(i, i ^ k) for i in range(shards)])  28.1 us
    ppermute x7, waiting for transfers between devices, total(): lax.ppermute(value, axis, [(i, i ^ k) for i in range(size)])  19.3 us
    pallas_call x3, Pallas kernels, finish(): pl.pallas_call(planes_fill, grid_spec=pltpu.PrefetchScalarGridSpec(num_sc...  18.4 us
  transfers between devices with their start and end apart: 53, of which 21 were waited for; matrix products, arithmetic and copies ran while one was open for 26% of the time, Pallas kernels for 30%

profile of v3, /device:TPU:0, one launch (start us, length us, event | category | flops | bytes accessed | tf_op | source)
XLA Modules:
  0.0 408.9 jit_solution(11958324179591110847)
XLA Ops:
  26.9 6.1 %convolution_bitcast_fusion.3.proj_ref = f32[3,256,512]{2,1,0:T(8,128)} fusion(bf16[3,2048,512]{2,1,0:T(8,128)(2,1)} %param.14, bf16[64,2048]{1,0:T(8,128)(2,1)S(1)} %get-tuple-element.119, bf16[64,2048]{1,0:T(8,128)(2,1)S(1)} %get-tuple-element.118, bf16[64,2048]{1,0:T(8,128)(2,1)S(1)} %get-tuple-element.117, bf16[64,2048]{1,0:T(8,128)(2,1)S(1)} %get-tuple-element.116), kind=kOutput, calls=%fused_computation.21 | convolution fusion | flops 1614807040 | bytes 8912896 | tf_op jit(solution)/shard_map/td,sde->ste/dot_general | solution.py:493
  41.8 14.2 %mixer_forward.1 = (bf16[256,512]{1,0:T(8,128)(2,1)S(1)}, f32[3,256,512]{2,1,0:T(8,128)S(1)}, f32[256,512]{1,0:T(8,128)S(1)}, f32[256,512]{1,0:T(8,128)S(1)}, f3...) custom-call(s32[5]{0:T(128)S(1)} %pad_add_fusion.info_ref, f32[3,256,512]{2,1,0:T(8,128)} %convolution_bitcast_fusion.3.proj_ref, ...), custom_call_target="tpu_custom_call" | custom-call | flops 10000000000 | bytes 10485760 | tf_op jit(solution)/shard_map/mixer_forward/pallas_call | solution.py:232
  66.4 6.6 %collective-permute-done.8 = bf16[64,2048]{1,0:T(8,128)(2,1)S(1)} collective-permute-done((bf16[64,2048]{1,0:T(8,128)(2,1)S(1)}, bf16[64,2048]{1,0:T(8,128)(2,1)S(1)}, u32[]{:S(2)}, u32[]{:S(2)}) %collective-permute-start.8) | collective-permute-done | bytes 262176 | tf_op jit(solution)/shard_map/ppermute | solution.py:513
  90.7 4.8 %collective-permute-done.10 = bf16[64,2048]{1,0:T(8,128)(2,1)S(1)} collective-permute-done((bf16[64,2048]{1,0:T(8,128)(2,1)}, bf16[64,2048]{1,0:T(8,128)(2,1)S(1)}, u32[]{:S(2)}, u32[]{:S(2)}) %collective-permute-start.10) | collective-permute-done | bytes 262176 | tf_op jit(solution)/shard_map/ppermute | solution.py:513
  95.6 6.8 %convolution_bitcast_fusion = f32[2,256,1408]{2,1,0:T(8,128)S(1)} fusion(bf16[2,2048,1408]{2,1,0:T(8,128)(2,1)} %gate_up_ref.3, bf16[64,2048]{1,0:T(8,128)(2,1)S(1)} %collective-permute-done.11, bf16[64,2048]{1,0:T(8,128)(2,1)S(1)} %collective-permute-done.10, bf16[64,2048]{1,0:T(8,128)(2,1)S(1)} %collective-permute-done.9, ...), kind=kOutput, calls=%fused_computation.6 | convolution fusion | flops 2956984320 | bytes 15466496 | tf_op jit(solution)/shard_map/td,sdf->stf/dot_general | solution.py:493
  102.4 6.3 %fusion.19 = (bf16[1,256,1408]{2,1,0:T(8,128)(2,1)S(1)}, bf16[1,256,1408]{2,1,0:T(8,128)(2,1)S(1)}) fusion(f32[2,256,1408]{2,1,0:T(8,128)S(1)} %convolution_bitcast_fusion, bf16[256,2048]{1,0:T(8,128)(2,1)} %constant_dynamic-update-slice_fusion, bf16[1408,2048]{1,0:T(8,128)(2,1)} %down_ref.3), kind=kOutput, calls=%fused_computation.50 | convolution fusion | flops 1481080832 | bytes 11141120 | tf_op jit(solution)/shard_map/td,fd->tf/dot_general | solution.py:493
  108.7 7.6 %fusion.3 = bf16[256,2048]{1,0:T(8,128)(2,1)S(1)} fusion(bf16[2,2048,1408]{2,1,0:T(8,128)(2,1)} %gate_up_ref.3, bf16[1,256,1408]{2,1,0:T(8,128)(2,1)S(1)} %get-tuple-element.102, bf16[1,256,1408]{2,1,0:T(8,128)(2,1)S(1)} %get-tuple-element.101), kind=kOutput, calls=%fused_computation.11 | convolution fusion | flops 2954035200 | bytes 14024704 | tf_op jit(solution)/shard_map/stf,sdf->td/dot_general | solution.py:493
  121.6 4.8 %convolution_convert_fusion.2 = bf16[256,2048]{1,0:T(8,128)(2,1)} fusion(bf16[1408,2048]{1,0:T(8,128)(2,1)S(1)} %bitcast.161, f32[2,256,1408]{2,1,0:T(8,128)} %copy-done.50), kind=kOutput, calls=%fused_computation.14 | convolution fusion | flops 1479081984 | bytes 9699328 | tf_op jit(solution)/shard_map/tf,fd->td/dot_general | solution.py:493
  141.3 6.7 %collective-permute-done.19 = bf16[64,2048]{1,0:T(8,128)(2,1)} collective-permute-done((bf16[64,2048]{1,0:T(8,128)(2,1)}, bf16[64,2048]{1,0:T(8,128)(2,1)}, u32[]{:S(2)}, u32[]{:S(2)}) %collective-permute-start.19) | collective-permute-done | bytes 262176 | tf_op jit(solution)/shard_map/ppermute | solution.py:513
  157.9 10.0 %mixer_backward.1 = (bf16[3,256,512]{2,1,0:T(8,128)(2,1)}, f32[256,128]{1,0:T(8,128)S(1)}, f32[16,512]{1,0:T(8,128)S(1)}, f32[8,128]{1,0:T(8,128)S(1)}) custom-call(s32[5]{0:T(128)S(1)} %pad_add_fusion.info_ref, f32[256,512]{1,0:T(8,128)S(1)} %fusion.38.grad_ref, f32[3,256,512]{2,1,0:T(8,128)} %convolution_bitcast_fusion.3.proj_ref, ...), custom_call_target="tpu_custom_call" | custom-call | flops 20000000000 | bytes 14680064 | tf_op jit(solution)/shard_map/mixer_backward/pallas_call | solution.py:256
  172.5 6.2 %convolution_bitcast_fusion.1 = f32[256,2048]{1,0:T(8,128)} fusion(bf16[3,256,512]{2,1,0:T(8,128)(2,1)} %get-tuple-element.68, bf16[3,2048,512]{2,1,0:T(8,128)(2,1)} %param.14), kind=kOutput, calls=%fused_computation.8 | convolution fusion | flops 1610612736 | bytes 9175040 | tf_op jit(solution)/shard_map/ste,sde->td/dot_general | solution.py:493
  182.5 11.8 %collective-permute-done.21 = bf16[4,64,2048]{2,1,0:T(8,128)(2,1)S(1)} collective-permute-done((bf16[4,64,2048]{2,1,0:T(8,128)(2,1)}, bf16[4,64,2048]{2,1,0:T(8,128)(2,1)S(1)}, u32[]{:S(2)}, u32[]{:S(2)}) %collective-permute-start.21) | collective-permute-done | bytes 1048608 | tf_op jit(solution)/shard_map/ppermute | solution.py:518
  205.7 14.8 %collective-permute-done.26 = bf16[2,64,2048]{2,1,0:T(8,128)(2,1)} collective-permute-done((bf16[2,64,2048]{2,1,0:T(8,128)(2,1)}, bf16[2,64,2048]{2,1,0:T(8,128)(2,1)}, u32[]{:S(2)}, u32[]{:S(2)}) %collective-permute-start.26) | collective-permute-done | bytes 524320 | tf_op jit(solution)/shard_map/ppermute | solution.py:518
  224.4 20.0 %feed_forward_rows.2.refs_0_.refs_4_ = bf16[3,512,1408]{2,1,0:T(8,128)(2,1)} custom-call(bf16[512,2048]{1,0:T(8,128)(2,1)} %bitcast.125, bf16[4,2,128,2048]{3,2,1,0:T(8,128)(2,1)} %bitcast.134, bf16[2,2048,1408]{2,1,0:T(8,128)(2,1)} %gate_up_ref.3, bf16[1408,2048]{1,0:T(8,128)(2,1)} %down_ref.3), custom_call_target="tpu_custom_call" | custom-call | flops 8858370048 | bytes 17301504 | tf_op jit(solution)/shard_map/feed_forward_rows/pallas_call | solution.py:315
  245.9 19.9 %feed_forward_rows.3.refs_1_.refs_5_ = bf16[3,512,1408]{2,1,0:T(8,128)(2,1)} custom-call(bf16[512,2048]{1,0:T(8,128)(2,1)} %bitcast.127, bf16[4,2,128,2048]{3,2,1,0:T(8,128)(2,1)} %bitcast.135, bf16[2,2048,1408]{2,1,0:T(8,128)(2,1)} %gate_up_ref.3, bf16[1408,2048]{1,0:T(8,128)(2,1)} %down_ref.3), custom_call_target="tpu_custom_call" | custom-call | flops 8858370048 | bytes 17301504 | tf_op jit(solution)/shard_map/feed_forward_rows/pallas_call | solution.py:315
  280.2 13.2 %turned_grad.1 = (f32[1408,2048]{1,0:T(8,128)}, bf16[1408,1024]{1,0:T(8,128)(2,1)}) custom-call(s32[1]{0:T(128)} %bitcast.32.core_ref, bf16[3,512,1408]{2,1,0:T(8,128)(2,1)} %feed_forward_rows.2.refs_0_.refs_4_, bf16[3,512,1408]{2,1,0:T(8,128)(2,1)} %feed_forward_rows.3.refs_1_.refs_5_, bf16[3,512,1408]{2,1,0:T(8,128)(2,1)} %collective-permute-done.32.refs_2_.refs_6_, ...), custom_call_target="tpu_custom_call" | custom-call | flops 1476395008 | bytes 2883584 | tf_op jit(solution)/shard_map/turned_grad/pallas_call | solution.py:436
  293.4 21.2 %planes_grad.2 = (f32[2,2048,1408]{2,1,0:T(8,128)}, bf16[2,1024,1408]{2,1,0:T(8,128)(2,1)}) custom-call(s32[1]{0:T(128)} %bitcast.32.core_ref, bf16[512,2048]{1,0:T(8,128)(2,1)S(1)} %bitcast.126, bf16[512,2048]{1,0:T(8,128)(2,1)S(1)} %bitcast.129, bf16[512,2048]{1,0:T(8,128)(2,1)} %collective-permute-done.28.refs_2_, ...), custom_call_target="tpu_custom_call" | custom-call | flops 2952790016 | bytes 5767168 | tf_op jit(solution)/shard_map/planes_grad/pallas_call | solution.py:362
  318.6 5.9 %collective-permute-done.35 = f32[145,128]{1,0:T(8,128)S(1)} collective-permute-done((f32[145,128]{1,0:T(8,128)S(1)}, f32[145,128]{1,0:T(8,128)S(1)}, u32[]{:S(2)}, u32[]{:S(2)}) %collective-permute-start.35) | collective-permute-done | bytes 74272 | tf_op jit(solution)/shard_map/ppermute | solution.py:644
  325.2 12.3 %planes_grad.3 = (f32[3,2048,512]{2,1,0:T(8,128)}, bf16[3,1024,512]{2,1,0:T(8,128)(2,1)}) custom-call(s32[1]{0:T(128)} %bitcast.32.core_ref, bf16[1024,2048]{1,0:T(8,128)(2,1)} %bitcast.45.refs_0_, bf16[1024,2048]{1,0:T(8,128)(2,1)} %collective-permute-done.42.refs_1_, bf16[3,1024,512]{2,1,0:T(8,128)(2,1)} %all-gather.10.cloned.1.call-done.refs_2_, ...), custom_call_target="tpu_custom_call" | custom-call | flops 1610612736 | bytes 3145728 | tf_op jit(solution)/shard_map/planes_grad/pallas_call | solution.py:362
  341.3 10.9 %collective-permute-done.37 = f32[145,128]{1,0:T(8,128)S(1)} collective-permute-done((f32[145,128]{1,0:T(8,128)}, f32[145,128]{1,0:T(8,128)S(1)}, u32[]{:S(2)}, u32[]{:S(2)}) %collective-permute-start.37) | collective-permute-done | bytes 74272 | tf_op jit(solution)/shard_map/ppermute | solution.py:644
  374.9 5.2 %fusion.5 = f32[512,2048]{1,0:T(8,128)} fusion(bf16[256,2048]{1,0:T(8,128)(2,1)} %collective-permute-done.47, bf16[256,2048]{1,0:T(8,128)(2,1)} %reduce_sum.120, pred[]{:T(512)S(6)} %eq.11), kind=kLoop, calls=%fused_computation.19 | loop fusion | flops 10485760 | bytes 6291457 | tf_op jit(solution)/shard_map/convert_element_type | solution.py:668
  380.1 4.8 %turned_fill.1 = f32[1408,2048]{1,0:T(8,128)} custom-call(s32[1]{0:T(128)} %bitcast.32.core_ref, f32[1408,2048]{1,0:T(8,128)} %get-tuple-element.90.whole_ref, bf16[1408,1024]{1,0:T(8,128)(2,1)} %collective-permute-done.46.part_ref), custom_call_target="tpu_custom_call", output_to_operand_aliasing={{}: (1, {})} | custom-call | flops 1441792 | bytes 8650752 | tf_op jit(solution)/shard_map/turned_fill/pallas_call | solution.py:458
  385.0 8.4 %planes_fill.2 = f32[2,2048,1408]{2,1,0:T(8,128)} custom-call(s32[1]{0:T(128)} %bitcast.32.core_ref, f32[2,2048,1408]{2,1,0:T(8,128)} %get-tuple-element.89.whole_ref, bf16[2,1024,1408]{2,1,0:T(8,128)(2,1)} %collective-permute-done.45.part_ref), custom_call_target="tpu_custom_call", output_to_operand_aliasing={{}: (1, {})} | custom-call | flops 2883584 | bytes 17301504 | tf_op jit(solution)/shard_map/planes_fill/pallas_call | solution.py:383
  396.9 5.1 %planes_fill.3 = f32[3,2048,512]{2,1,0:T(8,128)} custom-call(s32[1]{0:T(128)} %bitcast.32.core_ref, f32[3,2048,512]{2,1,0:T(8,128)} %get-tuple-element.87.whole_ref, bf16[3,1024,512]{2,1,0:T(8,128)(2,1)S(1)} %copy-done.6), custom_call_target="tpu_custom_call", output_to_operand_aliasing={{}: (1, {})} | custom-call | flops 1572864 | bytes 9437184 | tf_op jit(solution)/shard_map/planes_fill/pallas_call | solution.py:383
  (284 shorter events, 160.4 us)
Async XLA Ops:
  7.2 54.5 %all-gather.12.cloned.1.call-start = ((), (), s32[]{:S(2)}) async-start(), calls=%async_computation.1 | async-start | bytes 1310720 | tf_op jit(solution)/shard_map/all_gather | solution.py:550
  13.8 21.4 %collective-permute-start.4 = (bf16[64,2048]{1,0:T(8,128)(2,1)}, bf16[64,2048]{1,0:T(8,128)(2,1)}, u32[]{:S(2)}, u32[]{:S(2)}) collective-permute-start(bf16[64,2048]{1,0:T(8,128)(2,1)} %param.23), channel_id=1, source_target_pairs={{0,2},{1,3},{2,0},{3,1},{4,6},{5,7},{6,4},{7,5},{8,10},{9,11},{10,... | collective-permute-start | bytes 786440 | tf_op jit(solution)/shard_map/ppermute | solution.py:513
  15.3 118.6 %all-gather.14.cloned.1.call-start = ((), (), s32[]{:S(2)}) async-start(), calls=%async_computation.2 | async-start | bytes 5242880 | tf_op jit(solution)/shard_map/all_gather | solution.py:554
  41.4 128.2 %all-gather.16.cloned.1.call-start = ((), (), s32[]{:S(2)}) async-start(), calls=%async_computation.3 | async-start | bytes 1310720 | tf_op jit(solution)/shard_map/all_gather | solution.py:563
  83.9 32.9 %collective-permute-start.12 = (bf16[4,64,2048]{2,1,0:T(8,128)(2,1)}, bf16[4,64,2048]{2,1,0:T(8,128)(2,1)S(1)}, u32[]{:S(2)}, u32[]{:S(2)}) collective-permute-start(bf16[4,64,2048]{2,1,0:T(8,128)(2,1)} %bitcast.147), channel_id=1, source_target_pairs={{0,1},{1,0},{2,3},{3,2},{4,5},{5,4},{6,7},{7,6},{8,9},{9,8},{10,11... | collective-permute-start | bytes 3145736 | tf_op jit(solution)/shard_map/ppermute | solution.py:518
  84.7 33.2 %collective-permute-start.13 = (bf16[4,64,2048]{2,1,0:T(8,128)(2,1)}, bf16[4,64,2048]{2,1,0:T(8,128)(2,1)S(1)}, u32[]{:S(2)}, u32[]{:S(2)}) collective-permute-start(bf16[4,64,2048]{2,1,0:T(8,128)(2,1)} %bitcast.148), channel_id=1, source_target_pairs={{0,2},{1,3},{2,0},{3,1},{4,6},{5,7},{6,4},{7,5},{8,10},{9,11},{10,... | collective-permute-start | bytes 3145736 | tf_op jit(solution)/shard_map/ppermute | solution.py:518
  141.0 60.9 %collective-permute-start.22 = (bf16[4,256,2048]{2,1,0:T(8,128)(2,1)}, bf16[4,256,2048]{2,1,0:T(8,128)(2,1)}, u32[]{:S(2)}, u32[]{:S(2)}) collective-permute-start(bf16[4,256,2048]{2,1,0:T(8,128)(2,1)} %bitcast.133), channel_id=1, source_target_pairs={{0,4},{4,0},{1,5},{5,1},{2,6},{6,2},{3,7},{7,3},{8,12},{12,8},{9,1... | collective-permute-start | bytes 12582920 | tf_op jit(solution)/shard_map/ppermute | solution.py:335
  141.1 131.0 %all-gather.10.cloned.1.call-start = ((), (), s32[]{:S(2)}) async-start(), calls=%async_computation | async-start | bytes 3932160 | tf_op jit(solution)/shard_map/all_gather | solution.py:588
  155.7 47.3 %collective-permute-start.23 = (bf16[256,2048]{1,0:T(8,128)(2,1)}, bf16[256,2048]{1,0:T(8,128)(2,1)}, u32[]{:S(2)}, u32[]{:S(2)}) collective-permute-start(bf16[256,2048]{1,0:T(8,128)(2,1)} %constant_dynamic-slice_fusion), channel_id=1, source_target_pairs={{0,4},{4,0},{1,5},{5,1},{2,6},{6,2},{3,7},{7,3},{8,12},{12,8},{9,1... | collective-permute-start | bytes 3145736 | tf_op jit(solution)/shard_map/ppermute | solution.py:335
  169.6 24.6 %collective-permute-start.21 = (bf16[4,64,2048]{2,1,0:T(8,128)(2,1)}, bf16[4,64,2048]{2,1,0:T(8,128)(2,1)S(1)}, u32[]{:S(2)}, u32[]{:S(2)}) collective-permute-start(bf16[4,64,2048]{2,1,0:T(8,128)(2,1)} %bitcast.154), channel_id=1, source_target_pairs={{0,1},{1,0},{2,3},{3,2},{4,5},{5,4},{6,7},{7,6},{8,9},{9,8},{10,11... | collective-permute-start | bytes 3145736 | tf_op jit(solution)/shard_map/ppermute | solution.py:518
  171.1 24.8 %collective-permute-start.20 = (bf16[4,64,2048]{2,1,0:T(8,128)(2,1)}, bf16[4,64,2048]{2,1,0:T(8,128)(2,1)S(1)}, u32[]{:S(2)}, u32[]{:S(2)}) collective-permute-start(bf16[4,64,2048]{2,1,0:T(8,128)(2,1)} %bitcast.155), channel_id=1, source_target_pairs={{0,2},{1,3},{2,0},{3,1},{4,6},{5,7},{6,4},{7,5},{8,10},{9,11},{10,... | collective-permute-start | bytes 3145736 | tf_op jit(solution)/shard_map/ppermute | solution.py:518
  178.8 176.5 %all-gather.18.cloned.1.call-start = ((), (), s32[]{:S(2)}) async-start(), calls=%async_computation.4 | async-start | bytes 5242880 | tf_op jit(solution)/shard_map/all_gather | solution.py:621
  194.3 28.4 %collective-permute-start.25 = (bf16[2,64,2048]{2,1,0:T(8,128)(2,1)S(1)}, bf16[2,64,2048]{2,1,0:T(8,128)(2,1)}, u32[]{:S(2)}, u32[]{:S(2)}) collective-permute-start(bf16[2,64,2048]{2,1,0:T(8,128)(2,1)S(1)} %slice.141), channel_id=1, source_target_pairs={{0,2},{1,3},{2,0},{3,1},{4,6},{5,7},{6,4},{7,5},{8,10},{9,11},{10,... | collective-permute-start | bytes 1572872 | tf_op jit(solution)/shard_map/ppermute | solution.py:518
  196.8 25.9 %collective-permute-start.24 = (bf16[2,64,2048]{2,1,0:T(8,128)(2,1)}, bf16[2,64,2048]{2,1,0:T(8,128)(2,1)}, u32[]{:S(2)}, u32[]{:S(2)}) collective-permute-start(bf16[2,64,2048]{2,1,0:T(8,128)(2,1)} %slice.140), channel_id=1, source_target_pairs={{0,1},{1,0},{2,3},{3,2},{4,5},{5,4},{6,7},{7,6},{8,9},{9,8},{10,11... | collective-permute-start | bytes 1572872 | tf_op jit(solution)/shard_map/ppermute | solution.py:518
  203.0 42.9 %collective-permute-start.28 = (bf16[512,2048]{1,0:T(8,128)(2,1)S(1)}, bf16[512,2048]{1,0:T(8,128)(2,1)}, u32[]{:S(2)}, u32[]{:S(2)}) collective-permute-start(bf16[512,2048]{1,0:T(8,128)(2,1)S(1)} %bitcast.124), channel_id=1, source_target_pairs={{0,4},{4,0},{1,5},{5,1},{2,6},{6,2},{3,7},{7,3},{8,12},{12,8},{9,1... | collective-permute-start | bytes 6291464 | tf_op jit(solution)/shard_map/ppermute | solution.py:335
  244.4 33.8 %collective-permute-start.32 = (bf16[3,512,1408]{2,1,0:T(8,128)(2,1)}, bf16[3,512,1408]{2,1,0:T(8,128)(2,1)}, u32[]{:S(2)}, u32[]{:S(2)}) collective-permute-start(bf16[3,512,1408]{2,1,0:T(8,128)(2,1)} %feed_forward_rows.2.refs_0_.refs_4_), channel_id=1, source_target_pairs={{0,4},{4,0},{1,5},{5,1},{2,6},{6,2},{3,7},{7,3},{8,12},{12,8},{9,1... | collective-permute-start | bytes 12976136 | tf_op jit(solution)/shard_map/ppermute | solution.py:335
  271.6 53.6 %collective-permute-start.42 = (bf16[1024,2048]{1,0:T(8,128)(2,1)}, bf16[1024,2048]{1,0:T(8,128)(2,1)}, u32[]{:S(2)}, u32[]{:S(2)}) collective-permute-start(bf16[1024,2048]{1,0:T(8,128)(2,1)} %bitcast.45.refs_0_), channel_id=1, source_target_pairs={{0,4},{4,0},{1,5},{5,1},{2,6},{6,2},{3,7},{7,3},{8,12},{12,8},{9,1... | collective-permute-start | bytes 12582920 | tf_op jit(solution)/shard_map/ppermute | solution.py:335
  272.0 53.1 %collective-permute-start.43 = (bf16[3,1024,512]{2,1,0:T(8,128)(2,1)}, bf16[3,1024,512]{2,1,0:T(8,128)(2,1)}, u32[]{:S(2)}, u32[]{:S(2)}) collective-permute-start(bf16[3,1024,512]{2,1,0:T(8,128)(2,1)} %all-gather.10.cloned.1.call-done.refs_2_), channel_id=1, source_target_pairs={{0,4},{4,0},{1,5},{5,1},{2,6},{6,2},{3,7},{7,3},{8,12},{12,8},{9,1... | collective-permute-start | bytes 9437192 | tf_op jit(solution)/shard_map/ppermute | solution.py:335
  276.7 38.0 %collective-permute-start.31 = (bf16[2,64,2048]{2,1,0:T(8,128)(2,1)S(1)}, bf16[2,64,2048]{2,1,0:T(8,128)(2,1)S(1)}, u32[]{:S(2)}, u32[]{:S(2)}) collective-permute-start(bf16[2,64,2048]{2,1,0:T(8,128)(2,1)S(1)} %get-tuple-element.104), channel_id=1, source_target_pairs={{0,3},{1,2},{2,1},{3,0},{4,7},{5,6},{6,5},{7,4},{8,11},{9,10},{10,... | collective-permute-start | bytes 1572872 | tf_op jit(solution)/shard_map/ppermute | solution.py:513
  278.2 37.3 %collective-permute-start.30 = (bf16[2,64,2048]{2,1,0:T(8,128)(2,1)}, bf16[2,64,2048]{2,1,0:T(8,128)(2,1)}, u32[]{:S(2)}, u32[]{:S(2)}) collective-permute-start(bf16[2,64,2048]{2,1,0:T(8,128)(2,1)} %get-tuple-element.105), channel_id=1, source_target_pairs={{0,2},{1,3},{2,0},{3,1},{4,6},{5,7},{6,4},{7,5},{8,10},{9,11},{10,... | collective-permute-start | bytes 1572872 | tf_op jit(solution)/shard_map/ppermute | solution.py:513
  279.6 35.9 %collective-permute-start.29 = (bf16[2,64,2048]{2,1,0:T(8,128)(2,1)S(1)}, bf16[2,64,2048]{2,1,0:T(8,128)(2,1)}, u32[]{:S(2)}, u32[]{:S(2)}) collective-permute-start(bf16[2,64,2048]{2,1,0:T(8,128)(2,1)S(1)} %get-tuple-element.103), channel_id=1, source_target_pairs={{0,1},{1,0},{2,3},{3,2},{4,5},{5,4},{6,7},{7,6},{8,9},{9,8},{10,11... | collective-permute-start | bytes 1572872 | tf_op jit(solution)/shard_map/ppermute | solution.py:513
  314.7 70.3 %collective-permute-start.45 = (bf16[2,1024,1408]{2,1,0:T(8,128)(2,1)}, bf16[2,1024,1408]{2,1,0:T(8,128)(2,1)}, u32[]{:S(2)}, u32[]{:S(2)}) collective-permute-start(bf16[2,1024,1408]{2,1,0:T(8,128)(2,1)} %get-tuple-element.85), channel_id=1, source_target_pairs={{0,4},{4,0},{1,5},{5,1},{2,6},{6,2},{3,7},{7,3},{8,12},{12,8},{9,1... | collective-permute-start | bytes 17301512 | tf_op jit(solution)/shard_map/ppermute | solution.py:335
  337.5 55.9 %collective-permute-start.44 = (bf16[3,1024,512]{2,1,0:T(8,128)(2,1)}, bf16[3,1024,512]{2,1,0:T(8,128)(2,1)S(1)}, u32[]{:S(2)}, u32[]{:S(2)}) collective-permute-start(bf16[3,1024,512]{2,1,0:T(8,128)(2,1)} %get-tuple-element.88), channel_id=1, source_target_pairs={{0,4},{4,0},{1,5},{5,1},{2,6},{6,2},{3,7},{7,3},{8,12},{12,8},{9,1... | collective-permute-start | bytes 9437192 | tf_op jit(solution)/shard_map/ppermute | solution.py:335
  337.7 42.4 %collective-permute-start.46 = (bf16[1408,1024]{1,0:T(8,128)(2,1)}, bf16[1408,1024]{1,0:T(8,128)(2,1)}, u32[]{:S(2)}, u32[]{:S(2)}) collective-permute-start(bf16[1408,1024]{1,0:T(8,128)(2,1)} %get-tuple-element.80), channel_id=1, source_target_pairs={{0,4},{4,0},{1,5},{5,1},{2,6},{6,2},{3,7},{7,3},{8,12},{12,8},{9,1... | collective-permute-start | bytes 8650760 | tf_op jit(solution)/shard_map/ppermute | solution.py:335
  (82 other events, 940.6 us)
Sparse Core Ops, SparseCore 0:
  15.4 27.3 all-gather.11
  44.9 80.1 all-gather.13
  141.2 28.3 all-gather.15
  178.9 61.0 all-gather.9
  267.6 87.5 all-gather.17

commit v4 on v3

--- a/solution.py
+++ b/solution.py
@@ -522,7 +522,7 @@
         for k in range(half + 1, shards):
             via = k ^ half
             cut = pieces[0].shape[0] // 2
-            far.append(jnp.concatenate([move(pieces[half][:cut], via), move(pieces[via][cut:], half)]))
+            far.append((move(pieces[half][:cut], via), move(pieces[via][cut:], half)))
         return far
 
     def gather_rows(own):
@@ -603,35 +603,39 @@
     cot_other = swap(cot_line)
     cot_line = cot_line.reshape(line, 2, half * rows, model)
     second_lines, line_rows, others = [], [], []
-    second_parts = second_parts + relay(second_parts)
+    second_far = relay(second_parts)
     hidden_near = [after(piece, second_parts[half]) for piece in hidden_near]
     hidden_far = relay([hidden_line, *hidden_near])
+
+    def joined(pair):
+        return jnp.concatenate([after(part, line_rows[0]) for part in pair])
+
     for h in range(2):
-        pieces = second_parts[h * half:(h + 1) * half]
+        pieces = second_parts[:half]
         if h == 1:
-            pieces = [after(piece, line_rows[0], out_half) for piece in pieces]
+            pieces = [after(second_parts[half], line_rows[0], out_half)] + [joined(pair) for pair in second_far]
         piece = jnp.stack(pieces, 1).reshape(line * half * rows, model)
         if h == 0:
             piece = after(piece, both, cot_other, second_parts[half])
         else:
-            piece = after(piece, *hidden_far, *others)
+            piece = after(piece, *[part for pair in hidden_far for part in pair], *others)
         second_lines.append(piece)
         others.append(swap(piece))
         line_rows.append(feed_forward_rows(piece, cot_line, h, gate_up_weight, down_weight))
     out_every = lax.all_gather(after(out_half, line_rows[0]), "z", axis=0)
-    hidden_every = jnp.stack([hidden_line, *hidden_near, *hidden_far])
+    hidden_every = jnp.stack([hidden_line, *hidden_near, *[joined(pair) for pair in hidden_far]])
+    both_parts = after(both, line_rows[0])
+    first_grad, ffn_rows = sum(
+        piece.astype(f32) for piece in exchange([both_parts[:, k] for k in range(shards)])
+    )
     row_others = [swap(part) for part in line_rows]
     down_part, down_finish = turned_grad(
-        core[None], [after(line_rows[0], row_others[0], projected_line, *others), line_rows[1], *row_others],
+        core[None], [after(line_rows[0], row_others[0], projected_line, first_grad, *others), line_rows[1], *row_others],
         [cot_line, cot_other.reshape(cot_line.shape)],
     )
     normed_every = norm_rows(hidden_every.astype(f32), norm1_gain).astype(bf16)
     normed_every = normed_every.transpose(1, 0, 2, 3).reshape(line * length, model)
 
-    both_parts = after(both, line_rows[1])
-    first_grad, ffn_rows = sum(
-        piece.astype(f32) for piece in exchange([both_parts[:, k] for k in range(shards)])
-    )
     first_grad = after(first_grad, down_part)
     block_out = (middle + ffn_rows).astype(bf16)
     rows_part, norm1_gain_grad = norm_back(first_grad, rows_in, norm1_gain)
@@ -656,8 +660,10 @@
         core[None], [after(normed_every, small, gate_up_part), swap(normed_every)],
         [projected_line, swap(projected_line)], 3,
     )
-    down_grad = down_finish(after(swap(down_part), qkv_part, out_every))
-    small = total(small, "z", line)
+    down_grad = down_finish(after(swap(down_part), qkv_part))
+    gate_up_grad = gate_up_finish(after(swap(gate_up_part), down_grad))
+    out_every = after(out_every, gate_up_grad)
+    small = total(after(small, out_every), "z", line)
     small = small.reshape(-1)
     gain_size = gains.size
     gains = total(small[:gain_size].reshape(-1, 128), "head", shards).reshape(-1)
@@ -666,7 +672,6 @@
     out_grad = jnp.where(
         core == 0, jnp.concatenate([out_rows, out_other]), jnp.concatenate([out_other, out_rows])
     ).astype(f32)
-    gate_up_grad = gate_up_finish(after(swap(gate_up_part), down_grad, small))
     qkv_grad = qkv_finish(after(swap(qkv_part), gate_up_grad))
     beta_size = beta_grad.size
     beta_grad = small[gain_size:gain_size + beta_size].reshape(beta_grad.shape[::-1]).T

time: 413 us -> 406 us (0.983)
    ppermute x21, waiting for transfers between devices: 44.2 us -> 62.9 us  [exchange(): lax.ppermute(parts[k], 'head', [(i, i ^ k) for i in range(shards)])]
    ppermute x8, waiting for transfers between devices: 28.2 us -> 19.3 us  [move(): return lax.ppermute(value, 'head', [(i, i ^ k) for i in range(shards)])]
    unnamed x115 -> x112, local copies, waits for them, and re-layouts: 15 us -> 13.9 us
  transfers between devices with their start and end apart: 53 -> 53, of which waited for: 21 -> 21; matrix products, arithmetic and copies ran while one was open for 26% -> 22% of each run, Pallas kernels for 30% -> 32%
where the time goes in v4:
time: 406 us; the launch traced here: 402 us
  Pallas kernels  130 us (32%)
  waiting for transfers between devices  101 us (25%)
  starting transfers between devices  47.5 us (12%)
  matrix products  44.1 us (11%)
  other arithmetic  41.1 us (10%)
  local copies, waits for them, and re-layouts  23.8 us (6%)
  between operations  14.8 us (4%)
    ppermute x21, waiting for transfers between devices, exchange(): lax.ppermute(parts[k], 'head', [(i, i ^ k) for i in range(shards)])  62.9 us
    dot_general x12, matrix products, dot(): return jnp.einsum(equation, left, right, preferred_element_type=f32)  44.1 us
    pallas_call x2, Pallas kernels, feed_forward_rows(): pl.pallas_call(rows_kernel, grid=(model // tile,), in_specs=[pl.BlockSpec...  39.8 us
    pallas_call x2, Pallas kernels, planes_grad(): pl.pallas_call(functools.partial(planes_kernel, pieces), grid_spec=pltpu....  34.4 us
    ppermute x21, starting transfers between devices, exchange(): lax.ppermute(parts[k], 'head', [(i, i ^ k) for i in range(shards)])  28.5 us
    ppermute x8, waiting for transfers between devices, move(): return lax.ppermute(value, 'head', [(i, i ^ k) for i in range(shards)])  19.3 us
    pallas_call x3, Pallas kernels, finish(): pl.pallas_call(planes_fill, grid_spec=pltpu.PrefetchScalarGridSpec(num_sc...  18.4 us
    ppermute x7, waiting for transfers between devices, total(): lax.ppermute(value, axis, [(i, i ^ k) for i in range(size)])  18.3 us
  transfers between devices with their start and end apart: 53, of which 21 were waited for; matrix products, arithmetic and copies ran while one was open for 22% of the time, Pallas kernels for 32%

profile of v4, /device:TPU:0, one launch (start us, length us, event | category | flops | bytes accessed | tf_op | source)
XLA Modules:
  0.0 402.1 jit_solution(6338117965261182763)
XLA Ops:
  26.9 6.1 %convolution_bitcast_fusion.3.proj_ref = f32[3,256,512]{2,1,0:T(8,128)} fusion(bf16[3,2048,512]{2,1,0:T(8,128)(2,1)} %param.14, bf16[64,2048]{1,0:T(8,128)(2,1)S(1)} %get-tuple-element.129, bf16[64,2048]{1,0:T(8,128)(2,1)S(1)} %get-tuple-element.128, bf16[64,2048]{1,0:T(8,128)(2,1)S(1)} %get-tuple-element.127, bf16[64,2048]{1,0:T(8,128)(2,1)S(1)} %get-tuple-element.126), kind=kOutput, calls=%fused_computation.21 | convolution fusion | flops 1614807040 | bytes 8912896 | tf_op jit(solution)/shard_map/td,sde->ste/dot_general | solution.py:493
  41.9 14.2 %mixer_forward.1 = (bf16[256,512]{1,0:T(8,128)(2,1)S(1)}, f32[3,256,512]{2,1,0:T(8,128)S(1)}, f32[256,512]{1,0:T(8,128)S(1)}, f32[256,512]{1,0:T(8,128)S(1)}, f3...) custom-call(s32[5]{0:T(128)S(1)} %pad_add_fusion.info_ref, f32[3,256,512]{2,1,0:T(8,128)} %convolution_bitcast_fusion.3.proj_ref, ...), custom_call_target="tpu_custom_call" | custom-call | flops 10000000000 | bytes 10485760 | tf_op jit(solution)/shard_map/mixer_forward/pallas_call | solution.py:232
  66.6 6.6 %collective-permute-done.8 = bf16[64,2048]{1,0:T(8,128)(2,1)S(1)} collective-permute-done((bf16[64,2048]{1,0:T(8,128)(2,1)S(1)}, bf16[64,2048]{1,0:T(8,128)(2,1)S(1)}, u32[]{:S(2)}, u32[]{:S(2)}) %collective-permute-start.8) | collective-permute-done | bytes 262176 | tf_op jit(solution)/shard_map/ppermute | solution.py:513
  86.1 4.8 %collective-permute-done.11 = bf16[64,2048]{1,0:T(8,128)(2,1)S(1)} collective-permute-done((bf16[64,2048]{1,0:T(8,128)(2,1)}, bf16[64,2048]{1,0:T(8,128)(2,1)S(1)}, u32[]{:S(2)}, u32[]{:S(2)}) %collective-permute-start.11) | collective-permute-done | bytes 262176 | tf_op jit(solution)/shard_map/ppermute | solution.py:513
  90.9 4.8 %collective-permute-done.10 = bf16[64,2048]{1,0:T(8,128)(2,1)S(1)} collective-permute-done((bf16[64,2048]{1,0:T(8,128)(2,1)}, bf16[64,2048]{1,0:T(8,128)(2,1)S(1)}, u32[]{:S(2)}, u32[]{:S(2)}) %collective-permute-start.10) | collective-permute-done | bytes 262176 | tf_op jit(solution)/shard_map/ppermute | solution.py:513
  95.7 6.8 %convolution_bitcast_fusion = f32[2,256,1408]{2,1,0:T(8,128)S(1)} fusion(bf16[2,2048,1408]{2,1,0:T(8,128)(2,1)} %gate_up_ref.3, bf16[64,2048]{1,0:T(8,128)(2,1)S(1)} %collective-permute-done.11, bf16[64,2048]{1,0:T(8,128)(2,1)S(1)} %collective-permute-done.10, bf16[64,2048]{1,0:T(8,128)(2,1)S(1)} %collective-permute-done.9, ...), kind=kOutput, calls=%fused_computation.6 | convolution fusion | flops 2956984320 | bytes 15466496 | tf_op jit(solution)/shard_map/td,sdf->stf/dot_general | solution.py:493
  102.6 6.3 %fusion.19 = (bf16[1,256,1408]{2,1,0:T(8,128)(2,1)S(1)}, bf16[1,256,1408]{2,1,0:T(8,128)(2,1)S(1)}) fusion(f32[2,256,1408]{2,1,0:T(8,128)S(1)} %convolution_bitcast_fusion, bf16[256,2048]{1,0:T(8,128)(2,1)} %constant_dynamic-update-slice_fusion, bf16[1408,2048]{1,0:T(8,128)(2,1)} %down_ref.3), kind=kOutput, calls=%fused_computation.51 | convolution fusion | flops 1481080832 | bytes 11141120 | tf_op jit(solution)/shard_map/td,fd->tf/dot_general | solution.py:493
  108.9 7.6 %fusion.3 = bf16[256,2048]{1,0:T(8,128)(2,1)S(1)} fusion(bf16[2,2048,1408]{2,1,0:T(8,128)(2,1)} %gate_up_ref.3, bf16[1,256,1408]{2,1,0:T(8,128)(2,1)S(1)} %get-tuple-element.112, bf16[1,256,1408]{2,1,0:T(8,128)(2,1)S(1)} %get-tuple-element.111), kind=kOutput, calls=%fused_computation.11 | convolution fusion | flops 2954035200 | bytes 14024704 | tf_op jit(solution)/shard_map/stf,sdf->td/dot_general | solution.py:493
  141.5 6.7 %collective-permute-done.19 = bf16[64,2048]{1,0:T(8,128)(2,1)} collective-permute-done((bf16[64,2048]{1,0:T(8,128)(2,1)}, bf16[64,2048]{1,0:T(8,128)(2,1)}, u32[]{:S(2)}, u32[]{:S(2)}) %collective-permute-start.19) | collective-permute-done | bytes 262176 | tf_op jit(solution)/shard_map/ppermute | solution.py:513
  154.7 10.0 %mixer_backward.1 = (bf16[3,256,512]{2,1,0:T(8,128)(2,1)}, f32[256,128]{1,0:T(8,128)S(1)}, f32[16,512]{1,0:T(8,128)S(1)}, f32[8,128]{1,0:T(8,128)S(1)}) custom-call(s32[5]{0:T(128)S(1)} %pad_add_fusion.info_ref, f32[256,512]{1,0:T(8,128)S(1)} %fusion.38.grad_ref, f32[3,256,512]{2,1,0:T(8,128)} %convolution_bitcast_fusion.3.proj_ref, ...), custom_call_target="tpu_custom_call" | custom-call | flops 20000000000 | bytes 14680064 | tf_op jit(solution)/shard_map/mixer_backward/pallas_call | solution.py:256
  164.8 4.9 %convolution_bitcast_fusion.1 = f32[256,2048]{1,0:T(8,128)S(1)} fusion(bf16[3,256,512]{2,1,0:T(8,128)(2,1)} %get-tuple-element.73, bf16[3,2048,512]{2,1,0:T(8,128)(2,1)} %param.14), kind=kOutput, calls=%fused_computation.8 | convolution fusion | flops 1610612736 | bytes 9175040 | tf_op jit(solution)/shard_map/ste,sde->td/dot_general | solution.py:493
  178.5 16.6 %collective-permute-done.20 = bf16[4,64,2048]{2,1,0:T(8,128)(2,1)S(1)} collective-permute-done((bf16[4,64,2048]{2,1,0:T(8,128)(2,1)}, bf16[4,64,2048]{2,1,0:T(8,128)(2,1)S(1)}, u32[]{:S(2)}, u32[]{:S(2)}) %collective-permute-start.20) | collective-permute-done | bytes 1048608 | tf_op jit(solution)/shard_map/ppermute | solution.py:518
  208.0 20.0 %feed_forward_rows.2.refs_0_.refs_4_ = bf16[3,512,1408]{2,1,0:T(8,128)(2,1)} custom-call(bf16[512,2048]{1,0:T(8,128)(2,1)} %bitcast.125, bf16[4,2,128,2048]{3,2,1,0:T(8,128)(2,1)} %bitcast.134, bf16[2,2048,1408]{2,1,0:T(8,128)(2,1)} %gate_up_ref.3, bf16[1408,2048]{1,0:T(8,128)(2,1)} %down_ref.3), custom_call_target="tpu_custom_call" | custom-call | flops 8858370048 | bytes 17301504 | tf_op jit(solution)/shard_map/feed_forward_rows/pallas_call | solution.py:315
  231.5 19.9 %feed_forward_rows.3.refs_1_.refs_5_ = bf16[3,512,1408]{2,1,0:T(8,128)(2,1)} custom-call(bf16[512,2048]{1,0:T(8,128)(2,1)} %bitcast.127, bf16[4,2,128,2048]{3,2,1,0:T(8,128)(2,1)} %bitcast.135, bf16[2,2048,1408]{2,1,0:T(8,128)(2,1)} %gate_up_ref.3, bf16[1408,2048]{1,0:T(8,128)(2,1)} %down_ref.3), custom_call_target="tpu_custom_call" | custom-call | flops 8858370048 | bytes 17301504 | tf_op jit(solution)/shard_map/feed_forward_rows/pallas_call | solution.py:315
  259.2 9.1 %collective-permute-done.25 = bf16[2,64,2048]{2,1,0:T(8,128)(2,1)} collective-permute-done((bf16[2,64,2048]{2,1,0:T(8,128)(2,1)}, bf16[2,64,2048]{2,1,0:T(8,128)(2,1)}, u32[]{:S(2)}, u32[]{:S(2)}) %collective-permute-start.25) | collective-permute-done | bytes 524320 | tf_op jit(solution)/shard_map/ppermute | solution.py:513
  272.2 7.3 %collective-permute-done.24 = bf16[2,64,2048]{2,1,0:T(8,128)(2,1)} collective-permute-done((bf16[2,64,2048]{2,1,0:T(8,128)(2,1)}, bf16[2,64,2048]{2,1,0:T(8,128)(2,1)}, u32[]{:S(2)}, u32[]{:S(2)}) %collective-permute-start.24) | collective-permute-done | bytes 524320 | tf_op jit(solution)/shard_map/ppermute | solution.py:513
  284.6 13.1 %turned_grad.1 = (f32[1408,2048]{1,0:T(8,128)}, bf16[1408,1024]{1,0:T(8,128)(2,1)S(1)}) custom-call(s32[1]{0:T(128)} %bitcast.28.core_ref, bf16[3,512,1408]{2,1,0:T(8,128)(2,1)} %feed_forward_rows.2.refs_0_.refs_4_, bf16[3,512,1408]{2,1,0:T(8,128)(2,1)} %feed_forward_rows.3.refs_1_.refs_5_, bf16[3,512,1408]{2,1,0:T(8,128)(2,1)} %collective-permute-done.26.refs_2_.refs_6_, ...), custom_call_target="tpu_custom_call" | custom-call | flops 1476395008 | bytes 2883584 | tf_op jit(solution)/shard_map/turned_grad/pallas_call | solution.py:436
  297.8 22.1 %planes_grad.2 = (f32[2,2048,1408]{2,1,0:T(8,128)}, bf16[2,1024,1408]{2,1,0:T(8,128)(2,1)}) custom-call(s32[1]{0:T(128)} %bitcast.28.core_ref, bf16[512,2048]{1,0:T(8,128)(2,1)S(1)} %bitcast.126, bf16[512,2048]{1,0:T(8,128)(2,1)S(1)} %bitcast.129, bf16[512,2048]{1,0:T(8,128)(2,1)} %collective-permute-done.27.refs_2_, ...), custom_call_target="tpu_custom_call" | custom-call | flops 2952790016 | bytes 5767168 | tf_op jit(solution)/shard_map/planes_grad/pallas_call | solution.py:362
  321.8 16.6 %collective-permute-done.35 = f32[145,128]{1,0:T(8,128)S(1)} collective-permute-done((f32[145,128]{1,0:T(8,128)S(1)}, f32[145,128]{1,0:T(8,128)S(1)}, u32[]{:S(2)}, u32[]{:S(2)}) %collective-permute-start.35) | collective-permute-done | bytes 74272 | tf_op jit(solution)/shard_map/ppermute | solution.py:648
  338.4 12.3 %planes_grad.3 = (f32[3,2048,512]{2,1,0:T(8,128)}, bf16[3,1024,512]{2,1,0:T(8,128)(2,1)}) custom-call(s32[1]{0:T(128)} %bitcast.28.core_ref, bf16[1024,2048]{1,0:T(8,128)(2,1)} %bitcast.45.refs_0_, bf16[1024,2048]{1,0:T(8,128)(2,1)} %collective-permute-done.38.refs_1_, bf16[3,1024,512]{2,1,0:T(8,128)(2,1)} %all-gather.10.cloned.1.call-done.refs_2_, ...), custom_call_target="tpu_custom_call" | custom-call | flops 1610612736 | bytes 3145728 | tf_op jit(solution)/shard_map/planes_grad/pallas_call | solution.py:362
  350.8 4.8 %turned_fill.1 = f32[1408,2048]{1,0:T(8,128)} custom-call(s32[1]{0:T(128)} %bitcast.28.core_ref, f32[1408,2048]{1,0:T(8,128)} %get-tuple-element.96.whole_ref, bf16[1408,1024]{1,0:T(8,128)(2,1)} %collective-permute-done.37.part_ref), custom_call_target="tpu_custom_call", output_to_operand_aliasing={{}: (1, {})} | custom-call | flops 1441792 | bytes 8650752 | tf_op jit(solution)/shard_map/turned_fill/pallas_call | solution.py:458
  355.7 8.4 %planes_fill.2 = f32[2,2048,1408]{2,1,0:T(8,128)} custom-call(s32[1]{0:T(128)} %bitcast.28.core_ref, f32[2,2048,1408]{2,1,0:T(8,128)} %get-tuple-element.94.whole_ref, bf16[2,1024,1408]{2,1,0:T(8,128)(2,1)} %collective-permute-done.36.part_ref), custom_call_target="tpu_custom_call", output_to_operand_aliasing={{}: (1, {})} | custom-call | flops 2883584 | bytes 17301504 | tf_op jit(solution)/shard_map/planes_fill/pallas_call | solution.py:383
  381.9 5.2 %planes_fill.3 = f32[3,2048,512]{2,1,0:T(8,128)} custom-call(s32[1]{0:T(128)} %bitcast.28.core_ref, f32[3,2048,512]{2,1,0:T(8,128)} %get-tuple-element.103.whole_ref, bf16[3,1024,512]{2,1,0:T(8,128)(2,1)S(1)} %collective-permute-done.46.part_ref), custom_call_target="tpu_custom_call", output_to_operand_aliasing={{}: (1, {})} | custom-call | flops 1572864 | bytes 9437184 | tf_op jit(solution)/shard_map/planes_fill/pallas_call | solution.py:383
  390.2 5.1 %fusion.5 = f32[512,2048]{1,0:T(8,128)} fusion(bf16[256,2048]{1,0:T(8,128)(2,1)} %collective-permute-done.47, bf16[256,2048]{1,0:T(8,128)(2,1)} %reduce_sum.120, pred[]{:T(512)S(6)} %eq.11), kind=kLoop, calls=%fused_computation.19 | loop fusion | flops 10485760 | bytes 6291457 | tf_op jit(solution)/shard_map/convert_element_type | solution.py:674
  (281 shorter events, 148.0 us)
Async XLA Ops:
  7.2 54.7 %all-gather.12.cloned.1.call-start = ((), (), s32[]{:S(2)}) async-start(), calls=%async_computation.1 | async-start | bytes 1310720 | tf_op jit(solution)/shard_map/all_gather | solution.py:550
  15.3 118.8 %all-gather.14.cloned.1.call-start = ((), (), s32[]{:S(2)}) async-start(), calls=%async_computation.2 | async-start | bytes 5242880 | tf_op jit(solution)/shard_map/all_gather | solution.py:554
  41.5 128.3 %all-gather.16.cloned.1.call-start = ((), (), s32[]{:S(2)}) async-start(), calls=%async_computation.3 | async-start | bytes 1310720 | tf_op jit(solution)/shard_map/all_gather | solution.py:563
  84.1 32.8 %collective-permute-start.12 = (bf16[4,64,2048]{2,1,0:T(8,128)(2,1)}, bf16[4,64,2048]{2,1,0:T(8,128)(2,1)S(1)}, u32[]{:S(2)}, u32[]{:S(2)}) collective-permute-start(bf16[4,64,2048]{2,1,0:T(8,128)(2,1)} %bitcast.144), channel_id=1, source_target_pairs={{0,1},{1,0},{2,3},{3,2},{4,5},{5,4},{6,7},{7,6},{8,9},{9,8},{10,11... | collective-permute-start | bytes 3145736 | tf_op jit(solution)/shard_map/ppermute | solution.py:518
  84.9 33.2 %collective-permute-start.13 = (bf16[4,64,2048]{2,1,0:T(8,128)(2,1)}, bf16[4,64,2048]{2,1,0:T(8,128)(2,1)S(1)}, u32[]{:S(2)}, u32[]{:S(2)}) collective-permute-start(bf16[4,64,2048]{2,1,0:T(8,128)(2,1)} %bitcast.145), channel_id=1, source_target_pairs={{0,2},{1,3},{2,0},{3,1},{4,6},{5,7},{6,4},{7,5},{8,10},{9,11},{10,... | collective-permute-start | bytes 3145736 | tf_op jit(solution)/shard_map/ppermute | solution.py:518
  141.2 56.2 %collective-permute-start.21 = (bf16[4,256,2048]{2,1,0:T(8,128)(2,1)}, bf16[4,256,2048]{2,1,0:T(8,128)(2,1)}, u32[]{:S(2)}, u32[]{:S(2)}) collective-permute-start(bf16[4,256,2048]{2,1,0:T(8,128)(2,1)} %bitcast.133), channel_id=1, source_target_pairs={{0,4},{4,0},{1,5},{5,1},{2,6},{6,2},{3,7},{7,3},{8,12},{12,8},{9,1... | collective-permute-start | bytes 12582920 | tf_op jit(solution)/shard_map/ppermute | solution.py:335
  141.2 143.4 %all-gather.10.cloned.1.call-start = ((), (), s32[]{:S(2)}) async-start(), calls=%async_computation | async-start | bytes 3932160 | tf_op jit(solution)/shard_map/all_gather | solution.py:588
  164.8 199.3 %all-gather.18.cloned.1.call-start = ((), (), s32[]{:S(2)}) async-start(), calls=%async_computation.4 | async-start | bytes 5242880 | tf_op jit(solution)/shard_map/all_gather | solution.py:625
  169.8 25.3 %collective-permute-start.20 = (bf16[4,64,2048]{2,1,0:T(8,128)(2,1)}, bf16[4,64,2048]{2,1,0:T(8,128)(2,1)S(1)}, u32[]{:S(2)}, u32[]{:S(2)}) collective-permute-start(bf16[4,64,2048]{2,1,0:T(8,128)(2,1)} %bitcast.151), channel_id=1, source_target_pairs={{0,1},{1,0},{2,3},{3,2},{4,5},{5,4},{6,7},{7,6},{8,9},{9,8},{10,11... | collective-permute-start | bytes 3145736 | tf_op jit(solution)/shard_map/ppermute | solution.py:518
  173.2 24.2 %collective-permute-start.22 = (bf16[4,64,2048]{2,1,0:T(8,128)(2,1)S(1)}, bf16[4,64,2048]{2,1,0:T(8,128)(2,1)S(1)}, u32[]{:S(2)}, u32[]{:S(2)}) collective-permute-start(bf16[4,64,2048]{2,1,0:T(8,128)(2,1)S(1)} %bitcast.152), channel_id=1, source_target_pairs={{0,2},{1,3},{2,0},{3,1},{4,6},{5,7},{6,4},{7,5},{8,10},{9,11},{10,... | collective-permute-start | bytes 3145736 | tf_op jit(solution)/shard_map/ppermute | solution.py:518
  175.8 22.6 %collective-permute-start.28 = (bf16[256,2048]{1,0:T(8,128)(2,1)}, bf16[256,2048]{1,0:T(8,128)(2,1)}, u32[]{:S(2)}, u32[]{:S(2)}) collective-permute-start(bf16[256,2048]{1,0:T(8,128)(2,1)} %constant_dynamic-slice_fusion), channel_id=1, source_target_pairs={{0,4},{4,0},{1,5},{5,1},{2,6},{6,2},{3,7},{7,3},{8,12},{12,8},{9,1... | collective-permute-start | bytes 3145736 | tf_op jit(solution)/shard_map/ppermute | solution.py:335
  198.4 32.4 %collective-permute-start.27 = (bf16[512,2048]{1,0:T(8,128)(2,1)S(1)}, bf16[512,2048]{1,0:T(8,128)(2,1)}, u32[]{:S(2)}, u32[]{:S(2)}) collective-permute-start(bf16[512,2048]{1,0:T(8,128)(2,1)S(1)} %bitcast.124), channel_id=1, source_target_pairs={{0,4},{4,0},{1,5},{5,1},{2,6},{6,2},{3,7},{7,3},{8,12},{12,8},{9,1... | collective-permute-start | bytes 6291464 | tf_op jit(solution)/shard_map/ppermute | solution.py:335
  202.5 25.5 %collective-permute-start.30 = (bf16[2,64,2048]{2,1,0:T(8,128)(2,1)S(1)}, bf16[2,64,2048]{2,1,0:T(8,128)(2,1)S(1)}, u32[]{:S(2)}, u32[]{:S(2)}) collective-permute-start(bf16[2,64,2048]{2,1,0:T(8,128)(2,1)S(1)} %slice.141), channel_id=1, source_target_pairs={{0,2},{1,3},{2,0},{3,1},{4,6},{5,7},{6,4},{7,5},{8,10},{9,11},{10,... | collective-permute-start | bytes 1572872 | tf_op jit(solution)/shard_map/ppermute | solution.py:518
  205.2 22.9 %collective-permute-start.29 = (bf16[2,64,2048]{2,1,0:T(8,128)(2,1)S(1)}, bf16[2,64,2048]{2,1,0:T(8,128)(2,1)S(1)}, u32[]{:S(2)}, u32[]{:S(2)}) collective-permute-start(bf16[2,64,2048]{2,1,0:T(8,128)(2,1)S(1)} %slice.140), channel_id=1, source_target_pairs={{0,1},{1,0},{2,3},{3,2},{4,5},{5,4},{6,7},{7,6},{8,9},{9,8},{10,11... | collective-permute-start | bytes 1572872 | tf_op jit(solution)/shard_map/ppermute | solution.py:518
  205.9 24.8 %collective-permute-start.31 = (bf16[2,64,2048]{2,1,0:T(8,128)(2,1)S(1)}, bf16[2,64,2048]{2,1,0:T(8,128)(2,1)S(1)}, u32[]{:S(2)}, u32[]{:S(2)}) collective-permute-start(bf16[2,64,2048]{2,1,0:T(8,128)(2,1)S(1)} %slice.124), channel_id=1, source_target_pairs={{0,1},{1,0},{2,3},{3,2},{4,5},{5,4},{6,7},{7,6},{8,9},{9,8},{10,11... | collective-permute-start | bytes 1572872 | tf_op jit(solution)/shard_map/ppermute | solution.py:518
  207.4 23.3 %collective-permute-start.32 = (bf16[2,64,2048]{2,1,0:T(8,128)(2,1)S(1)}, bf16[2,64,2048]{2,1,0:T(8,128)(2,1)S(1)}, u32[]{:S(2)}, u32[]{:S(2)}) collective-permute-start(bf16[2,64,2048]{2,1,0:T(8,128)(2,1)S(1)} %slice.125), channel_id=1, source_target_pairs={{0,2},{1,3},{2,0},{3,1},{4,6},{5,7},{6,4},{7,5},{8,10},{9,11},{10,... | collective-permute-start | bytes 1572872 | tf_op jit(solution)/shard_map/ppermute | solution.py:518
  228.0 56.6 %collective-permute-start.26 = (bf16[3,512,1408]{2,1,0:T(8,128)(2,1)}, bf16[3,512,1408]{2,1,0:T(8,128)(2,1)}, u32[]{:S(2)}, u32[]{:S(2)}) collective-permute-start(bf16[3,512,1408]{2,1,0:T(8,128)(2,1)} %feed_forward_rows.2.refs_0_.refs_4_), channel_id=1, source_target_pairs={{0,4},{4,0},{1,5},{5,1},{2,6},{6,2},{3,7},{7,3},{8,12},{12,8},{9,1... | collective-permute-start | bytes 12976136 | tf_op jit(solution)/shard_map/ppermute | solution.py:335
  251.4 33.2 %collective-permute-start.34 = (bf16[3,512,1408]{2,1,0:T(8,128)(2,1)}, bf16[3,512,1408]{2,1,0:T(8,128)(2,1)}, u32[]{:S(2)}, u32[]{:S(2)}) collective-permute-start(bf16[3,512,1408]{2,1,0:T(8,128)(2,1)} %feed_forward_rows.3.refs_1_.refs_5_), channel_id=1, source_target_pairs={{0,4},{4,0},{1,5},{5,1},{2,6},{6,2},{3,7},{7,3},{8,12},{12,8},{9,1... | collective-permute-start | bytes 12976136 | tf_op jit(solution)/shard_map/ppermute | solution.py:335
  254.2 25.3 %collective-permute-start.24 = (bf16[2,64,2048]{2,1,0:T(8,128)(2,1)}, bf16[2,64,2048]{2,1,0:T(8,128)(2,1)}, u32[]{:S(2)}, u32[]{:S(2)}) collective-permute-start(bf16[2,64,2048]{2,1,0:T(8,128)(2,1)} %get-tuple-element.115), channel_id=1, source_target_pairs={{0,2},{1,3},{2,0},{3,1},{4,6},{5,7},{6,4},{7,5},{8,10},{9,11},{10,... | collective-permute-start | bytes 1572872 | tf_op jit(solution)/shard_map/ppermute | solution.py:513
  256.7 27.9 %collective-permute-start.33 = (bf16[512,2048]{1,0:T(8,128)(2,1)S(1)}, bf16[512,2048]{1,0:T(8,128)(2,1)}, u32[]{:S(2)}, u32[]{:S(2)}) collective-permute-start(bf16[512,2048]{1,0:T(8,128)(2,1)S(1)} %bitcast.128), channel_id=1, source_target_pairs={{0,4},{4,0},{1,5},{5,1},{2,6},{6,2},{3,7},{7,3},{8,12},{12,8},{9,1... | collective-permute-start | bytes 6291464 | tf_op jit(solution)/shard_map/ppermute | solution.py:335
  279.5 58.9 %collective-permute-start.38 = (bf16[1024,2048]{1,0:T(8,128)(2,1)}, bf16[1024,2048]{1,0:T(8,128)(2,1)}, u32[]{:S(2)}, u32[]{:S(2)}) collective-permute-start(bf16[1024,2048]{1,0:T(8,128)(2,1)} %bitcast.45.refs_0_), channel_id=1, source_target_pairs={{0,4},{4,0},{1,5},{5,1},{2,6},{6,2},{3,7},{7,3},{8,12},{12,8},{9,1... | collective-permute-start | bytes 12582920 | tf_op jit(solution)/shard_map/ppermute | solution.py:335
  319.9 35.7 %collective-permute-start.36 = (bf16[2,1024,1408]{2,1,0:T(8,128)(2,1)}, bf16[2,1024,1408]{2,1,0:T(8,128)(2,1)}, u32[]{:S(2)}, u32[]{:S(2)}) collective-permute-start(bf16[2,1024,1408]{2,1,0:T(8,128)(2,1)} %get-tuple-element.95), channel_id=1, source_target_pairs={{0,4},{4,0},{1,5},{5,1},{2,6},{6,2},{3,7},{7,3},{8,12},{12,8},{9,1... | collective-permute-start | bytes 17301512 | tf_op jit(solution)/shard_map/ppermute | solution.py:335
  320.8 30.0 %collective-permute-start.37 = (bf16[1408,1024]{1,0:T(8,128)(2,1)}, bf16[1408,1024]{1,0:T(8,128)(2,1)}, u32[]{:S(2)}, u32[]{:S(2)}) collective-permute-start(bf16[1408,1024]{1,0:T(8,128)(2,1)} %copy-done.5), channel_id=1, source_target_pairs={{0,4},{4,0},{1,5},{5,1},{2,6},{6,2},{3,7},{7,3},{8,12},{12,8},{9,1... | collective-permute-start | bytes 8650760 | tf_op jit(solution)/shard_map/ppermute | solution.py:335
  350.7 31.2 %collective-permute-start.46 = (bf16[3,1024,512]{2,1,0:T(8,128)(2,1)}, bf16[3,1024,512]{2,1,0:T(8,128)(2,1)S(1)}, u32[]{:S(2)}, u32[]{:S(2)}) collective-permute-start(bf16[3,1024,512]{2,1,0:T(8,128)(2,1)} %get-tuple-element.98), channel_id=1, source_target_pairs={{0,4},{4,0},{1,5},{5,1},{2,6},{6,2},{3,7},{7,3},{8,12},{12,8},{9,1... | collective-permute-start | bytes 9437192 | tf_op jit(solution)/shard_map/ppermute | solution.py:335
  (81 other events, 951.3 us)
Sparse Core Ops, SparseCore 0:
  15.4 27.3 all-gather.11
  44.4 80.1 all-gather.13
  141.3 28.3 all-gather.15
  171.2 62.7 all-gather.9
  255.6 80.9 all-gather.17

commit v5 on v4

--- a/solution.py
+++ b/solution.py
@@ -657,7 +657,7 @@
     )
     small = total(small, "core", 2)
     qkv_part, qkv_finish = planes_grad(
-        core[None], [after(normed_every, small, gate_up_part), swap(normed_every)],
+        core[None], [after(normed_every, gate_up_part), swap(normed_every)],
         [projected_line, swap(projected_line)], 3,
     )
     down_grad = down_finish(after(swap(down_part), qkv_part))

time: 406 us -> 407 us (level)
    ppermute x12, waiting for transfers between devices: 0.03 us -> 13.5 us  [swap(): return lax.ppermute(value, 'core', [(0, 1), (1, 0)])]
    ppermute x7, waiting for transfers between devices: 18.3 us -> 5.21 us  [total(): lax.ppermute(value, axis, [(i, i ^ k) for i in range(size)])]
    unnamed x112 -> x120, local copies, waits for them, and re-layouts: 13.9 us -> 13.7 us
  transfers between devices with their start and end apart: 53 -> 53, of which waited for: 21 -> 22; matrix products, arithmetic and copies ran while one was open for 22% -> 23% of each run, Pallas kernels for 32% -> 32%
where the time goes in v5:
time: 407 us; the launch traced here: 403 us
  Pallas kernels  130 us (32%)
  waiting for transfers between devices  101 us (25%)
  starting transfers between devices  47.4 us (12%)
  matrix products  43.8 us (11%)
  other arithmetic  41.7 us (10%)
  local copies, waits for them, and re-layouts  24.4 us (6%)
  between operations  14.9 us (4%)
    ppermute x21, waiting for transfers between devices, exchange(): lax.ppermute(parts[k], 'head', [(i, i ^ k) for i in range(shards)])  62.5 us
    dot_general x12, matrix products, dot(): return jnp.einsum(equation, left, right, preferred_element_type=f32)  43.8 us
    pallas_call x2, Pallas kernels, feed_forward_rows(): pl.pallas_call(rows_kernel, grid=(model // tile,), in_specs=[pl.BlockSpec...  40.1 us
    pallas_call x2, Pallas kernels, planes_grad(): pl.pallas_call(functools.partial(planes_kernel, pieces), grid_spec=pltpu....  33.7 us
    ppermute x21, starting transfers between devices, exchange(): lax.ppermute(parts[k], 'head', [(i, i ^ k) for i in range(shards)])  28.6 us
    ppermute x8, waiting for transfers between devices, move(): return lax.ppermute(value, 'head', [(i, i ^ k) for i in range(shards)])  19.4 us
    pallas_call x3, Pallas kernels, finish(): pl.pallas_call(planes_fill, grid_spec=pltpu.PrefetchScalarGridSpec(num_sc...  18.5 us
    pallas_call x1, Pallas kernels, mixer_forward(): pl.pallas_call(functools.partial(forward_kernel, rows, shards, blocks), o...  14.2 us
  transfers between devices with their start and end apart: 53, of which 22 were waited for; matrix products, arithmetic and copies ran while one was open for 23% of the time, Pallas kernels for 32%

profile of v5, /device:TPU:0, one launch (start us, length us, event | category | flops | bytes accessed | tf_op | source)
XLA Modules:
  0.0 402.8 jit_solution(15891717725327376101)
XLA Ops:
  26.9 6.1 %convolution_bitcast_fusion.3.proj_ref = f32[3,256,512]{2,1,0:T(8,128)} fusion(bf16[3,2048,512]{2,1,0:T(8,128)(2,1)} %param.14, bf16[64,2048]{1,0:T(8,128)(2,1)S(1)} %get-tuple-element.129, bf16[64,2048]{1,0:T(8,128)(2,1)S(1)} %get-tuple-element.128, bf16[64,2048]{1,0:T(8,128)(2,1)S(1)} %get-tuple-element.127, bf16[64,2048]{1,0:T(8,128)(2,1)S(1)} %get-tuple-element.126), kind=kOutput, calls=%fused_computation.21 | convolution fusion | flops 1614807040 | bytes 8912896 | tf_op jit(solution)/shard_map/td,sde->ste/dot_general | solution.py:493
  41.8 14.2 %mixer_forward.1 = (bf16[256,512]{1,0:T(8,128)(2,1)S(1)}, f32[3,256,512]{2,1,0:T(8,128)S(1)}, f32[256,512]{1,0:T(8,128)S(1)}, f32[256,512]{1,0:T(8,128)S(1)}, f3...) custom-call(s32[5]{0:T(128)S(1)} %pad_add_fusion.info_ref, f32[3,256,512]{2,1,0:T(8,128)} %convolution_bitcast_fusion.3.proj_ref, ...), custom_call_target="tpu_custom_call" | custom-call | flops 10000000000 | bytes 10485760 | tf_op jit(solution)/shard_map/mixer_forward/pallas_call | solution.py:232
  66.5 6.6 %collective-permute-done.8 = bf16[64,2048]{1,0:T(8,128)(2,1)S(1)} collective-permute-done((bf16[64,2048]{1,0:T(8,128)(2,1)S(1)}, bf16[64,2048]{1,0:T(8,128)(2,1)S(1)}, u32[]{:S(2)}, u32[]{:S(2)}) %collective-permute-start.8) | collective-permute-done | bytes 262176 | tf_op jit(solution)/shard_map/ppermute | solution.py:513
  90.0 4.8 %collective-permute-done.10 = bf16[64,2048]{1,0:T(8,128)(2,1)S(1)} collective-permute-done((bf16[64,2048]{1,0:T(8,128)(2,1)S(1)}, bf16[64,2048]{1,0:T(8,128)(2,1)S(1)}, u32[]{:S(2)}, u32[]{:S(2)}) %collective-permute-start.10) | collective-permute-done | bytes 262176 | tf_op jit(solution)/shard_map/ppermute | solution.py:513
  94.8 6.8 %convolution_bitcast_fusion = f32[2,256,1408]{2,1,0:T(8,128)S(1)} fusion(bf16[2,2048,1408]{2,1,0:T(8,128)(2,1)} %gate_up_ref.3, bf16[64,2048]{1,0:T(8,128)(2,1)S(1)} %collective-permute-done.11, bf16[64,2048]{1,0:T(8,128)(2,1)S(1)} %collective-permute-done.10, bf16[64,2048]{1,0:T(8,128)(2,1)S(1)} %collective-permute-done.9, ...), kind=kOutput, calls=%fused_computation.6 | convolution fusion | flops 2956984320 | bytes 15466496 | tf_op jit(solution)/shard_map/td,sdf->stf/dot_general | solution.py:493
  101.7 6.3 %fusion.19 = (bf16[1,256,1408]{2,1,0:T(8,128)(2,1)S(1)}, bf16[1,256,1408]{2,1,0:T(8,128)(2,1)S(1)}) fusion(f32[2,256,1408]{2,1,0:T(8,128)S(1)} %convolution_bitcast_fusion, bf16[256,2048]{1,0:T(8,128)(2,1)} %constant_dynamic-update-slice_fusion, bf16[1408,2048]{1,0:T(8,128)(2,1)} %down_ref.3), kind=kOutput, calls=%fused_computation.51 | convolution fusion | flops 1481080832 | bytes 11141120 | tf_op jit(solution)/shard_map/td,fd->tf/dot_general | solution.py:493
  108.0 7.6 %fusion.3 = bf16[256,2048]{1,0:T(8,128)(2,1)S(1)} fusion(bf16[2,2048,1408]{2,1,0:T(8,128)(2,1)} %gate_up_ref.3, bf16[1,256,1408]{2,1,0:T(8,128)(2,1)S(1)} %get-tuple-element.112, bf16[1,256,1408]{2,1,0:T(8,128)(2,1)S(1)} %get-tuple-element.111), kind=kOutput, calls=%fused_computation.11 | convolution fusion | flops 2954035200 | bytes 14024704 | tf_op jit(solution)/shard_map/stf,sdf->td/dot_general | solution.py:493
  127.5 4.7 %collective-permute-done.15 = bf16[64,2048]{1,0:T(8,128)(2,1)S(1)} collective-permute-done((bf16[64,2048]{1,0:T(8,128)(2,1)S(1)}, bf16[64,2048]{1,0:T(8,128)(2,1)S(1)}, u32[]{:S(2)}, u32[]{:S(2)}) %collective-permute-start.15) | collective-permute-done | bytes 262176 | tf_op jit(solution)/shard_map/ppermute | solution.py:513
  140.5 6.6 %collective-permute-done.19 = bf16[64,2048]{1,0:T(8,128)(2,1)S(1)} collective-permute-done((bf16[64,2048]{1,0:T(8,128)(2,1)}, bf16[64,2048]{1,0:T(8,128)(2,1)S(1)}, u32[]{:S(2)}, u32[]{:S(2)}) %collective-permute-start.19) | collective-permute-done | bytes 262176 | tf_op jit(solution)/shard_map/ppermute | solution.py:513
  153.7 10.0 %mixer_backward.1 = (bf16[3,256,512]{2,1,0:T(8,128)(2,1)}, f32[256,128]{1,0:T(8,128)S(1)}, f32[16,512]{1,0:T(8,128)S(1)}, f32[8,128]{1,0:T(8,128)S(1)}) custom-call(s32[5]{0:T(128)S(1)} %pad_add_fusion.info_ref, f32[256,512]{1,0:T(8,128)S(1)} %fusion.38.grad_ref, f32[3,256,512]{2,1,0:T(8,128)} %convolution_bitcast_fusion.3.proj_ref, ...), custom_call_target="tpu_custom_call" | custom-call | flops 20000000000 | bytes 14680064 | tf_op jit(solution)/shard_map/mixer_backward/pallas_call | solution.py:256
  163.8 4.9 %convolution_bitcast_fusion.1 = f32[256,2048]{1,0:T(8,128)S(1)} fusion(bf16[3,256,512]{2,1,0:T(8,128)(2,1)} %get-tuple-element.73, bf16[3,2048,512]{2,1,0:T(8,128)(2,1)} %param.14), kind=kOutput, calls=%fused_computation.8 | convolution fusion | flops 1610612736 | bytes 9175040 | tf_op jit(solution)/shard_map/ste,sde->td/dot_general | solution.py:493
  177.4 16.7 %collective-permute-done.20 = bf16[4,64,2048]{2,1,0:T(8,128)(2,1)S(1)} collective-permute-done((bf16[4,64,2048]{2,1,0:T(8,128)(2,1)}, bf16[4,64,2048]{2,1,0:T(8,128)(2,1)S(1)}, u32[]{:S(2)}, u32[]{:S(2)}) %collective-permute-start.20) | collective-permute-done | bytes 1048608 | tf_op jit(solution)/shard_map/ppermute | solution.py:518
  207.1 20.0 %feed_forward_rows.2.refs_0_.refs_4_ = bf16[3,512,1408]{2,1,0:T(8,128)(2,1)} custom-call(bf16[512,2048]{1,0:T(8,128)(2,1)} %bitcast.125, bf16[4,2,128,2048]{3,2,1,0:T(8,128)(2,1)} %bitcast.134, bf16[2,2048,1408]{2,1,0:T(8,128)(2,1)} %gate_up_ref.3, bf16[1408,2048]{1,0:T(8,128)(2,1)} %down_ref.3), custom_call_target="tpu_custom_call" | custom-call | flops 8858370048 | bytes 17301504 | tf_op jit(solution)/shard_map/feed_forward_rows/pallas_call | solution.py:315
  229.8 20.1 %feed_forward_rows.3.refs_1_.refs_5_ = bf16[3,512,1408]{2,1,0:T(8,128)(2,1)} custom-call(bf16[512,2048]{1,0:T(8,128)(2,1)} %bitcast.127, bf16[4,2,128,2048]{3,2,1,0:T(8,128)(2,1)} %bitcast.135, bf16[2,2048,1408]{2,1,0:T(8,128)(2,1)} %gate_up_ref.3, bf16[1408,2048]{1,0:T(8,128)(2,1)} %down_ref.3), custom_call_target="tpu_custom_call" | custom-call | flops 8858370048 | bytes 17301504 | tf_op jit(solution)/shard_map/feed_forward_rows/pallas_call | solution.py:315
  257.9 8.9 %collective-permute-done.25 = bf16[2,64,2048]{2,1,0:T(8,128)(2,1)} collective-permute-done((bf16[2,64,2048]{2,1,0:T(8,128)(2,1)}, bf16[2,64,2048]{2,1,0:T(8,128)(2,1)}, u32[]{:S(2)}, u32[]{:S(2)}) %collective-permute-start.25) | collective-permute-done | bytes 524320 | tf_op jit(solution)/shard_map/ppermute | solution.py:513
  270.7 7.3 %collective-permute-done.24 = bf16[2,64,2048]{2,1,0:T(8,128)(2,1)} collective-permute-done((bf16[2,64,2048]{2,1,0:T(8,128)(2,1)}, bf16[2,64,2048]{2,1,0:T(8,128)(2,1)}, u32[]{:S(2)}, u32[]{:S(2)}) %collective-permute-start.24) | collective-permute-done | bytes 524320 | tf_op jit(solution)/shard_map/ppermute | solution.py:513
  282.9 13.2 %turned_grad.1 = (f32[1408,2048]{1,0:T(8,128)}, bf16[1408,1024]{1,0:T(8,128)(2,1)}) custom-call(s32[1]{0:T(128)} %bitcast.28.core_ref, bf16[3,512,1408]{2,1,0:T(8,128)(2,1)} %feed_forward_rows.2.refs_0_.refs_4_, bf16[3,512,1408]{2,1,0:T(8,128)(2,1)} %feed_forward_rows.3.refs_1_.refs_5_, bf16[3,512,1408]{2,1,0:T(8,128)(2,1)} %collective-permute-done.26.refs_2_.refs_6_, ...), custom_call_target="tpu_custom_call" | custom-call | flops 1476395008 | bytes 2883584 | tf_op jit(solution)/shard_map/turned_grad/pallas_call | solution.py:436
  296.1 21.4 %planes_grad.2 = (f32[2,2048,1408]{2,1,0:T(8,128)}, bf16[2,1024,1408]{2,1,0:T(8,128)(2,1)}) custom-call(s32[1]{0:T(128)} %bitcast.28.core_ref, bf16[512,2048]{1,0:T(8,128)(2,1)S(1)} %bitcast.126, bf16[512,2048]{1,0:T(8,128)(2,1)S(1)} %bitcast.129, bf16[512,2048]{1,0:T(8,128)(2,1)} %collective-permute-done.27.refs_2_, ...), custom_call_target="tpu_custom_call" | custom-call | flops 2952790016 | bytes 5767168 | tf_op jit(solution)/shard_map/planes_grad/pallas_call | solution.py:362
  318.3 13.5 %collective-permute-done.39.refs_3_ = bf16[3,1024,512]{2,1,0:T(8,128)(2,1)S(1)} collective-permute-done((bf16[3,1024,512]{2,1,0:T(8,128)(2,1)S(1)}, bf16[3,1024,512]{2,1,0:T(8,128)(2,1)S(1)}, u32[]{:S(2)}, u32[]{:S(2)}) %collective-permute-start.39) | collective-permute-done | bytes 3145760 | tf_op jit(solution)/shard_map/ppermute | solution.py:335
  333.5 12.2 %planes_grad.3 = (f32[3,2048,512]{2,1,0:T(8,128)}, bf16[3,1024,512]{2,1,0:T(8,128)(2,1)}) custom-call(s32[1]{0:T(128)} %bitcast.28.core_ref, bf16[1024,2048]{1,0:T(8,128)(2,1)} %bitcast.45.refs_0_, bf16[1024,2048]{1,0:T(8,128)(2,1)} %collective-permute-done.38.refs_1_, bf16[3,1024,512]{2,1,0:T(8,128)(2,1)} %all-gather.10.cloned.1.call-done.refs_2_, ...), custom_call_target="tpu_custom_call" | custom-call | flops 1610612736 | bytes 3145728 | tf_op jit(solution)/shard_map/planes_grad/pallas_call | solution.py:362
  351.7 4.8 %turned_fill.1 = f32[1408,2048]{1,0:T(8,128)} custom-call(s32[1]{0:T(128)} %bitcast.28.core_ref, f32[1408,2048]{1,0:T(8,128)} %get-tuple-element.96.whole_ref, bf16[1408,1024]{1,0:T(8,128)(2,1)} %collective-permute-done.37.part_ref), custom_call_target="tpu_custom_call", output_to_operand_aliasing={{}: (1, {})} | custom-call | flops 1441792 | bytes 8650752 | tf_op jit(solution)/shard_map/turned_fill/pallas_call | solution.py:458
  356.6 8.4 %planes_fill.2 = f32[2,2048,1408]{2,1,0:T(8,128)} custom-call(s32[1]{0:T(128)} %bitcast.28.core_ref, f32[2,2048,1408]{2,1,0:T(8,128)} %get-tuple-element.94.whole_ref, bf16[2,1024,1408]{2,1,0:T(8,128)(2,1)} %collective-permute-done.36.part_ref), custom_call_target="tpu_custom_call", output_to_operand_aliasing={{}: (1, {})} | custom-call | flops 2883584 | bytes 17301504 | tf_op jit(solution)/shard_map/planes_fill/pallas_call | solution.py:383
  382.6 5.2 %planes_fill.3 = f32[3,2048,512]{2,1,0:T(8,128)} custom-call(s32[1]{0:T(128)} %bitcast.28.core_ref, f32[3,2048,512]{2,1,0:T(8,128)} %get-tuple-element.103.whole_ref, bf16[3,1024,512]{2,1,0:T(8,128)(2,1)S(1)} %collective-permute-done.46.part_ref), custom_call_target="tpu_custom_call", output_to_operand_aliasing={{}: (1, {})} | custom-call | flops 1572864 | bytes 9437184 | tf_op jit(solution)/shard_map/planes_fill/pallas_call | solution.py:383
  390.9 5.1 %fusion.5 = f32[512,2048]{1,0:T(8,128)} fusion(bf16[256,2048]{1,0:T(8,128)(2,1)} %collective-permute-done.47, bf16[256,2048]{1,0:T(8,128)(2,1)} %reduce_sum.120, pred[]{:T(512)S(6)} %eq.11), kind=kLoop, calls=%fused_computation.19 | loop fusion | flops 10485760 | bytes 6291457 | tf_op jit(solution)/shard_map/convert_element_type | solution.py:674
  (289 shorter events, 152.4 us)
Async XLA Ops:
  7.2 54.6 %all-gather.12.cloned.1.call-start = ((), (), s32[]{:S(2)}) async-start(), calls=%async_computation.1 | async-start | bytes 1310720 | tf_op jit(solution)/shard_map/all_gather | solution.py:550
  15.3 117.8 %all-gather.14.cloned.1.call-start = ((), (), s32[]{:S(2)}) async-start(), calls=%async_computation.2 | async-start | bytes 5242880 | tf_op jit(solution)/shard_map/all_gather | solution.py:554
  41.5 127.4 %all-gather.16.cloned.1.call-start = ((), (), s32[]{:S(2)}) async-start(), calls=%async_computation.3 | async-start | bytes 1310720 | tf_op jit(solution)/shard_map/all_gather | solution.py:563
  83.4 32.6 %collective-permute-start.12 = (bf16[4,64,2048]{2,1,0:T(8,128)(2,1)}, bf16[4,64,2048]{2,1,0:T(8,128)(2,1)S(1)}, u32[]{:S(2)}, u32[]{:S(2)}) collective-permute-start(bf16[4,64,2048]{2,1,0:T(8,128)(2,1)} %bitcast.144), channel_id=1, source_target_pairs={{0,1},{1,0},{2,3},{3,2},{4,5},{5,4},{6,7},{7,6},{8,9},{9,8},{10,11... | collective-permute-start | bytes 3145736 | tf_op jit(solution)/shard_map/ppermute | solution.py:518
  84.2 33.0 %collective-permute-start.13 = (bf16[4,64,2048]{2,1,0:T(8,128)(2,1)}, bf16[4,64,2048]{2,1,0:T(8,128)(2,1)S(1)}, u32[]{:S(2)}, u32[]{:S(2)}) collective-permute-start(bf16[4,64,2048]{2,1,0:T(8,128)(2,1)} %bitcast.145), channel_id=1, source_target_pairs={{0,2},{1,3},{2,0},{3,1},{4,6},{5,7},{6,4},{7,5},{8,10},{9,11},{10,... | collective-permute-start | bytes 3145736 | tf_op jit(solution)/shard_map/ppermute | solution.py:518
  140.2 56.1 %collective-permute-start.21 = (bf16[4,256,2048]{2,1,0:T(8,128)(2,1)}, bf16[4,256,2048]{2,1,0:T(8,128)(2,1)}, u32[]{:S(2)}, u32[]{:S(2)}) collective-permute-start(bf16[4,256,2048]{2,1,0:T(8,128)(2,1)} %bitcast.133), channel_id=1, source_target_pairs={{0,4},{4,0},{1,5},{5,1},{2,6},{6,2},{3,7},{7,3},{8,12},{12,8},{9,1... | collective-permute-start | bytes 12582920 | tf_op jit(solution)/shard_map/ppermute | solution.py:335
  140.3 142.6 %all-gather.10.cloned.1.call-start = ((), (), s32[]{:S(2)}) async-start(), calls=%async_computation | async-start | bytes 3932160 | tf_op jit(solution)/shard_map/all_gather | solution.py:588
  163.8 201.3 %all-gather.18.cloned.1.call-start = ((), (), s32[]{:S(2)}) async-start(), calls=%async_computation.4 | async-start | bytes 5242880 | tf_op jit(solution)/shard_map/all_gather | solution.py:625
  168.8 25.3 %collective-permute-start.20 = (bf16[4,64,2048]{2,1,0:T(8,128)(2,1)}, bf16[4,64,2048]{2,1,0:T(8,128)(2,1)S(1)}, u32[]{:S(2)}, u32[]{:S(2)}) collective-permute-start(bf16[4,64,2048]{2,1,0:T(8,128)(2,1)} %bitcast.151), channel_id=1, source_target_pairs={{0,1},{1,0},{2,3},{3,2},{4,5},{5,4},{6,7},{7,6},{8,9},{9,8},{10,11... | collective-permute-start | bytes 3145736 | tf_op jit(solution)/shard_map/ppermute | solution.py:518
  172.1 24.2 %collective-permute-start.22 = (bf16[4,64,2048]{2,1,0:T(8,128)(2,1)S(1)}, bf16[4,64,2048]{2,1,0:T(8,128)(2,1)S(1)}, u32[]{:S(2)}, u32[]{:S(2)}) collective-permute-start(bf16[4,64,2048]{2,1,0:T(8,128)(2,1)S(1)} %bitcast.152), channel_id=1, source_target_pairs={{0,2},{1,3},{2,0},{3,1},{4,6},{5,7},{6,4},{7,5},{8,10},{9,11},{10,... | collective-permute-start | bytes 3145736 | tf_op jit(solution)/shard_map/ppermute | solution.py:518
  174.7 21.6 %collective-permute-start.28 = (bf16[256,2048]{1,0:T(8,128)(2,1)}, bf16[256,2048]{1,0:T(8,128)(2,1)}, u32[]{:S(2)}, u32[]{:S(2)}) collective-permute-start(bf16[256,2048]{1,0:T(8,128)(2,1)} %constant_dynamic-slice_fusion), channel_id=1, source_target_pairs={{0,4},{4,0},{1,5},{5,1},{2,6},{6,2},{3,7},{7,3},{8,12},{12,8},{9,1... | collective-permute-start | bytes 3145736 | tf_op jit(solution)/shard_map/ppermute | solution.py:335
  196.3 33.5 %collective-permute-start.27 = (bf16[512,2048]{1,0:T(8,128)(2,1)S(1)}, bf16[512,2048]{1,0:T(8,128)(2,1)}, u32[]{:S(2)}, u32[]{:S(2)}) collective-permute-start(bf16[512,2048]{1,0:T(8,128)(2,1)S(1)} %bitcast.124), channel_id=1, source_target_pairs={{0,4},{4,0},{1,5},{5,1},{2,6},{6,2},{3,7},{7,3},{8,12},{12,8},{9,1... | collective-permute-start | bytes 6291464 | tf_op jit(solution)/shard_map/ppermute | solution.py:335
  201.6 25.4 %collective-permute-start.30 = (bf16[2,64,2048]{2,1,0:T(8,128)(2,1)S(1)}, bf16[2,64,2048]{2,1,0:T(8,128)(2,1)S(1)}, u32[]{:S(2)}, u32[]{:S(2)}) collective-permute-start(bf16[2,64,2048]{2,1,0:T(8,128)(2,1)S(1)} %slice.141), channel_id=1, source_target_pairs={{0,2},{1,3},{2,0},{3,1},{4,6},{5,7},{6,4},{7,5},{8,10},{9,11},{10,... | collective-permute-start | bytes 1572872 | tf_op jit(solution)/shard_map/ppermute | solution.py:518
  204.2 22.9 %collective-permute-start.29 = (bf16[2,64,2048]{2,1,0:T(8,128)(2,1)S(1)}, bf16[2,64,2048]{2,1,0:T(8,128)(2,1)S(1)}, u32[]{:S(2)}, u32[]{:S(2)}) collective-permute-start(bf16[2,64,2048]{2,1,0:T(8,128)(2,1)S(1)} %slice.140), channel_id=1, source_target_pairs={{0,1},{1,0},{2,3},{3,2},{4,5},{5,4},{6,7},{7,6},{8,9},{9,8},{10,11... | collective-permute-start | bytes 1572872 | tf_op jit(solution)/shard_map/ppermute | solution.py:518
  204.9 24.8 %collective-permute-start.31 = (bf16[2,64,2048]{2,1,0:T(8,128)(2,1)S(1)}, bf16[2,64,2048]{2,1,0:T(8,128)(2,1)S(1)}, u32[]{:S(2)}, u32[]{:S(2)}) collective-permute-start(bf16[2,64,2048]{2,1,0:T(8,128)(2,1)S(1)} %slice.124), channel_id=1, source_target_pairs={{0,1},{1,0},{2,3},{3,2},{4,5},{5,4},{6,7},{7,6},{8,9},{9,8},{10,11... | collective-permute-start | bytes 1572872 | tf_op jit(solution)/shard_map/ppermute | solution.py:518
  206.4 23.3 %collective-permute-start.32 = (bf16[2,64,2048]{2,1,0:T(8,128)(2,1)S(1)}, bf16[2,64,2048]{2,1,0:T(8,128)(2,1)S(1)}, u32[]{:S(2)}, u32[]{:S(2)}) collective-permute-start(bf16[2,64,2048]{2,1,0:T(8,128)(2,1)S(1)} %slice.125), channel_id=1, source_target_pairs={{0,2},{1,3},{2,0},{3,1},{4,6},{5,7},{6,4},{7,5},{8,10},{9,11},{10,... | collective-permute-start | bytes 1572872 | tf_op jit(solution)/shard_map/ppermute | solution.py:518
  227.0 55.8 %collective-permute-start.26 = (bf16[3,512,1408]{2,1,0:T(8,128)(2,1)}, bf16[3,512,1408]{2,1,0:T(8,128)(2,1)}, u32[]{:S(2)}, u32[]{:S(2)}) collective-permute-start(bf16[3,512,1408]{2,1,0:T(8,128)(2,1)} %feed_forward_rows.2.refs_0_.refs_4_), channel_id=1, source_target_pairs={{0,4},{4,0},{1,5},{5,1},{2,6},{6,2},{3,7},{7,3},{8,12},{12,8},{9,1... | collective-permute-start | bytes 12976136 | tf_op jit(solution)/shard_map/ppermute | solution.py:335
  249.9 32.9 %collective-permute-start.34 = (bf16[3,512,1408]{2,1,0:T(8,128)(2,1)}, bf16[3,512,1408]{2,1,0:T(8,128)(2,1)}, u32[]{:S(2)}, u32[]{:S(2)}) collective-permute-start(bf16[3,512,1408]{2,1,0:T(8,128)(2,1)} %feed_forward_rows.3.refs_1_.refs_5_), channel_id=1, source_target_pairs={{0,4},{4,0},{1,5},{5,1},{2,6},{6,2},{3,7},{7,3},{8,12},{12,8},{9,1... | collective-permute-start | bytes 12976136 | tf_op jit(solution)/shard_map/ppermute | solution.py:335
  252.7 25.3 %collective-permute-start.24 = (bf16[2,64,2048]{2,1,0:T(8,128)(2,1)}, bf16[2,64,2048]{2,1,0:T(8,128)(2,1)}, u32[]{:S(2)}, u32[]{:S(2)}) collective-permute-start(bf16[2,64,2048]{2,1,0:T(8,128)(2,1)} %get-tuple-element.115), channel_id=1, source_target_pairs={{0,2},{1,3},{2,0},{3,1},{4,6},{5,7},{6,4},{7,5},{8,10},{9,11},{10,... | collective-permute-start | bytes 1572872 | tf_op jit(solution)/shard_map/ppermute | solution.py:513
  255.3 27.6 %collective-permute-start.33 = (bf16[512,2048]{1,0:T(8,128)(2,1)S(1)}, bf16[512,2048]{1,0:T(8,128)(2,1)}, u32[]{:S(2)}, u32[]{:S(2)}) collective-permute-start(bf16[512,2048]{1,0:T(8,128)(2,1)S(1)} %bitcast.128), channel_id=1, source_target_pairs={{0,4},{4,0},{1,5},{5,1},{2,6},{6,2},{3,7},{7,3},{8,12},{12,8},{9,1... | collective-permute-start | bytes 6291464 | tf_op jit(solution)/shard_map/ppermute | solution.py:335
  278.0 53.8 %collective-permute-start.38 = (bf16[1024,2048]{1,0:T(8,128)(2,1)}, bf16[1024,2048]{1,0:T(8,128)(2,1)}, u32[]{:S(2)}, u32[]{:S(2)}) collective-permute-start(bf16[1024,2048]{1,0:T(8,128)(2,1)} %bitcast.45.refs_0_), channel_id=1, source_target_pairs={{0,4},{4,0},{1,5},{5,1},{2,6},{6,2},{3,7},{7,3},{8,12},{12,8},{9,1... | collective-permute-start | bytes 12582920 | tf_op jit(solution)/shard_map/ppermute | solution.py:335
  317.6 38.9 %collective-permute-start.36 = (bf16[2,1024,1408]{2,1,0:T(8,128)(2,1)}, bf16[2,1024,1408]{2,1,0:T(8,128)(2,1)}, u32[]{:S(2)}, u32[]{:S(2)}) collective-permute-start(bf16[2,1024,1408]{2,1,0:T(8,128)(2,1)} %get-tuple-element.95), channel_id=1, source_target_pairs={{0,4},{4,0},{1,5},{5,1},{2,6},{6,2},{3,7},{7,3},{8,12},{12,8},{9,1... | collective-permute-start | bytes 17301512 | tf_op jit(solution)/shard_map/ppermute | solution.py:335
  318.2 33.5 %collective-permute-start.37 = (bf16[1408,1024]{1,0:T(8,128)(2,1)}, bf16[1408,1024]{1,0:T(8,128)(2,1)}, u32[]{:S(2)}, u32[]{:S(2)}) collective-permute-start(bf16[1408,1024]{1,0:T(8,128)(2,1)} %get-tuple-element.86), channel_id=1, source_target_pairs={{0,4},{4,0},{1,5},{5,1},{2,6},{6,2},{3,7},{7,3},{8,12},{12,8},{9,1... | collective-permute-start | bytes 8650760 | tf_op jit(solution)/shard_map/ppermute | solution.py:335
  345.7 36.9 %collective-permute-start.46 = (bf16[3,1024,512]{2,1,0:T(8,128)(2,1)}, bf16[3,1024,512]{2,1,0:T(8,128)(2,1)S(1)}, u32[]{:S(2)}, u32[]{:S(2)}) collective-permute-start(bf16[3,1024,512]{2,1,0:T(8,128)(2,1)} %get-tuple-element.98), channel_id=1, source_target_pairs={{0,4},{4,0},{1,5},{5,1},{2,6},{6,2},{3,7},{7,3},{8,12},{12,8},{9,1... | collective-permute-start | bytes 9437192 | tf_op jit(solution)/shard_map/ppermute | solution.py:335
  (85 other events, 1007.9 us)
Sparse Core Ops, SparseCore 0:
  15.4 27.3 all-gather.11
  44.4 80.1 all-gather.13
  140.4 28.3 all-gather.15
  170.2 62.7 all-gather.9
  254.1 80.9 all-gather.17
